TPU v7x, 512 devices: a whole 4x8x8 slice. The times are simulated.
512 devices in a mesh: dp: 64 (over z_lo, y, core), mp: 8 (over x, z_hi).
Axes of the slice: x: 4, y: 8, z: 8 (z_hi: 2, z_lo: 4; z = z_hi * 4 + z_lo), core: 2. Of those that a mesh axis runs over, the one named last changes fastest.
Arguments:
- context: bfloat16 [65536, 2048], P('dp', 'mp'), may hold values from -6 to 6
- cotangent: bfloat16 [65536, 4096], P(('dp', 'mp')), may hold values from -24 to 24
- lengths: int32 [2048], P(('dp', 'mp')), may hold values from 1 to 32, as said below
- weight: float32 [2048, 4096], P('mp', 'dp'), may hold values from -0.125 to 0.125
- row_stat: float32 [2048], P('mp'), may hold values from 0.01 to 0.3
- col_stat: float32 [4096], P('dp'), may hold values from 0.01 to 0.3
Outputs:
- context_grad: bfloat16 [65536, 2048], P('dp', 'mp')
- update: float32 [2048, 4096], P('mp', 'dp')
- row_new: float32 [2048], P('mp')
- col_new: float32 [4096], P('dp')
Inputs may be any that keep to these rules, and one draw needn't show every extreme that they name: The first lengths entry of each sequence's 32 slots are real tokens, the rest padding.
All inputs are finite; a program needn't handle non-finite values.
Results may differ from a plain program's by a relative error of at most 0.0049.
Values may be sent and summed in bfloat16 or wider, within the bound.
No kernel may reach another device: no remote copies, remote signals or barrier semaphores. Data moves between devices by JAX's collectives and lax.ppermute only.
A program may use at most 64 MiB of HBM per device.

v0:
```python
import jax
import jax.numpy as jnp
from jax import lax
from jax.sharding import PartitionSpec as P

decay_rate = 0.9
square_eps = 1e-30


def per_device(context, cotangent, lengths, weight, row_stat, col_stat):
    data_groups = lax.axis_size("dp")
    seq_here = lengths.shape[0]
    target_len = cotangent.shape[0] // seq_here
    model_width = cotangent.shape[1]
    position = jnp.arange(target_len, dtype=jnp.int32)
    inside = position[None, :] < lengths[:, None]
    shaped = cotangent.reshape(seq_here, target_len, model_width)
    masked = jnp.where(inside[:, :, None], shaped, jnp.zeros((), cotangent.dtype)).reshape(
        -1, model_width
    )
    weight_b = weight.astype(jnp.bfloat16)
    head_cols = context.shape[1]
    gathered = lax.all_gather(masked, "mp", axis=0, tiled=True)
    back_ctx = lax.dot_general(
        gathered,
        lax.all_gather(weight_b, "dp", axis=1, tiled=True),
        (((1,), (1,)), ((), ())),
        preferred_element_type=jnp.float32,
    )
    grad_term = lax.dot_general(
        context, gathered, (((0,), (0,)), ((), ())), preferred_element_type=jnp.float32
    )
    context_grad = back_ctx.astype(jnp.bfloat16)
    grad = lax.psum_scatter(grad_term, "dp", scatter_dimension=1, tiled=True) / data_groups
    square = grad * grad + square_eps
    inner_total = head_cols * lax.axis_size("mp")
    row_all = lax.psum(jnp.sum(square, axis=1), "dp")
    row_new = decay_rate * row_stat + (1.0 - decay_rate) * (row_all / model_width)
    col_all = lax.psum(jnp.sum(square, axis=0), "mp")
    col_new = decay_rate * col_stat + (1.0 - decay_rate) * (col_all / inner_total)
    raw_update = grad / jnp.sqrt(row_new[:, None] * col_new[None, :])
    square_sum = lax.psum(jnp.sum(raw_update * raw_update), ("dp", "mp"))
    update_rms = jnp.sqrt(square_sum / (inner_total * model_width))
    update = raw_update / jnp.maximum(1.0, update_rms)
    return (context_grad, update, row_new, col_new)


def solution(mesh):
    in_specs = (
        P("dp", "mp"),
        P(("dp", "mp"), None),
        P(("dp", "mp")),
        P("mp", "dp"),
        P("mp"),
        P("dp"),
    )
    out_specs = (P("dp", "mp"), P("mp", "dp"), P("mp"), P("dp"))
    return jax.shard_map(
        per_device, mesh=mesh, in_specs=in_specs, out_specs=out_specs, check_vma=False
    )
```

profile of v0, /device:TPU:1, one launch (start us, length us, event | category | flops | bytes accessed | tf_op | source)
XLA Modules:
  0.0 763.4 jit_solution(10491318361762110344)
XLA Ops:
  7.2 0.0 copy-start
  7.2 0.0 all-gather.3.cloned.1.call-start
  7.2 0.8 iota_compare_fusion
  8.0 0.1 lt.23
  8.1 2.4 broadcast_select_fusion
  10.5 0.0 all-gather.3.cloned.1.call-update
  10.5 0.0 copy-start.2
  10.6 0.0 copy-start.6
  10.6 0.0 copy-start.5
  10.6 0.0 reduce-scatter.2.cloned.1.call-start
  10.6 184.7 %all-gather.3.cloned.1.call-done = bf16[1024,4096]{1,0:T(8,128)(2,1)} async-done(((bf16[128,4096]{1,0:T(8,128)(2,1)}), bf16[1024,4096]{1,0:T(8,128)(2,1)}) %all-gather.3.cloned.1.call-update) | async-done | bytes 8388624 | tf_op jit(solution)/shard_map/all_gather | solution.py:23
  195.3 0.0 copy-done
  195.3 7.8 %convolution_bitcast_fusion = f32[256,4096]{0,1:T(8,128)} fusion(bf16[1024,4096]{1,0:T(8,128)(2,1)} %all-gather.3.cloned.1.call-done, bf16[1024,256]{1,0:T(8,128)(2,1)S(1)} %copy-done), kind=kOutput, calls=%fused_computation | convolution fusion | flops 2147483648 | bytes 13107200 | tf_op jit(solution)/shard_map/dot_general | solution.py:30
  203.1 0.0 reduce-scatter.2.cloned.1.call-update
  203.1 0.0 all-gather.5.cloned.1.call-start
  203.2 0.0 copy-done.2
  203.2 0.6 convert_element_type.6
  203.8 0.0 all-gather.5.cloned.1.call-update
  203.9 279.7 %reduce-scatter.2.cloned.1.call-done = f32[256,64]{0,1:T(8,128)} async-done(((f32[256,4096]{0,1:T(8,128)}), f32[256,64]{0,1:T(8,128)}) %reduce-scatter.2.cloned.1.call-update) | async-done | bytes 65552 | tf_op jit(solution)/shard_map/reduce_scatter | solution.py:34
  483.5 0.0 copy-start.1
  483.5 1.0 fusion.1
  484.6 28.3 %psum.22 = f32[64]{0:T(128)S(1)} all-reduce(f32[64]{0:T(128)S(1)} %get-tuple-element.5), channel_id=1, replica_groups=mesh['dp'=64,'mp'=8] {'mp'}, use_global_device_ids=true, to_apply=%region_4.5 | all-reduce | flops 64 | bytes 512 | tf_op jit(solution)/shard_map/psum | solution.py:39
  512.9 140.5 %psum.21 = f32[256]{0:T(256)S(1)} all-reduce(f32[256]{0:T(256)S(1)} %get-tuple-element.4), channel_id=1, replica_groups=mesh['dp'=64,'mp'=8] {'dp'}, use_global_device_ids=true, to_apply=%region_2.3 | all-reduce | flops 256 | bytes 2048 | tf_op jit(solution)/shard_map/psum | solution.py:37
  653.4 0.0 copy-done.6
  653.4 0.0 copy-done.5
  653.4 0.0 copy-start.4
  653.5 0.0 copy-start.3
  653.5 1.5 multiply_reduce_fusion
  655.0 0.0 all-gather.5.cloned.1.call-done
  655.0 7.1 convolution_convert_fusion
  662.1 93.3 %psum.23 = f32[]{:T(128)} all-reduce(f32[]{:T(128)} %multiply_reduce_fusion), channel_id=1, replica_groups=mesh['dp'=64,'mp'=8] {'dp','mp'}, use_global_device_ids=true, to_apply=%region_6.7 | all-reduce | flops 1 | bytes 8 | tf_op jit(solution)/shard_map/psum | solution.py:42
  756.1 0.0 copy-done.1
  756.1 0.7 fusion.2
  756.9 0.0 copy-done.4
  756.9 0.0 copy-done.3
  (2 shorter events, 0.0 us)
Async XLA Ops:
  7.2 188.1 %copy-start = (bf16[1024,256]{1,0:T(8,128)(2,1)S(1)}, bf16[1024,256]{1,0:T(8,128)(2,1)}, u32[]{:S(2)}) copy-start(bf16[1024,256]{1,0:T(8,128)(2,1)} %param.6) | copy-start | bytes 1572868
  7.2 188.1 %all-gather.3.cloned.1.call-start = ((), (), s32[]{:S(2)}) async-start(), calls=%async_computation.1 | async-start | bytes 9437184 | tf_op jit(solution)/shard_map/all_gather | solution.py:23
  10.5 192.7 %copy-start.2 = (f32[256,64]{0,1:T(8,128)S(1)}, f32[256,64]{0,1:T(8,128)}, u32[]{:S(2)}) copy-start(f32[256,64]{0,1:T(8,128)} %param.9) | copy-start | bytes 196612
  10.6 642.9 %copy-start.6 = (f32[64]{0:T(128)S(1)}, f32[64]{0:T(128)}, u32[]{:S(2)}) copy-start(f32[64]{0:T(128)} %param.11) | copy-start | bytes 772
  10.6 642.9 %copy-start.5 = (f32[256]{0:T(256)S(1)}, f32[256]{0:T(256)}, u32[]{:S(2)}) copy-start(f32[256]{0:T(256)} %param.10) | copy-start | bytes 3076
  10.6 473.0 %reduce-scatter.2.cloned.1.call-start = ((), (), s32[]{:S(2)}) async-start(), calls=%async_computation.3 | async-start | bytes 4259840 | tf_op jit(solution)/shard_map/reduce_scatter | solution.py:34
  203.1 451.8 %all-gather.5.cloned.1.call-start = ((), (), s32[]{:S(2)}) async-start(), calls=%async_computation.2 | async-start | bytes 2129920 | tf_op jit(solution)/shard_map/all_gather | solution.py:26
  483.5 272.6 %copy-start.1 = (f32[256,64]{0,1:T(8,128)S(1)}, f32[256,64]{0,1:T(8,128)}, u32[]{:S(2)}) copy-start(f32[256,64]{0,1:T(8,128)} %reduce-scatter.2.cloned.1.call-done) | copy-start | bytes 196612
  653.4 103.4 %copy-start.4 = (f32[64]{0:T(128)}, f32[64]{0:T(128)S(1)}, u32[]{:S(2)}) copy-start(f32[64]{0:T(128)S(1)} %multiply_add_fusion.2) | copy-start | bytes 772
  653.5 103.4 %copy-start.3 = (f32[256]{0:T(256)}, f32[256]{0:T(256)S(1)}, u32[]{:S(2)}) copy-start(f32[256]{0:T(256)S(1)} %multiply_add_fusion.1) | copy-start | bytes 3076
Sparse Core Ops, SparseCore 0:
  11.2 184.0 all-gather.2
  203.3 280.2 reduce-scatter.1
  486.3 118.0 all-gather.4
where the time goes:
time: 764 us; the launch traced here: 763 us
  waiting for transfers between devices  464 us (61%)
  blocking collectives  262 us (34%)
  matrix products  14.9 us (2%)
  between operations  14.5 us (2%)
    reduce_scatter x1, waiting for transfers between devices, per_device(): lax.psum_scatter(grad_term, 'dp', scatter_dimension=1, tiled=True)  280 us
    all_gather x1, waiting for transfers between devices, per_device(): gathered = lax.all_gather(masked, 'mp', axis=0, tiled=True)  185 us
    psum x1, blocking collectives, per_device(): row_all = lax.psum(jnp.sum(square, axis=1), 'dp')  140 us
    psum x1, blocking collectives, per_device(): square_sum = lax.psum(jnp.sum(raw_update * raw_update), ('dp', 'mp'))  93.3 us
    psum x1, blocking collectives, per_device(): col_all = lax.psum(jnp.sum(square, axis=0), 'mp')  28.3 us
  transfers between devices with their start and end apart: 3, of which 2 were waited for; matrix products, arithmetic and copies ran while one was open for 0% of the time, Pallas kernels for 0%

commit v1 on v0

v1 whole, which is shorter than its diff:
```python
import jax
import jax.numpy as jnp
from jax import lax
from jax.sharding import Mesh, PartitionSpec as P

decay_rate = 0.9
square_eps = 1e-30

SPLIT = (("zl", 4), ("y", 8), ("c", 2), ("x", 4), ("zh", 2))
SIZE = dict(SPLIT)
DP = ("zl", "y", "c")
MP = ("x", "zh")


def shift(value, axis, step):
    size = SIZE[axis]
    return lax.ppermute(value, axis, [(i, (i + step) % size) for i in range(size)])


def pick(value, index, axis=0):
    return lax.dynamic_index_in_dim(value, index, axis, keepdims=False)


def psum_each(value, axes):
    for axis in axes:
        value = lax.psum(value, axis)
    return value


def per_device(context, cotangent, lengths, weight, row_stat, col_stat):
    groups = SIZE["zl"] * SIZE["y"] * SIZE["c"]
    x, zh, y, c, zl = (lax.axis_index(a) for a in ("x", "zh", "y", "c", "zl"))
    seq_here = lengths.shape[0]
    tokens, width = cotangent.shape
    target_len = tokens // seq_here
    heads = context.shape[1]
    position = jnp.arange(target_len, dtype=jnp.int32)
    inside = position[None, :] < lengths[:, None]
    shaped = cotangent.reshape(seq_here, target_len, width)
    masked = jnp.where(inside[:, :, None], shaped, jnp.zeros((), cotangent.dtype)).reshape(
        tokens, width
    )
    weight_t = lax.all_gather(weight.T.astype(jnp.bfloat16), DP, axis=0, tiled=True)

    other = shift(masked, "zh", 1)
    steps = (1, 3, 2)
    blocks = [masked] + [shift(masked, "x", s) for s in steps]
    blocks += [other] + [shift(other, "x", s) for s in steps]
    gathered = jnp.concatenate(blocks, axis=0)
    places = [
        ((x - s) % SIZE["x"]) * SIZE["zh"] + (zh if half == 0 else 1 - zh)
        for half in range(2)
        for s in (0,) + steps
    ]
    ctx = context.reshape(SIZE["x"] * SIZE["zh"], tokens, heads)
    ctx = jnp.concatenate([pick(ctx, p) for p in places], axis=0)

    grad_t = lax.dot_general(
        gathered, ctx, (((0,), (0,)), ((), ())), preferred_element_type=jnp.float32
    )
    back = lax.dot_general(
        gathered, weight_t, (((1,), (0,)), ((), ())), preferred_element_type=jnp.float32
    ).astype(jnp.bfloat16)
    back = back.reshape(len(places), tokens, heads)
    context_grad = jnp.zeros_like(back)
    for i, p in enumerate(places):
        context_grad = lax.dynamic_update_index_in_dim(context_grad, back[i], p, 0)
    context_grad = context_grad.reshape(context.shape)

    cols = width // groups
    parts = grad_t.reshape(SIZE["zl"], SIZE["y"], SIZE["c"], cols, heads)
    parts = pick(parts, c, 2) + shift(pick(parts, 1 - c, 2), "c", 1)
    narrow = parts.astype(jnp.bfloat16)
    total = pick(parts, y, 1)
    for s in (1, 7, 2, 6, 3, 5, 4):
        total = total + shift(pick(narrow, (y + s) % SIZE["y"], 1), "y", s).astype(jnp.float32)
    part = pick(total, zl)
    for s in (1, 3, 2):
        part = part + shift(pick(total, (zl + s) % SIZE["zl"]), "zl", s)
    grad = part / groups

    square = grad * grad + square_eps
    inner_total = heads * SIZE["x"] * SIZE["zh"]
    col_all = psum_each(jnp.sum(square, axis=1), MP)
    col_new = decay_rate * col_stat + (1.0 - decay_rate) * (col_all / inner_total)
    scaled = grad * grad / col_new[:, None]
    row_all, row_scaled = psum_each(jnp.stack([jnp.sum(square, axis=0), jnp.sum(scaled, axis=0)]), DP)
    row_new = decay_rate * row_stat + (1.0 - decay_rate) * (row_all / width)
    square_sum = psum_each(jnp.sum(row_scaled / row_new), MP)
    raw_update = grad / jnp.sqrt(row_new[None, :] * col_new[:, None])
    update_rms = jnp.sqrt(square_sum / (inner_total * width))
    update = (raw_update / jnp.maximum(1.0, update_rms)).T
    return (context_grad, update, row_new, col_new)


def solution(mesh):
    names = tuple(name for name, _ in SPLIT)
    fine = Mesh(mesh.devices.reshape(tuple(size for _, size in SPLIT)), names)
    in_specs = (P(DP, MP), P(DP + MP, None), P(DP + MP), P(MP, DP), P(MP), P(DP))
    out_specs = (P(DP, MP), P(MP, DP), P(MP), P(DP))
    return jax.shard_map(
        per_device, mesh=fine, in_specs=in_specs, out_specs=out_specs, check_vma=False
    )
```

time: 764 us -> 305 us (0.40)
  waiting for transfers between devices: 464 us -> 99.3 us
  blocking collectives: 262 us -> 63.2 us
  starting transfers between devices: 0.12 us -> 79 us
  local copies, waits for them, and re-layouts: 0.13 us -> 24.2 us
    reduce_scatter x1 -> x0, waiting for transfers between devices: 280 us -> none  [per_device(): lax.psum_scatter(grad_term, 'dp', scatter_dimension=1, tiled=True)]
    psum x3 -> x7, blocking collectives: 262 us -> 63.2 us  [psum_each(): value = lax.psum(value, axis)]
    all_gather x2 -> x1, waiting for transfers between devices: 185 us -> 53.6 us  [per_device(): lax.all_gather(weight.T.astype(jnp.bfloat16), DP, axis=0, tiled=True)]
    ppermute x0 -> x18, starting transfers between devices: none -> 79 us  [shift(): lax.ppermute(value, axis, [(i, (i + step) % size) for i in range(size)])]
    ppermute x0 -> x18, waiting for transfers between devices: none -> 45.7 us  [shift(): lax.ppermute(value, axis, [(i, (i + step) % size) for i in range(size)])]
    unnamed x14 -> x27, local copies, waits for them, and re-layouts: 0.05 us -> 21.2 us
  transfers between devices with their start and end apart: 3 -> 19, of which waited for: 2 -> 9; matrix products, arithmetic and copies ran while one was open for 0% -> 12% of each run, Pallas kernels for 0% -> 0%
where the time goes in v1:
time: 305 us; the launch traced here: 302 us
  waiting for transfers between devices  99.3 us (33%)
  starting transfers between devices  79 us (26%)
  blocking collectives  63.2 us (21%)
  local copies, waits for them, and re-layouts  24.2 us (8%)
  between operations  15.3 us (5%)
  matrix products  12.5 us (4%)
  other arithmetic  8.41 us (3%)
    ppermute x18, starting transfers between devices, shift(): lax.ppermute(value, axis, [(i, (i + step) % size) for i in range(size)])  79 us
    psum x7, blocking collectives, psum_each(): value = lax.psum(value, axis)  63.2 us
    all_gather x1, waiting for transfers between devices, per_device(): lax.all_gather(weight.T.astype(jnp.bfloat16), DP, axis=0, tiled=True)  53.6 us
    ppermute x18, waiting for transfers between devices, shift(): lax.ppermute(value, axis, [(i, (i + step) % size) for i in range(size)])  45.7 us
    unnamed x27, local copies, waits for them, and re-layouts  21.2 us
    dot_general x1, matrix products, per_device(): lax.dot_general(gathered, weight_t, (((1,), (0,)), ((), ())), preferred_e...  6.45 us
  transfers between devices with their start and end apart: 19, of which 9 were waited for; matrix products, arithmetic and copies ran while one was open for 12% of the time, Pallas kernels for 0%

profile of v1, /device:TPU:1, one launch (start us, length us, event | category | flops | bytes accessed | tf_op | source)
XLA Modules:
  0.0 301.8 jit_solution(5566448500314028675)
XLA Ops:
  7.2 0.7 iota_compare_fusion
  7.9 0.1 lt.169
  8.0 2.5 constant_dynamic-update-slice_fusion.7
  10.6 3.9 %collective-permute-start = (bf16[128,4096]{1,0:T(8,128)(2,1)S(1)}, bf16[128,4096]{1,0:T(8,128)(2,1)}, u32[]{:S(2)}, u32[]{:S(2)}) collective-permute-start(bf16[128,4096]{1,0:T(8,128)(2,1)S(1)} %get-tuple-element.13), channel_id=1, source_target_pairs={{0,2},{2,4},{4,6},{6,0},{1,3},{3,5},{5,7},{7,1},{8,10},{10,12},{12... | collective-permute-start | bytes 3145736 | tf_op jit(solution)/shard_map/ppermute | solution.py:17
  14.5 3.2 %collective-permute-start.1 = (bf16[128,4096]{1,0:T(8,128)(2,1)S(1)}, bf16[128,4096]{1,0:T(8,128)(2,1)}, u32[]{:S(2)}, u32[]{:S(2)}) collective-permute-start(bf16[128,4096]{1,0:T(8,128)(2,1)S(1)} %get-tuple-element.13), channel_id=1, source_target_pairs={{0,6},{2,0},{4,2},{6,4},{1,7},{3,1},{5,3},{7,5},{8,14},{10,8},{12,... | collective-permute-start | bytes 3145736 | tf_op jit(solution)/shard_map/ppermute | solution.py:17
  17.7 3.6 %collective-permute-start.2 = (bf16[128,4096]{1,0:T(8,128)(2,1)S(1)}, bf16[128,4096]{1,0:T(8,128)(2,1)S(1)}, u32[]{:S(2)}, u32[]{:S(2)}) collective-permute-start(bf16[128,4096]{1,0:T(8,128)(2,1)S(1)} %get-tuple-element.13), channel_id=1, source_target_pairs={{0,4},{2,6},{4,0},{6,2},{1,5},{3,7},{5,1},{7,3},{8,12},{10,14},{12... | collective-permute-start | bytes 3145736 | tf_op jit(solution)/shard_map/ppermute | solution.py:17
  21.3 10.6 %collective-permute-start.3 = (bf16[128,4096]{1,0:T(8,128)(2,1)S(1)}, bf16[128,4096]{1,0:T(8,128)(2,1)S(1)}, u32[]{:S(2)}, u32[]{:S(2)}) collective-permute-start(bf16[128,4096]{1,0:T(8,128)(2,1)S(1)} %get-tuple-element.13), channel_id=1, source_target_pairs={{0,1},{1,0},{2,3},{3,2},{4,5},{5,4},{6,7},{7,6},{8,9},{9,8},{10,11... | collective-permute-start | bytes 3145736 | tf_op jit(solution)/shard_map/ppermute | solution.py:17
  32.0 1.5 convert_bitcast_fusion
  33.5 1.5 bitcast_dynamic-update-slice_fusion.7
  35.0 1.5 bitcast_dynamic-update-slice_fusion.6
  36.5 1.5 bitcast_dynamic-update-slice_fusion.5
  37.9 1.5 bitcast_dynamic-update-slice_fusion.4
  39.4 1.5 bitcast_dynamic-update-slice_fusion.3
  40.9 1.5 bitcast_dynamic-update-slice_fusion.2
  42.4 1.5 bitcast_dynamic-update-slice_fusion.1
  43.8 1.5 bitcast_dynamic-update-slice_fusion
  45.3 8.8 %collective-permute-done.3 = bf16[128,4096]{1,0:T(8,128)(2,1)S(1)} collective-permute-done((bf16[128,4096]{1,0:T(8,128)(2,1)S(1)}, bf16[128,4096]{1,0:T(8,128)(2,1)S(1)}, u32[]{:S(2)}, u32[]{:S(2)}) %collective-permute-start.3) | collective-permute-done | bytes 1048608 | tf_op jit(solution)/shard_map/ppermute | solution.py:17
  54.2 2.0 collective-permute-start.4
  56.2 4.5 %collective-permute-start.5 = (bf16[128,4096]{1,0:T(8,128)(2,1)S(1)}, bf16[128,4096]{1,0:T(8,128)(2,1)S(1)}, u32[]{:S(2)}, u32[]{:S(2)}) collective-permute-start(bf16[128,4096]{1,0:T(8,128)(2,1)S(1)} %collective-permute-done.3), channel_id=1, source_target_pairs={{0,6},{2,0},{4,2},{6,4},{1,7},{3,1},{5,3},{7,5},{8,14},{10,8},{12,... | collective-permute-start | bytes 3145736 | tf_op jit(solution)/shard_map/ppermute | solution.py:17
  60.7 1.9 collective-permute-start.6
  62.6 2.3 constant_dynamic-update-slice_fusion.6
  64.9 2.3 constant_dynamic-update-slice_fusion.5
  67.2 1.1 constant_dynamic-update-slice_fusion.4
  68.3 1.0 constant_dynamic-update-slice_fusion.3
  69.4 9.7 %collective-permute-done.4 = bf16[128,4096]{1,0:T(8,128)(2,1)S(1)} collective-permute-done((bf16[128,4096]{1,0:T(8,128)(2,1)S(1)}, bf16[128,4096]{1,0:T(8,128)(2,1)S(1)}, u32[]{:S(2)}, u32[]{:S(2)}) %collective-permute-start.4) | collective-permute-done | bytes 1048608 | tf_op jit(solution)/shard_map/ppermute | solution.py:17
  79.0 1.1 constant_dynamic-update-slice_fusion.2
  80.1 1.1 constant_dynamic-update-slice_fusion.1
  81.2 17.6 %collective-permute-done.6 = bf16[128,4096]{1,0:T(8,128)(2,1)S(1)} collective-permute-done((bf16[128,4096]{1,0:T(8,128)(2,1)S(1)}, bf16[128,4096]{1,0:T(8,128)(2,1)S(1)}, u32[]{:S(2)}, u32[]{:S(2)}) %collective-permute-start.6) | collective-permute-done | bytes 1048608 | tf_op jit(solution)/shard_map/ppermute | solution.py:17
  98.8 1.1 constant_dynamic-update-slice_fusion
  99.8 6.0 %fusion.19 = f32[4096,256]{1,0:T(8,128)S(1)} fusion(bf16[1024,4096]{1,0:T(8,128)(2,1)} %constant_dynamic-update-slice_fusion, bf16[1024,256]{1,0:T(8,128)(2,1)} %bitcast_dynamic-update-slice_fusion), kind=kOutput, calls=%fused_computation.69 | convolution fusion | flops 2147483648 | bytes 13107200 | tf_op jit(solution)/shard_map/dot_general | solution.py:58
  105.9 1.9 copy-done
  107.8 0.1 dynamic-slice_bitcast_fusion
  107.9 13.3 %collective-permute-start.7 = (f32[4,8,64,256]{3,2,1,0:T(8,128)S(1)}, f32[4,8,64,256]{3,2,1,0:T(8,128)}, u32[]{:S(2)}, u32[]{:S(2)}) collective-permute-start(f32[4,8,64,256]{3,2,1,0:T(8,128)S(1)} %dynamic-slice_bitcast_fusion), channel_id=1, source_target_pairs={{0,8},{8,0},{1,9},{9,1},{2,10},{10,2},{3,11},{11,3},{4,12},{12,4},... | collective-permute-start | bytes 6291464 | tf_op jit(solution)/shard_map/ppermute | solution.py:17
  121.4 53.6 %all-gather.2.cloned.1.call-done = bf16[4096,256]{1,0:T(8,128)(2,1)} async-done(((bf16[64,256]{1,0:T(8,128)(2,1)}), bf16[4096,256]{1,0:T(8,128)(2,1)}) %all-gather.2.cloned.1.call-update) | async-done | bytes 2097168 | tf_op jit(solution)/shard_map/all_gather | solution.py:43
  175.0 6.5 %convolution_convert_fusion = bf16[1024,256]{1,0:T(8,128)(2,1)S(1)} fusion(bf16[1024,4096]{1,0:T(8,128)(2,1)} %constant_dynamic-update-slice_fusion, bf16[4096,256]{1,0:T(8,128)(2,1)} %all-gather.2.cloned.1.call-done), kind=kOutput, calls=%fused_computation.2 | convolution fusion | flops 2147745792 | bytes 11010048 | tf_op jit(solution)/shard_map/dot_general | solution.py:61
  181.6 2.0 fusion.18
  183.6 0.1 dynamic-slice_bitcast_fusion.7
  183.7 5.3 %collective-permute-start.14 = (bf16[4,64,256]{2,1,0:T(8,128)(2,1)S(1)}, bf16[4,64,256]{2,1,0:T(8,128)(2,1)S(1)}, u32[]{:S(2)}, u32[]{:S(2)}) collective-permute-start(bf16[4,64,256]{2,1,0:T(8,128)(2,1)S(1)} %get-tuple-element.15), channel_id=1, source_target_pairs={{0,64},{16,80},{32,96},{48,112},{64,0},{80,16},{96,32},{112,48},{1... | collective-permute-start | bytes 393224 | tf_op jit(solution)/shard_map/ppermute | solution.py:17
  189.0 2.5 collective-permute-start.13
  191.5 4.6 %collective-permute-start.12 = (bf16[4,64,256]{2,1,0:T(8,128)(2,1)S(1)}, bf16[4,64,256]{2,1,0:T(8,128)(2,1)S(1)}, u32[]{:S(2)}, u32[]{:S(2)}) collective-permute-start(bf16[4,64,256]{2,1,0:T(8,128)(2,1)S(1)} %get-tuple-element.17), channel_id=1, source_target_pairs={{0,48},{16,64},{32,80},{48,96},{64,112},{80,0},{96,16},{112,32},{1... | collective-permute-start | bytes 393224 | tf_op jit(solution)/shard_map/ppermute | solution.py:17
  196.1 4.3 %collective-permute-start.11 = (bf16[4,64,256]{2,1,0:T(8,128)(2,1)S(1)}, bf16[4,64,256]{2,1,0:T(8,128)(2,1)S(1)}, u32[]{:S(2)}, u32[]{:S(2)}) collective-permute-start(bf16[4,64,256]{2,1,0:T(8,128)(2,1)S(1)} %get-tuple-element.18), channel_id=1, source_target_pairs={{0,96},{16,112},{32,0},{48,16},{64,32},{80,48},{96,64},{112,80},{1... | collective-permute-start | bytes 393224 | tf_op jit(solution)/shard_map/ppermute | solution.py:17
  200.4 2.0 collective-permute-start.10
  202.4 4.8 %collective-permute-start.9 = (bf16[4,64,256]{2,1,0:T(8,128)(2,1)S(1)}, bf16[4,64,256]{2,1,0:T(8,128)(2,1)S(1)}, u32[]{:S(2)}, u32[]{:S(2)}) collective-permute-start(bf16[4,64,256]{2,1,0:T(8,128)(2,1)S(1)} %get-tuple-element.20), channel_id=1, source_target_pairs={{0,112},{16,0},{32,16},{48,32},{64,48},{80,64},{96,80},{112,96},{1... | collective-permute-start | bytes 393224 | tf_op jit(solution)/shard_map/ppermute | solution.py:17
  207.2 1.9 collective-permute-start.8
  209.2 2.2 collective-permute-done.11
  211.4 2.5 collective-permute-done.9
  213.9 0.8 collective-permute-done.8
  214.7 0.1 fusion.5
  214.9 5.2 %collective-permute-start.17 = (f32[64,256]{1,0:T(8,128)S(1)}, f32[64,256]{1,0:T(8,128)S(1)}, u32[]{:S(2)}, u32[]{:S(2)}) collective-permute-start(f32[64,256]{1,0:T(8,128)S(1)} %get-tuple-element.22), channel_id=1, source_target_pairs={{0,256},{128,384},{256,0},{384,128},{1,257},{129,385},{257,1},{385... | collective-permute-start | bytes 196616 | tf_op jit(solution)/shard_map/ppermute | solution.py:17
  220.1 2.5 collective-permute-start.16
  222.6 2.8 collective-permute-start.15
  225.4 0.1 collective-permute-done.16
  225.5 3.9 %collective-permute-done.15 = f32[64,256]{1,0:T(8,128)S(1)} collective-permute-done((f32[64,256]{1,0:T(8,128)S(1)}, f32[64,256]{1,0:T(8,128)S(1)}, u32[]{:S(2)}, u32[]{:S(2)}) %collective-permute-start.15) | collective-permute-done | bytes 65568 | tf_op jit(solution)/shard_map/ppermute | solution.py:17
  229.5 0.1 add_reduce_fusion
  229.6 6.9 %psum.49 = f32[64]{0:T(128)S(1)} all-reduce(f32[64]{0:T(128)S(1)} %get-tuple-element.8), channel_id=1, replica_groups=mesh['zl'=4,'y'=8,'c'=2,'x'=4,'zh'=2] {'x'}, use_global_device_ids=true, to_apply=%region_2.3 | all-reduce | flops 64 | bytes 512 | tf_op jit(solution)/shard_map/psum | solution.py:26
  236.5 7.7 %psum.50 = f32[64]{0:T(128)S(1)} all-reduce(f32[64]{0:T(128)S(1)} %psum.49), channel_id=1, replica_groups=mesh['zl'=4,'y'=8,'c'=2,'x'=4,'zh'=2] {'zh'}, use_global_device_ids=true, to_apply=%region_3.4 | all-reduce | flops 64 | bytes 512 | tf_op jit(solution)/shard_map/psum | solution.py:26
  244.2 0.1 add_reduce_fusion.1
  244.3 6.9 %psum.51 = f32[2,256]{1,0:T(2,128)S(1)} all-reduce(f32[2,256]{1,0:T(2,128)S(1)} %pad_maximum_fusion), channel_id=1, replica_groups=mesh['zl'=4,'y'=8,'c'=2,'x'=4,'zh'=2] {'zl'}, use_global_device_ids=true, to_apply=%region_5.6 | all-reduce | flops 512 | bytes 4096 | tf_op jit(solution)/shard_map/psum | solution.py:26
  251.2 11.5 %psum.52 = f32[2,256]{1,0:T(2,128)S(1)} all-reduce(f32[2,256]{1,0:T(2,128)S(1)} %psum.51), channel_id=1, replica_groups=mesh['zl'=4,'y'=8,'c'=2,'x'=4,'zh'=2] {'y'}, use_global_device_ids=true, to_apply=%region_6.7 | all-reduce | flops 512 | bytes 4096 | tf_op jit(solution)/shard_map/psum | solution.py:26
  262.7 14.5 %psum.53 = f32[2,256]{1,0:T(2,128)S(1)} all-reduce(f32[2,256]{1,0:T(2,128)S(1)} %psum.52), channel_id=1, replica_groups=mesh['zl'=4,'y'=8,'c'=2,'x'=4,'zh'=2] {'c'}, use_global_device_ids=true, to_apply=%region_7.8 | all-reduce | flops 512 | bytes 4096 | tf_op jit(solution)/shard_map/psum | solution.py:26
  277.2 0.6 divide_reduce_fusion.1
  277.8 7.3 %psum.54 = f32[]{:T(128)} all-reduce(f32[]{:T(128)} %get-tuple-element.6), channel_id=1, replica_groups=mesh['zl'=4,'y'=8,'c'=2,'x'=4,'zh'=2] {'x'}, use_global_device_ids=true, to_apply=%region_9.10 | all-reduce | flops 1 | bytes 8 | tf_op jit(solution)/shard_map/psum | solution.py:26
  285.2 8.3 %psum.55 = f32[]{:T(128)} all-reduce(f32[]{:T(128)} %psum.54), channel_id=1, replica_groups=mesh['zl'=4,'y'=8,'c'=2,'x'=4,'zh'=2] {'zh'}, use_global_device_ids=true, to_apply=%region_10.11 | all-reduce | flops 1 | bytes 8 | tf_op jit(solution)/shard_map/psum | solution.py:26
  294.2 0.7 divide_bitcast_fusion
  (38 shorter events, 0.3 us)
Async XLA Ops:
  7.2 167.8 %all-gather.2.cloned.1.call-start = ((), (), s32[]{:S(2)}) async-start(), calls=%async_computation | async-start | bytes 2129920 | tf_op jit(solution)/shard_map/all_gather | solution.py:43
  10.6 50.1 %collective-permute-start = (bf16[128,4096]{1,0:T(8,128)(2,1)S(1)}, bf16[128,4096]{1,0:T(8,128)(2,1)}, u32[]{:S(2)}, u32[]{:S(2)}) collective-permute-start(bf16[128,4096]{1,0:T(8,128)(2,1)S(1)} %get-tuple-element.13), channel_id=1, source_target_pairs={{0,2},{2,4},{4,6},{6,0},{1,3},{3,5},{5,7},{7,1},{8,10},{10,12},{12... | collective-permute-start | bytes 3145736 | tf_op jit(solution)/shard_map/ppermute | solution.py:17
  14.5 50.4 %collective-permute-start.1 = (bf16[128,4096]{1,0:T(8,128)(2,1)S(1)}, bf16[128,4096]{1,0:T(8,128)(2,1)}, u32[]{:S(2)}, u32[]{:S(2)}) collective-permute-start(bf16[128,4096]{1,0:T(8,128)(2,1)S(1)} %get-tuple-element.13), channel_id=1, source_target_pairs={{0,6},{2,0},{4,2},{6,4},{1,7},{3,1},{5,3},{7,5},{8,14},{10,8},{12,... | collective-permute-start | bytes 3145736 | tf_op jit(solution)/shard_map/ppermute | solution.py:17
  17.7 49.6 %collective-permute-start.2 = (bf16[128,4096]{1,0:T(8,128)(2,1)S(1)}, bf16[128,4096]{1,0:T(8,128)(2,1)S(1)}, u32[]{:S(2)}, u32[]{:S(2)}) collective-permute-start(bf16[128,4096]{1,0:T(8,128)(2,1)S(1)} %get-tuple-element.13), channel_id=1, source_target_pairs={{0,4},{2,6},{4,0},{6,2},{1,5},{3,7},{5,1},{7,3},{8,12},{10,14},{12... | collective-permute-start | bytes 3145736 | tf_op jit(solution)/shard_map/ppermute | solution.py:17
  21.3 32.8 %collective-permute-start.3 = (bf16[128,4096]{1,0:T(8,128)(2,1)S(1)}, bf16[128,4096]{1,0:T(8,128)(2,1)S(1)}, u32[]{:S(2)}, u32[]{:S(2)}) collective-permute-start(bf16[128,4096]{1,0:T(8,128)(2,1)S(1)} %get-tuple-element.13), channel_id=1, source_target_pairs={{0,1},{1,0},{2,3},{3,2},{4,5},{5,4},{6,7},{7,6},{8,9},{9,8},{10,11... | collective-permute-start | bytes 3145736 | tf_op jit(solution)/shard_map/ppermute | solution.py:17
  54.2 24.9 %collective-permute-start.4 = (bf16[128,4096]{1,0:T(8,128)(2,1)S(1)}, bf16[128,4096]{1,0:T(8,128)(2,1)S(1)}, u32[]{:S(2)}, u32[]{:S(2)}) collective-permute-start(bf16[128,4096]{1,0:T(8,128)(2,1)S(1)} %collective-permute-done.3), channel_id=1, source_target_pairs={{0,2},{2,4},{4,6},{6,0},{1,3},{3,5},{5,7},{7,1},{8,10},{10,12},{12... | collective-permute-start | bytes 3145736 | tf_op jit(solution)/shard_map/ppermute | solution.py:17
  56.2 23.9 %collective-permute-start.5 = (bf16[128,4096]{1,0:T(8,128)(2,1)S(1)}, bf16[128,4096]{1,0:T(8,128)(2,1)S(1)}, u32[]{:S(2)}, u32[]{:S(2)}) collective-permute-start(bf16[128,4096]{1,0:T(8,128)(2,1)S(1)} %collective-permute-done.3), channel_id=1, source_target_pairs={{0,6},{2,0},{4,2},{6,4},{1,7},{3,1},{5,3},{7,5},{8,14},{10,8},{12,... | collective-permute-start | bytes 3145736 | tf_op jit(solution)/shard_map/ppermute | solution.py:17
  60.7 38.1 %collective-permute-start.6 = (bf16[128,4096]{1,0:T(8,128)(2,1)S(1)}, bf16[128,4096]{1,0:T(8,128)(2,1)S(1)}, u32[]{:S(2)}, u32[]{:S(2)}) collective-permute-start(bf16[128,4096]{1,0:T(8,128)(2,1)S(1)} %collective-permute-done.3), channel_id=1, source_target_pairs={{0,4},{2,6},{4,0},{6,2},{1,5},{3,7},{5,1},{7,3},{8,12},{10,14},{12... | collective-permute-start | bytes 3145736 | tf_op jit(solution)/shard_map/ppermute | solution.py:17
  105.9 1.9 copy-start
  107.9 73.7 %collective-permute-start.7 = (f32[4,8,64,256]{3,2,1,0:T(8,128)S(1)}, f32[4,8,64,256]{3,2,1,0:T(8,128)}, u32[]{:S(2)}, u32[]{:S(2)}) collective-permute-start(f32[4,8,64,256]{3,2,1,0:T(8,128)S(1)} %dynamic-slice_bitcast_fusion), channel_id=1, source_target_pairs={{0,8},{8,0},{1,9},{9,1},{2,10},{10,2},{3,11},{11,3},{4,12},{12,4},... | collective-permute-start | bytes 6291464 | tf_op jit(solution)/shard_map/ppermute | solution.py:17
  175.0 6.6 %copy-start.1 = (f32[4096,256]{1,0:T(8,128)S(1)}, f32[4096,256]{1,0:T(8,128)}, u32[]{:S(2)}) copy-start(f32[4096,256]{1,0:T(8,128)} %copy-done) | copy-start | bytes 12582916
  181.5 62.7 %copy-start.6 = (f32[64]{0:T(128)S(1)}, f32[64]{0:T(128)}, u32[]{:S(2)}) copy-start(f32[64]{0:T(128)} %param.11) | copy-start | bytes 772
  181.5 95.8 %copy-start.5 = (f32[256]{0:T(256)S(1)}, f32[256]{0:T(256)}, u32[]{:S(2)}) copy-start(f32[256]{0:T(256)} %param.10) | copy-start | bytes 3076
  183.7 18.7 %collective-permute-start.14 = (bf16[4,64,256]{2,1,0:T(8,128)(2,1)S(1)}, bf16[4,64,256]{2,1,0:T(8,128)(2,1)S(1)}, u32[]{:S(2)}, u32[]{:S(2)}) collective-permute-start(bf16[4,64,256]{2,1,0:T(8,128)(2,1)S(1)} %get-tuple-element.15), channel_id=1, source_target_pairs={{0,64},{16,80},{32,96},{48,112},{64,0},{80,16},{96,32},{112,48},{1... | collective-permute-start | bytes 393224 | tf_op jit(solution)/shard_map/ppermute | solution.py:17
  189.0 18.2 %collective-permute-start.13 = (bf16[4,64,256]{2,1,0:T(8,128)(2,1)S(1)}, bf16[4,64,256]{2,1,0:T(8,128)(2,1)S(1)}, u32[]{:S(2)}, u32[]{:S(2)}) collective-permute-start(bf16[4,64,256]{2,1,0:T(8,128)(2,1)S(1)} %get-tuple-element.16), channel_id=1, source_target_pairs={{0,80},{16,96},{32,112},{48,0},{64,16},{80,32},{96,48},{112,64},{1... | collective-permute-start | bytes 393224 | tf_op jit(solution)/shard_map/ppermute | solution.py:17
  191.5 17.7 %collective-permute-start.12 = (bf16[4,64,256]{2,1,0:T(8,128)(2,1)S(1)}, bf16[4,64,256]{2,1,0:T(8,128)(2,1)S(1)}, u32[]{:S(2)}, u32[]{:S(2)}) collective-permute-start(bf16[4,64,256]{2,1,0:T(8,128)(2,1)S(1)} %get-tuple-element.17), channel_id=1, source_target_pairs={{0,48},{16,64},{32,80},{48,96},{64,112},{80,0},{96,16},{112,32},{1... | collective-permute-start | bytes 393224 | tf_op jit(solution)/shard_map/ppermute | solution.py:17
  196.1 15.3 %collective-permute-start.11 = (bf16[4,64,256]{2,1,0:T(8,128)(2,1)S(1)}, bf16[4,64,256]{2,1,0:T(8,128)(2,1)S(1)}, u32[]{:S(2)}, u32[]{:S(2)}) collective-permute-start(bf16[4,64,256]{2,1,0:T(8,128)(2,1)S(1)} %get-tuple-element.18), channel_id=1, source_target_pairs={{0,96},{16,112},{32,0},{48,16},{64,32},{80,48},{96,64},{112,80},{1... | collective-permute-start | bytes 393224 | tf_op jit(solution)/shard_map/ppermute | solution.py:17
  200.4 11.0 %collective-permute-start.10 = (bf16[4,64,256]{2,1,0:T(8,128)(2,1)S(1)}, bf16[4,64,256]{2,1,0:T(8,128)(2,1)S(1)}, u32[]{:S(2)}, u32[]{:S(2)}) collective-permute-start(bf16[4,64,256]{2,1,0:T(8,128)(2,1)S(1)} %get-tuple-element.19), channel_id=1, source_target_pairs={{0,32},{16,48},{32,64},{48,80},{64,96},{80,112},{96,0},{112,16},{1... | collective-permute-start | bytes 393224 | tf_op jit(solution)/shard_map/ppermute | solution.py:17
  202.4 11.5 %collective-permute-start.9 = (bf16[4,64,256]{2,1,0:T(8,128)(2,1)S(1)}, bf16[4,64,256]{2,1,0:T(8,128)(2,1)S(1)}, u32[]{:S(2)}, u32[]{:S(2)}) collective-permute-start(bf16[4,64,256]{2,1,0:T(8,128)(2,1)S(1)} %get-tuple-element.20), channel_id=1, source_target_pairs={{0,112},{16,0},{32,16},{48,32},{64,48},{80,64},{96,80},{112,96},{1... | collective-permute-start | bytes 393224 | tf_op jit(solution)/shard_map/ppermute | solution.py:17
  207.2 7.5 %collective-permute-start.8 = (bf16[4,64,256]{2,1,0:T(8,128)(2,1)S(1)}, bf16[4,64,256]{2,1,0:T(8,128)(2,1)S(1)}, u32[]{:S(2)}, u32[]{:S(2)}) collective-permute-start(bf16[4,64,256]{2,1,0:T(8,128)(2,1)S(1)} %get-tuple-element.14), channel_id=1, source_target_pairs={{0,16},{16,32},{32,48},{48,64},{64,80},{80,96},{96,112},{112,0},{1... | collective-permute-start | bytes 393224 | tf_op jit(solution)/shard_map/ppermute | solution.py:17
  214.9 10.6 %collective-permute-start.17 = (f32[64,256]{1,0:T(8,128)S(1)}, f32[64,256]{1,0:T(8,128)S(1)}, u32[]{:S(2)}, u32[]{:S(2)}) collective-permute-start(f32[64,256]{1,0:T(8,128)S(1)} %get-tuple-element.22), channel_id=1, source_target_pairs={{0,256},{128,384},{256,0},{384,128},{1,257},{129,385},{257,1},{385... | collective-permute-start | bytes 196616 | tf_op jit(solution)/shard_map/ppermute | solution.py:17
  220.1 5.4 %collective-permute-start.16 = (f32[64,256]{1,0:T(8,128)S(1)}, f32[64,256]{1,0:T(8,128)S(1)}, u32[]{:S(2)}, u32[]{:S(2)}) collective-permute-start(f32[64,256]{1,0:T(8,128)S(1)} %get-tuple-element.23), channel_id=1, source_target_pairs={{0,384},{128,0},{256,128},{384,256},{1,385},{129,1},{257,129},{385... | collective-permute-start | bytes 196616 | tf_op jit(solution)/shard_map/ppermute | solution.py:17
  222.6 6.8 %collective-permute-start.15 = (f32[64,256]{1,0:T(8,128)S(1)}, f32[64,256]{1,0:T(8,128)S(1)}, u32[]{:S(2)}, u32[]{:S(2)}) collective-permute-start(f32[64,256]{1,0:T(8,128)S(1)} %get-tuple-element.21), channel_id=1, source_target_pairs={{0,128},{128,256},{256,384},{384,0},{1,129},{129,257},{257,385},{3... | collective-permute-start | bytes 196616 | tf_op jit(solution)/shard_map/ppermute | solution.py:17
  244.2 50.8 %copy-start.4 = (f32[64]{0:T(128)}, f32[64]{0:T(128)S(1)}, u32[]{:S(2)}) copy-start(f32[64]{0:T(128)S(1)} %multiply_add_fusion.1) | copy-start | bytes 772
  277.8 17.1 %copy-start.3 = (f32[256]{0:T(256)}, f32[256]{0:T(256)S(1)}, u32[]{:S(2)}) copy-start(f32[256]{0:T(256)S(1)} %get-tuple-element.7) | copy-start | bytes 3076
  285.2 9.8 %copy-start.2 = (bf16[8,128,256]{2,1,0:T(8,128)(2,1)}, bf16[8,128,256]{2,1,0:T(8,128)(2,1)S(1)}, u32[]{:S(2)}) copy-start(bf16[8,128,256]{2,1,0:T(8,128)(2,1)S(1)} %fusion.6) | copy-start | bytes 1572868
Sparse Core Ops, SparseCore 0:
  33.6 141.3 all-gather.1

commit v2 on v1

v2 whole, which is shorter than its diff:
```python
import jax
import jax.numpy as jnp
from jax import lax
from jax.sharding import Mesh, PartitionSpec as P

decay_rate = 0.9
square_eps = 1e-30

SPLIT = (("zb", 2), ("za", 2), ("y", 8), ("c", 2), ("x", 4), ("zh", 2))
SIZE = dict(SPLIT)
DP = ("zb", "za", "y", "c")
MP = ("x", "zh")


def shift(value, axis, step):
    size = SIZE[axis]
    return lax.ppermute(value, axis, [(i, (i + step) % size) for i in range(size)])


def flip(value, axis, mask=1):
    return lax.ppermute(value, axis, [(i, i ^ mask) for i in range(SIZE[axis])])


def shift_zl(value, step):
    return lax.ppermute(value, ("zb", "za"), [(i, (i + step) % 4) for i in range(4)])


def turn(value, cross):
    to = {"swap": lambda a, b: (b, a), "right": lambda a, b: (b, 1 - a), "left": lambda a, b: (1 - b, a)}[cross]
    pairs = []
    for a in range(2):
        for b in range(2):
            p, q = to(a, b)
            pairs.append((2 * a + b, 2 * p + q))
    return lax.ppermute(value, ("zb", "zh"), pairs)


def pick(value, index, axis=0):
    return lax.dynamic_index_in_dim(value, index, axis, keepdims=False)


def ordered(bit, mine, other, axis=0):
    first = jnp.where(bit == 0, mine, other)
    second = jnp.where(bit == 0, other, mine)
    return jnp.stack([first, second], axis=axis)


def per_device(context, cotangent, lengths, weight, row_stat, col_stat):
    groups = SIZE["zb"] * SIZE["za"] * SIZE["y"] * SIZE["c"]
    zb, za, y, c, x, zh = (lax.axis_index(name) for name, _ in SPLIT)
    seq_here = lengths.shape[0]
    tokens, width = cotangent.shape
    target_len = tokens // seq_here
    heads = context.shape[1]
    half = width // 2
    cols = width // groups
    position = jnp.arange(target_len, dtype=jnp.int32)
    inside = position[None, :] < lengths[:, None]
    shaped = cotangent.reshape(seq_here, target_len, width)
    masked = jnp.where(inside[:, :, None], shaped, jnp.zeros((), cotangent.dtype)).reshape(
        tokens, width
    )

    theirs = flip(lax.dynamic_slice_in_dim(masked, (1 - zh) * half, half, 1), "zh")
    mine = lax.dynamic_slice_in_dim(masked, zh * half, half, 1)
    steps = (1, 3, 2)
    blocks = [(x, zh, mine)] + [((x - s) % SIZE["x"], zh, shift(mine, "x", s)) for s in steps]
    context_other = flip(context, "zh")
    blocks += [(x, 1 - zh, theirs)]
    blocks += [((x - s) % SIZE["x"], 1 - zh, shift(theirs, "x", s)) for s in steps]
    gathered = jnp.zeros((SIZE["x"], SIZE["zh"], tokens, half), masked.dtype)
    for px, pz, block in blocks:
        gathered = lax.dynamic_update_slice(gathered, block[None, None], (px, pz, 0, 0))
    gathered = gathered.reshape(-1, half)
    both = ordered(zh, context, context_other, 1).reshape(context.shape[0], 2 * heads)

    slim = weight.T.astype(jnp.bfloat16)
    w = ordered(zb, turn(slim, "swap"), turn(slim, "left"), 1).reshape(cols, 2 * heads)
    w = ordered(za, w, flip(w, "za"))[:, None]
    for bit in range(3):
        other = flip(w, "y", 1 << bit)
        w = ordered((y >> bit) & 1, w, other, 1)
        w = w.reshape((2, -1) + w.shape[3:])
    w = ordered(c, w, flip(w, "c"), 2).reshape(half, 2 * heads)

    grad_t = lax.dot_general(
        gathered, both, (((0,), (0,)), ((), ())), preferred_element_type=jnp.float32
    )
    back = lax.dot_general(
        gathered, w, (((1,), (0,)), ((), ())), preferred_element_type=jnp.float32
    )
    back_mine = lax.dynamic_slice_in_dim(back, zh * heads, heads, 1)
    back_theirs = lax.dynamic_slice_in_dim(back, (1 - zh) * heads, heads, 1).astype(jnp.bfloat16)
    context_grad = (back_mine + flip(back_theirs, "zh").astype(jnp.float32)).astype(jnp.bfloat16)

    parts = grad_t.reshape(SIZE["za"], SIZE["y"], SIZE["c"], cols, 2 * heads)
    parts = pick(parts, c, 2) + flip(pick(parts, 1 - c, 2), "c")
    narrow = parts.astype(jnp.bfloat16)
    total = pick(parts, y, 1)
    for s in (1, 7, 2, 6, 3, 5, 4):
        total = total + shift(pick(narrow, (y + s) % SIZE["y"], 1), "y", s).astype(jnp.float32)
    total = total.reshape(SIZE["za"], 2, cols // 2, 2 * heads)
    zl = zb * 2 + za

    def piece(i):
        return lax.dynamic_slice(total, (i % 2, i // 2, 0, 0), (1, 1) + total.shape[2:])[0, 0]

    part = piece(zl)
    for s in (1, 3, 2):
        part = part + shift_zl(piece((zl + s) % 4), s)
    grad = part / groups

    two = grad.reshape(cols // 2, 2, heads)
    grad_own = ordered(zh, turn(pick(two, zb, 1), "swap"), turn(pick(two, 1 - zb, 1), "right"))
    grad_own = grad_own.reshape(cols, heads)

    square = grad * grad + square_eps
    inner_total = heads * SIZE["x"] * SIZE["zh"]
    stat_here = turn(col_stat, "swap")
    stat_here = lax.dynamic_slice_in_dim(stat_here, zb * (cols // 2), cols // 2, 0)
    col_all = lax.psum(jnp.sum(square, axis=1), "x")
    col_here = decay_rate * stat_here + (1.0 - decay_rate) * (col_all / inner_total)
    scaled = grad * grad / col_here[:, None]
    rows = jnp.concatenate([jnp.sum(square, axis=0), jnp.sum(scaled, axis=0)])
    rows = lax.psum(lax.psum(rows, "c"), "y")
    slots = jnp.zeros((SIZE["zh"], SIZE["za"], SIZE["zb"], cols // 2), jnp.float32)
    slots = lax.dynamic_update_slice(slots, col_here[None, None, None], (zh, za, zb, 0))
    rows = lax.psum(jnp.concatenate([rows, slots.reshape(-1)]), ("zb", "za", "zh"))
    slots = rows[4 * heads :].reshape(slots.shape)
    col_new = lax.dynamic_slice(slots, (zb, za, 0, 0), (1, 1, 2, cols // 2)).reshape(cols)
    row_all = rows[: 2 * heads].reshape(2, heads)
    row_scaled = rows[2 * heads : 4 * heads].reshape(2, heads)
    stat_rows = jnp.stack([row_stat, flip(row_stat, "zh")])
    stat_rows = jnp.where(zh == 0, stat_rows, stat_rows[::-1])
    rows_new = decay_rate * stat_rows + (1.0 - decay_rate) * (row_all / width)
    square_sum = lax.psum(jnp.sum(row_scaled / rows_new), "x")
    row_new = pick(rows_new, zh)
    raw_update = grad_own / jnp.sqrt(row_new[None, :] * col_new[:, None])
    update_rms = jnp.sqrt(square_sum / (inner_total * width))
    update = (raw_update / jnp.maximum(1.0, update_rms)).T
    return (context_grad, update, row_new, col_new)


def solution(mesh):
    names = tuple(name for name, _ in SPLIT)
    fine = Mesh(mesh.devices.reshape(tuple(size for _, size in SPLIT)), names)
    in_specs = (P(DP, MP), P(DP + MP, None), P(DP + MP), P(MP, DP), P(MP), P(DP))
    out_specs = (P(DP, MP), P(MP, DP), P(MP), P(DP))
    return jax.shard_map(
        per_device, mesh=fine, in_specs=in_specs, out_specs=out_specs, check_vma=False
    )
```

time: 305 us -> 299 us (0.980)
  the two profiles are of different devices: /device:TPU:1 before, /device:TPU:2 now
where the time goes in v2:
time: 299 us; the launch traced here: 297 us
  starting transfers between devices  150 us (50%)
  blocking collectives  60.8 us (20%)
  waiting for transfers between devices  32.7 us (11%)
  local copies, waits for them, and re-layouts  27 us (9%)
  other arithmetic  15.1 us (5%)
  matrix products  9.18 us (3%)
    ppermute x13, starting transfers between devices, shift(): lax.ppermute(value, axis, [(i, (i + step) % size) for i in range(size)])  45.8 us
    ppermute x10, starting transfers between devices, flip(): return lax.ppermute(value, axis, [(i, i ^ mask) for i in range(SIZE[axis])])  41 us
    ppermute x3, starting transfers between devices, shift_zl(): lax.ppermute(value, ('zb', 'za'), [(i, (i + step) % 4) for i in range(4)])  37.8 us
    ppermute x5, starting transfers between devices, turn(): return lax.ppermute(value, ('zb', 'zh'), pairs)  25.4 us
    psum x1, blocking collectives, per_device(): lax.psum(jnp.concatenate([rows, slots.reshape(-1)]), ('zb', 'za', 'zh'))  23 us
    ppermute x10, waiting for transfers between devices, flip(): return lax.ppermute(value, axis, [(i, i ^ mask) for i in range(SIZE[axis])])  22.3 us
    psum x2, blocking collectives, per_device(): rows = lax.psum(lax.psum(rows, 'c'), 'y')  16.8 us
    psum x1, blocking collectives, per_device(): square_sum = lax.psum(jnp.sum(row_scaled / rows_new), 'x')  11.6 us
  transfers between devices with their start and end apart: 31, of which 8 were waited for; matrix products, arithmetic and copies ran while one was open for 14% of the time, Pallas kernels for 0%

profile of v2, /device:TPU:2, one launch (start us, length us, event | category | flops | bytes accessed | tf_op | source)
XLA Modules:
  0.0 297.0 jit_solution(10714384069120881430)
XLA Ops:
  0.6 0.8 convert_bitcast_fusion
  2.1 12.7 %collective-permute-start.8 = (bf16[64,256]{1,0:T(8,128)(2,1)S(1)}, bf16[64,256]{1,0:T(8,128)(2,1)S(1)}, u32[]{:S(2)}, u32[]{:S(2)}) collective-permute-start(bf16[64,256]{1,0:T(8,128)(2,1)S(1)} %convert_bitcast_fusion), channel_id=1, source_target_pairs={{0,256},{1,0},{256,257},{257,1},{2,258},{3,2},{258,259},{259,3},{4... | collective-permute-start | bytes 98312 | tf_op jit(solution)/shard_map/ppermute | solution.py:35
  14.9 1.6 collective-permute-done.8
  16.5 3.6 %collective-permute-start.9 = (bf16[64,512]{1,0:T(8,128)(2,1)S(1)}, bf16[64,512]{1,0:T(8,128)(2,1)S(1)}, u32[]{:S(2)}, u32[]{:S(2)}) collective-permute-start(bf16[64,512]{1,0:T(8,128)(2,1)S(1)} %bitcast.153), channel_id=1, source_target_pairs={{0,128},{128,0},{1,129},{129,1},{2,130},{130,2},{3,131},{131,3},{4... | collective-permute-start | bytes 196616 | tf_op jit(solution)/shard_map/ppermute | solution.py:21
  20.9 1.7 collective-permute-done.9
  22.7 3.6 %collective-permute-start.10 = (bf16[2,1,64,512]{3,2,0,1:T(8,128)(2,1)S(1)}, bf16[2,1,64,512]{3,2,0,1:T(8,128)(2,1)S(1)}, u32[]{:S(2)}, u32[]{:S(2)}) collective-permute-start(bf16[2,1,64,512]{3,2,0,1:T(8,128)(2,1)S(1)} %maximum_bitcast_fusion.1), channel_id=1, source_target_pairs={{0,16},{16,0},{32,48},{48,32},{64,80},{80,64},{96,112},{112,96},{1... | collective-permute-start | bytes 393224 | tf_op jit(solution)/shard_map/ppermute | solution.py:21
  26.3 1.4 broadcast_select_fusion
  27.7 2.0 collective-permute-done.10
  29.8 4.5 %collective-permute-start.11 = (bf16[2,2,64,512]{3,2,0,1:T(8,128)(2,1)S(1)}, bf16[2,2,64,512]{3,2,0,1:T(8,128)(2,1)}, u32[]{:S(2)}, u32[]{:S(2)}) collective-permute-start(bf16[2,2,64,512]{3,2,0,1:T(8,128)(2,1)S(1)} %maximum_bitcast_fusion), channel_id=1, source_target_pairs={{0,32},{16,48},{32,0},{48,16},{64,96},{80,112},{96,64},{112,80},{1... | collective-permute-start | bytes 786440 | tf_op jit(solution)/shard_map/ppermute | solution.py:21
  34.3 2.6 broadcast_in_dim.53
  36.8 0.9 bitcast_dynamic-update-slice_fusion.7
  37.7 3.4 %collective-permute-start = (bf16[128,2048]{1,0:T(8,128)(2,1)S(1)}, bf16[128,2048]{1,0:T(8,128)(2,1)}, u32[]{:S(2)}, u32[]{:S(2)}) collective-permute-start(bf16[128,2048]{1,0:T(8,128)(2,1)S(1)} %get-tuple-element.13), channel_id=1, source_target_pairs={{0,2},{2,4},{4,6},{6,0},{1,3},{3,5},{5,7},{7,1},{8,10},{10,12},{12... | collective-permute-start | bytes 1572872 | tf_op jit(solution)/shard_map/ppermute | solution.py:17
  41.1 2.4 collective-permute-start.1
  43.6 4.0 %collective-permute-start.2 = (bf16[128,2048]{1,0:T(8,128)(2,1)S(1)}, bf16[128,2048]{1,0:T(8,128)(2,1)}, u32[]{:S(2)}, u32[]{:S(2)}) collective-permute-start(bf16[128,2048]{1,0:T(8,128)(2,1)S(1)} %get-tuple-element.13), channel_id=1, source_target_pairs={{0,4},{2,6},{4,0},{6,2},{1,5},{3,7},{5,1},{7,3},{8,12},{10,14},{12... | collective-permute-start | bytes 1572872 | tf_op jit(solution)/shard_map/ppermute | solution.py:17
  47.6 4.8 %collective-permute-start.15 = (bf16[1024,256]{1,0:T(8,128)(2,1)S(1)}, bf16[1024,256]{1,0:T(8,128)(2,1)S(1)}, u32[]{:S(2)}, u32[]{:S(2)}) collective-permute-start(bf16[1024,256]{1,0:T(8,128)(2,1)S(1)} %copy-done.3), channel_id=1, source_target_pairs={{0,1},{1,0},{2,3},{3,2},{4,5},{5,4},{6,7},{7,6},{8,9},{9,8},{10,11... | collective-permute-start | bytes 1572872 | tf_op jit(solution)/shard_map/ppermute | solution.py:21
  52.5 0.8 constant_dynamic-slice_fusion.4
  53.3 5.0 %collective-permute-start.3 = (bf16[128,2048]{1,0:T(8,128)(2,1)}, bf16[128,2048]{1,0:T(8,128)(2,1)}, u32[]{:S(2)}, u32[]{:S(2)}) collective-permute-start(bf16[128,2048]{1,0:T(8,128)(2,1)} %constant_dynamic-slice_fusion.4), channel_id=1, source_target_pairs={{0,1},{1,0},{2,3},{3,2},{4,5},{5,4},{6,7},{7,6},{8,9},{9,8},{10,11... | collective-permute-start | bytes 1572872 | tf_op jit(solution)/shard_map/ppermute | solution.py:21
  58.3 1.0 select_bitcast_fusion.7
  59.4 9.0 %collective-permute-done.15 = bf16[1024,256]{1,0:T(8,128)(2,1)S(1)} collective-permute-done((bf16[1024,256]{1,0:T(8,128)(2,1)S(1)}, bf16[1024,256]{1,0:T(8,128)(2,1)S(1)}, u32[]{:S(2)}, u32[]{:S(2)}) %collective-permute-start.15) | collective-permute-done | bytes 524320 | tf_op jit(solution)/shard_map/ppermute | solution.py:21
  68.4 5.9 %collective-permute-start.12 = (bf16[2,4,64,512]{3,2,0,1:T(8,128)(2,1)S(1)}, bf16[2,4,64,512]{3,2,0,1:T(8,128)(2,1)}, u32[]{:S(2)}, u32[]{:S(2)}) collective-permute-start(bf16[2,4,64,512]{3,2,0,1:T(8,128)(2,1)S(1)} %bitcast.149), channel_id=1, source_target_pairs={{0,64},{16,80},{32,96},{48,112},{64,0},{80,16},{96,32},{112,48},{1... | collective-permute-start | bytes 1572872 | tf_op jit(solution)/shard_map/ppermute | solution.py:21
  74.5 1.1 copy.28
  76.3 3.0 %collective-permute-start.4 = (bf16[128,2048]{1,0:T(8,128)(2,1)}, bf16[128,2048]{1,0:T(8,128)(2,1)S(1)}, u32[]{:S(2)}, u32[]{:S(2)}) collective-permute-start(bf16[128,2048]{1,0:T(8,128)(2,1)} %collective-permute-done.3), channel_id=1, source_target_pairs={{0,2},{2,4},{4,6},{6,0},{1,3},{3,5},{5,7},{7,1},{8,10},{10,12},{12... | collective-permute-start | bytes 1572872 | tf_op jit(solution)/shard_map/ppermute | solution.py:17
  79.4 2.8 collective-permute-start.5
  82.2 1.9 bitcast_dynamic-update-slice_fusion.6
  84.1 3.4 %collective-permute-start.6 = (bf16[128,2048]{1,0:T(8,128)(2,1)}, bf16[128,2048]{1,0:T(8,128)(2,1)S(1)}, u32[]{:S(2)}, u32[]{:S(2)}) collective-permute-start(bf16[128,2048]{1,0:T(8,128)(2,1)} %collective-permute-done.3), channel_id=1, source_target_pairs={{0,4},{2,6},{4,0},{6,2},{1,5},{3,7},{5,1},{7,3},{8,12},{10,14},{12... | collective-permute-start | bytes 1572872 | tf_op jit(solution)/shard_map/ppermute | solution.py:17
  87.5 1.9 bitcast_dynamic-update-slice_fusion.5
  89.4 1.9 bitcast_dynamic-update-slice_fusion.4
  91.3 1.9 bitcast_dynamic-update-slice_fusion.3
  93.2 1.1 select_bitcast_fusion.5
  94.5 1.9 collective-permute-start.13
  96.5 0.8 bitcast_dynamic-update-slice_fusion.2
  98.2 1.1 collective-permute-done.6
  99.2 0.9 bitcast_dynamic-update-slice_fusion
  100.1 6.4 %copy.27 = bf16[2048,1024]{1,0:T(8,128)(2,1)} copy(bf16[2048,1024]{0,1:T(8,128)(2,1)} %bitcast.28) | data formatting | bytes 8388608 | tf_op jit(solution)/shard_map/dot_general | solution.py:86
  106.5 4.5 %fusion = f32[2,8,2,64,512]{4,3,2,1,0:T(8,128)S(1)} fusion(bf16[2,8,2,64,1024]{4,3,2,1,0:T(8,128)(2,1)} %bitcast.148, bf16[1024,512,1,1,1]{1,0,2,3,4:T(8,128)(2,1)S(1)} %reshape.112), kind=kOutput, calls=%fused_computation.5 | convolution fusion | flops 2147483648 | bytes 9437184 | tf_op jit(solution)/shard_map/dot_general | solution.py:86
  111.1 1.9 copy-done
  113.2 1.9 collective-permute-start.16
  115.2 1.4 select_bitcast_fusion.1
  116.8 4.7 %fusion.14 = f32[1024,512]{1,0:T(8,128)S(1)} fusion(bf16[1024,2048]{1,0:T(8,128)(2,1)} %bitcast.8, bf16[2048,512]{1,0:T(8,128)(2,1)S(1)} %bitcast.150), kind=kOutput, calls=%fused_computation.83 | convolution fusion | flops 2147483648 | bytes 8388608 | tf_op jit(solution)/shard_map/dot_general | solution.py:89
  121.5 2.8 fusion.13
  125.1 5.9 %collective-permute-start.23 = (bf16[2,64,512]{2,1,0:T(8,128)(2,1)S(1)}, bf16[2,64,512]{2,1,0:T(8,128)(2,1)}, u32[]{:S(2)}, u32[]{:S(2)}) collective-permute-start(bf16[2,64,512]{2,1,0:T(8,128)(2,1)S(1)} %get-tuple-element.17), channel_id=1, source_target_pairs={{0,64},{16,80},{32,96},{48,112},{64,0},{80,16},{96,32},{112,48},{1... | collective-permute-start | bytes 393224 | tf_op jit(solution)/shard_map/ppermute | solution.py:17
  131.0 3.9 %collective-permute-start.22 = (bf16[2,64,512]{2,1,0:T(8,128)(2,1)S(1)}, bf16[2,64,512]{2,1,0:T(8,128)(2,1)}, u32[]{:S(2)}, u32[]{:S(2)}) collective-permute-start(bf16[2,64,512]{2,1,0:T(8,128)(2,1)S(1)} %get-tuple-element.18), channel_id=1, source_target_pairs={{0,80},{16,96},{32,112},{48,0},{64,16},{80,32},{96,48},{112,64},{1... | collective-permute-start | bytes 393224 | tf_op jit(solution)/shard_map/ppermute | solution.py:17
  135.0 3.7 %collective-permute-start.21 = (bf16[2,64,512]{2,1,0:T(8,128)(2,1)S(1)}, bf16[2,64,512]{2,1,0:T(8,128)(2,1)S(1)}, u32[]{:S(2)}, u32[]{:S(2)}) collective-permute-start(bf16[2,64,512]{2,1,0:T(8,128)(2,1)S(1)} %get-tuple-element.19), channel_id=1, source_target_pairs={{0,48},{16,64},{32,80},{48,96},{64,112},{80,0},{96,16},{112,32},{1... | collective-permute-start | bytes 393224 | tf_op jit(solution)/shard_map/ppermute | solution.py:17
  138.8 4.9 %collective-permute-start.14 = (bf16[1024,256]{1,0:T(8,128)(2,1)S(1)}, bf16[1024,256]{1,0:T(8,128)(2,1)S(1)}, u32[]{:S(2)}, u32[]{:S(2)}) collective-permute-start(bf16[1024,256]{1,0:T(8,128)(2,1)S(1)} %dynamic-slice_convert_fusion), channel_id=1, source_target_pairs={{0,1},{1,0},{2,3},{3,2},{4,5},{5,4},{6,7},{7,6},{8,9},{9,8},{10,11... | collective-permute-start | bytes 1572872 | tf_op jit(solution)/shard_map/ppermute | solution.py:21
  143.7 4.8 %collective-permute-start.29 = (f32[256]{0:T(256)S(1)}, f32[256]{0:T(256)S(1)}, u32[]{:S(2)}, u32[]{:S(2)}) collective-permute-start(f32[256]{0:T(256)S(1)} %copy-done.6), channel_id=1, source_target_pairs={{0,1},{1,0},{2,3},{3,2},{4,5},{5,4},{6,7},{7,6},{8,9},{9,8},{10,11... | collective-permute-start | bytes 3080 | tf_op jit(solution)/shard_map/ppermute | solution.py:21
  148.6 9.6 %collective-permute-done.29 = f32[256]{0:T(256)S(1)} collective-permute-done((f32[256]{0:T(256)S(1)}, f32[256]{0:T(256)S(1)}, u32[]{:S(2)}, u32[]{:S(2)}) %collective-permute-start.29) | collective-permute-done | bytes 1056 | tf_op jit(solution)/shard_map/ppermute | solution.py:21
  158.1 3.7 %collective-permute-start.20 = (bf16[2,64,512]{2,1,0:T(8,128)(2,1)}, bf16[2,64,512]{2,1,0:T(8,128)(2,1)}, u32[]{:S(2)}, u32[]{:S(2)}) collective-permute-start(bf16[2,64,512]{2,1,0:T(8,128)(2,1)} %get-tuple-element.20), channel_id=1, source_target_pairs={{0,96},{16,112},{32,0},{48,16},{64,32},{80,48},{96,64},{112,80},{1... | collective-permute-start | bytes 393224 | tf_op jit(solution)/shard_map/ppermute | solution.py:17
  161.9 3.5 %collective-permute-start.19 = (bf16[2,64,512]{2,1,0:T(8,128)(2,1)S(1)}, bf16[2,64,512]{2,1,0:T(8,128)(2,1)}, u32[]{:S(2)}, u32[]{:S(2)}) collective-permute-start(bf16[2,64,512]{2,1,0:T(8,128)(2,1)S(1)} %get-tuple-element.21), channel_id=1, source_target_pairs={{0,32},{16,48},{32,64},{48,80},{64,96},{80,112},{96,0},{112,16},{1... | collective-permute-start | bytes 393224 | tf_op jit(solution)/shard_map/ppermute | solution.py:17
  165.3 4.0 %collective-permute-start.18 = (bf16[2,64,512]{2,1,0:T(8,128)(2,1)S(1)}, bf16[2,64,512]{2,1,0:T(8,128)(2,1)}, u32[]{:S(2)}, u32[]{:S(2)}) collective-permute-start(bf16[2,64,512]{2,1,0:T(8,128)(2,1)S(1)} %get-tuple-element.22), channel_id=1, source_target_pairs={{0,112},{16,0},{32,16},{48,32},{64,48},{80,64},{96,80},{112,96},{1... | collective-permute-start | bytes 393224 | tf_op jit(solution)/shard_map/ppermute | solution.py:17
  170.0 1.9 collective-permute-start.17
  172.2 1.3 collective-permute-start.30
  173.5 4.6 %collective-permute-done.17 = bf16[2,64,512]{2,1,0:T(8,128)(2,1)} collective-permute-done((bf16[2,64,512]{2,1,0:T(8,128)(2,1)S(1)}, bf16[2,64,512]{2,1,0:T(8,128)(2,1)}, u32[]{:S(2)}, u32[]{:S(2)}) %collective-permute-start.17) | collective-permute-done | bytes 131104 | tf_op jit(solution)/shard_map/ppermute | solution.py:17
  178.1 1.4 fusion.7
  179.6 31.9 %collective-permute-start.26 = (f32[32,512]{1,0:T(8,128)S(1)}, f32[32,512]{1,0:T(8,128)S(1)}, u32[]{:S(2)}, u32[]{:S(2)}) collective-permute-start(f32[32,512]{1,0:T(8,128)S(1)} %get-tuple-element.30), channel_id=1, source_target_pairs={{0,256},{128,384},{256,0},{384,128},{1,257},{129,385},{257,1},{385... | collective-permute-start | bytes 196616 | tf_op jit(solution)/shard_map/ppermute | solution.py:25
  211.5 3.1 %collective-permute-start.25 = (f32[32,512]{1,0:T(8,128)S(1)}, f32[32,512]{1,0:T(8,128)S(1)}, u32[]{:S(2)}, u32[]{:S(2)}) collective-permute-start(f32[32,512]{1,0:T(8,128)S(1)} %get-tuple-element.31), channel_id=1, source_target_pairs={{0,384},{128,0},{256,128},{384,256},{1,385},{129,1},{257,129},{385... | collective-permute-start | bytes 196616 | tf_op jit(solution)/shard_map/ppermute | solution.py:25
  214.6 2.7 collective-permute-start.24
  217.4 2.1 add_convert_fusion
  219.5 3.1 %collective-permute-done.24 = f32[32,512]{1,0:T(8,128)S(1)} collective-permute-done((f32[32,512]{1,0:T(8,128)S(1)}, f32[32,512]{1,0:T(8,128)S(1)}, u32[]{:S(2)}, u32[]{:S(2)}) %collective-permute-start.24) | collective-permute-done | bytes 65568 | tf_op jit(solution)/shard_map/ppermute | solution.py:25
  222.8 9.4 %psum.35 = f32[32]{0:T(128)S(1)} all-reduce(f32[32]{0:T(128)S(1)} %get-tuple-element.8), channel_id=1, replica_groups=mesh['zb'=2,'za'=2,'y'=8,'c'=2,'x'=4,'zh'=2] {'x'}, use_global_device_ids=true, to_apply=%region_2.3 | all-reduce | flops 32 | bytes 256 | tf_op jit(solution)/shard_map/psum | solution.py:121
  232.5 2.5 psum.36
  235.0 14.3 %psum.37 = f32[1024]{0:T(1024)S(1)} all-reduce(f32[1024]{0:T(1024)S(1)} %psum.36), channel_id=1, replica_groups=mesh['zb'=2,'za'=2,'y'=8,'c'=2,'x'=4,'zh'=2] {'y'}, use_global_device_ids=true, to_apply=%region_5.6 | all-reduce | flops 1024 | bytes 8192 | tf_op jit(solution)/shard_map/psum | solution.py:125
  249.3 23.0 %psum.38 = f32[1280]{0:T(1024)S(1)} all-reduce(f32[1280]{0:T(1024)S(1)} %pad_maximum_fusion.5), channel_id=1, replica_groups=mesh['zb'=2,'za'=2,'y'=8,'c'=2,'x'=4,'zh'=2] {'zb','za','zh'}, use_global_device_ids=true, to_apply=%region_6.7 | all-reduce | flops 1280 | bytes 10240 | tf_op jit(solution)/shard_map/psum | solution.py:128
  273.1 10.1 %collective-permute-start.28 = (f32[32,256]{1,0:T(8,128)S(1)}, f32[32,256]{1,0:T(8,128)S(1)}, u32[]{:S(2)}, u32[]{:S(2)}) collective-permute-start(f32[32,256]{1,0:T(8,128)S(1)} %bitcast.157), channel_id=1, source_target_pairs={{0,1},{1,257},{256,0},{257,256},{2,3},{3,259},{258,2},{259,258},{4... | collective-permute-start | bytes 98312 | tf_op jit(solution)/shard_map/ppermute | solution.py:35
  283.9 11.6 %psum.39 = f32[]{:T(128)} all-reduce(f32[]{:T(128)} %get-tuple-element.6), channel_id=1, replica_groups=mesh['zb'=2,'za'=2,'y'=8,'c'=2,'x'=4,'zh'=2] {'x'}, use_global_device_ids=true, to_apply=%region_8.9 | all-reduce | flops 1 | bytes 8 | tf_op jit(solution)/shard_map/psum | solution.py:136
  (87 shorter events, 8.3 us)
Async XLA Ops:
  1.5 13.4 %collective-permute-start.7 = (bf16[64,256]{1,0:T(8,128)(2,1)S(1)}, bf16[64,256]{1,0:T(8,128)(2,1)S(1)}, u32[]{:S(2)}, u32[]{:S(2)}) collective-permute-start(bf16[64,256]{1,0:T(8,128)(2,1)S(1)} %convert_bitcast_fusion), channel_id=1, source_target_pairs={{0,0},{1,256},{256,1},{257,257},{2,2},{3,258},{258,3},{259,259},{4... | collective-permute-start | bytes 98312 | tf_op jit(solution)/shard_map/ppermute | solution.py:35
  2.1 14.3 %collective-permute-start.8 = (bf16[64,256]{1,0:T(8,128)(2,1)S(1)}, bf16[64,256]{1,0:T(8,128)(2,1)S(1)}, u32[]{:S(2)}, u32[]{:S(2)}) collective-permute-start(bf16[64,256]{1,0:T(8,128)(2,1)S(1)} %convert_bitcast_fusion), channel_id=1, source_target_pairs={{0,256},{1,0},{256,257},{257,1},{2,258},{3,2},{258,259},{259,3},{4... | collective-permute-start | bytes 98312 | tf_op jit(solution)/shard_map/ppermute | solution.py:35
  16.5 6.2 %collective-permute-start.9 = (bf16[64,512]{1,0:T(8,128)(2,1)S(1)}, bf16[64,512]{1,0:T(8,128)(2,1)S(1)}, u32[]{:S(2)}, u32[]{:S(2)}) collective-permute-start(bf16[64,512]{1,0:T(8,128)(2,1)S(1)} %bitcast.153), channel_id=1, source_target_pairs={{0,128},{128,0},{1,129},{129,1},{2,130},{130,2},{3,131},{131,3},{4... | collective-permute-start | bytes 196616 | tf_op jit(solution)/shard_map/ppermute | solution.py:21
  22.7 24.9 %copy-start.3 = (bf16[1024,256]{1,0:T(8,128)(2,1)S(1)}, bf16[1024,256]{1,0:T(8,128)(2,1)}, u32[]{:S(2)}) copy-start(bf16[1024,256]{1,0:T(8,128)(2,1)} %param.6) | copy-start | bytes 1572868
  22.7 7.0 %collective-permute-start.10 = (bf16[2,1,64,512]{3,2,0,1:T(8,128)(2,1)S(1)}, bf16[2,1,64,512]{3,2,0,1:T(8,128)(2,1)S(1)}, u32[]{:S(2)}, u32[]{:S(2)}) collective-permute-start(bf16[2,1,64,512]{3,2,0,1:T(8,128)(2,1)S(1)} %maximum_bitcast_fusion.1), channel_id=1, source_target_pairs={{0,16},{16,0},{32,48},{48,32},{64,80},{80,64},{96,112},{112,96},{1... | collective-permute-start | bytes 393224 | tf_op jit(solution)/shard_map/ppermute | solution.py:21
  29.8 23.6 %collective-permute-start.11 = (bf16[2,2,64,512]{3,2,0,1:T(8,128)(2,1)S(1)}, bf16[2,2,64,512]{3,2,0,1:T(8,128)(2,1)}, u32[]{:S(2)}, u32[]{:S(2)}) collective-permute-start(bf16[2,2,64,512]{3,2,0,1:T(8,128)(2,1)S(1)} %maximum_bitcast_fusion), channel_id=1, source_target_pairs={{0,32},{16,48},{32,0},{48,16},{64,96},{80,112},{96,64},{112,80},{1... | collective-permute-start | bytes 786440 | tf_op jit(solution)/shard_map/ppermute | solution.py:21
  37.7 41.6 %collective-permute-start = (bf16[128,2048]{1,0:T(8,128)(2,1)S(1)}, bf16[128,2048]{1,0:T(8,128)(2,1)}, u32[]{:S(2)}, u32[]{:S(2)}) collective-permute-start(bf16[128,2048]{1,0:T(8,128)(2,1)S(1)} %get-tuple-element.13), channel_id=1, source_target_pairs={{0,2},{2,4},{4,6},{6,0},{1,3},{3,5},{5,7},{7,1},{8,10},{10,12},{12... | collective-permute-start | bytes 1572872 | tf_op jit(solution)/shard_map/ppermute | solution.py:17
  41.1 42.9 %collective-permute-start.1 = (bf16[128,2048]{1,0:T(8,128)(2,1)S(1)}, bf16[128,2048]{1,0:T(8,128)(2,1)}, u32[]{:S(2)}, u32[]{:S(2)}) collective-permute-start(bf16[128,2048]{1,0:T(8,128)(2,1)S(1)} %get-tuple-element.13), channel_id=1, source_target_pairs={{0,6},{2,0},{4,2},{6,4},{1,7},{3,1},{5,3},{7,5},{8,14},{10,8},{12,... | collective-permute-start | bytes 1572872 | tf_op jit(solution)/shard_map/ppermute | solution.py:17
  43.6 45.8 %collective-permute-start.2 = (bf16[128,2048]{1,0:T(8,128)(2,1)S(1)}, bf16[128,2048]{1,0:T(8,128)(2,1)}, u32[]{:S(2)}, u32[]{:S(2)}) collective-permute-start(bf16[128,2048]{1,0:T(8,128)(2,1)S(1)} %get-tuple-element.13), channel_id=1, source_target_pairs={{0,4},{2,6},{4,0},{6,2},{1,5},{3,7},{5,1},{7,3},{8,12},{10,14},{12... | collective-permute-start | bytes 1572872 | tf_op jit(solution)/shard_map/ppermute | solution.py:17
  47.6 20.7 %collective-permute-start.15 = (bf16[1024,256]{1,0:T(8,128)(2,1)S(1)}, bf16[1024,256]{1,0:T(8,128)(2,1)S(1)}, u32[]{:S(2)}, u32[]{:S(2)}) collective-permute-start(bf16[1024,256]{1,0:T(8,128)(2,1)S(1)} %copy-done.3), channel_id=1, source_target_pairs={{0,1},{1,0},{2,3},{3,2},{4,5},{5,4},{6,7},{7,6},{8,9},{9,8},{10,11... | collective-permute-start | bytes 1572872 | tf_op jit(solution)/shard_map/ppermute | solution.py:21
  53.3 23.0 %collective-permute-start.3 = (bf16[128,2048]{1,0:T(8,128)(2,1)}, bf16[128,2048]{1,0:T(8,128)(2,1)}, u32[]{:S(2)}, u32[]{:S(2)}) collective-permute-start(bf16[128,2048]{1,0:T(8,128)(2,1)} %constant_dynamic-slice_fusion.4), channel_id=1, source_target_pairs={{0,1},{1,0},{2,3},{3,2},{4,5},{5,4},{6,7},{7,6},{8,9},{9,8},{10,11... | collective-permute-start | bytes 1572872 | tf_op jit(solution)/shard_map/ppermute | solution.py:21
  68.4 24.8 %collective-permute-start.12 = (bf16[2,4,64,512]{3,2,0,1:T(8,128)(2,1)S(1)}, bf16[2,4,64,512]{3,2,0,1:T(8,128)(2,1)}, u32[]{:S(2)}, u32[]{:S(2)}) collective-permute-start(bf16[2,4,64,512]{3,2,0,1:T(8,128)(2,1)S(1)} %bitcast.149), channel_id=1, source_target_pairs={{0,64},{16,80},{32,96},{48,112},{64,0},{80,16},{96,32},{112,48},{1... | collective-permute-start | bytes 1572872 | tf_op jit(solution)/shard_map/ppermute | solution.py:21
  76.3 20.2 %collective-permute-start.4 = (bf16[128,2048]{1,0:T(8,128)(2,1)}, bf16[128,2048]{1,0:T(8,128)(2,1)S(1)}, u32[]{:S(2)}, u32[]{:S(2)}) collective-permute-start(bf16[128,2048]{1,0:T(8,128)(2,1)} %collective-permute-done.3), channel_id=1, source_target_pairs={{0,2},{2,4},{4,6},{6,0},{1,3},{3,5},{5,7},{7,1},{8,10},{10,12},{12... | collective-permute-start | bytes 1572872 | tf_op jit(solution)/shard_map/ppermute | solution.py:17
  79.4 18.0 %collective-permute-start.5 = (bf16[128,2048]{1,0:T(8,128)(2,1)}, bf16[128,2048]{1,0:T(8,128)(2,1)S(1)}, u32[]{:S(2)}, u32[]{:S(2)}) collective-permute-start(bf16[128,2048]{1,0:T(8,128)(2,1)} %collective-permute-done.3), channel_id=1, source_target_pairs={{0,6},{2,0},{4,2},{6,4},{1,7},{3,1},{5,3},{7,5},{8,14},{10,8},{12,... | collective-permute-start | bytes 1572872 | tf_op jit(solution)/shard_map/ppermute | solution.py:17
  84.1 15.2 %collective-permute-start.6 = (bf16[128,2048]{1,0:T(8,128)(2,1)}, bf16[128,2048]{1,0:T(8,128)(2,1)S(1)}, u32[]{:S(2)}, u32[]{:S(2)}) collective-permute-start(bf16[128,2048]{1,0:T(8,128)(2,1)} %collective-permute-done.3), channel_id=1, source_target_pairs={{0,4},{2,6},{4,0},{6,2},{1,5},{3,7},{5,1},{7,3},{8,12},{10,14},{12... | collective-permute-start | bytes 1572872 | tf_op jit(solution)/shard_map/ppermute | solution.py:17
  94.5 20.7 %collective-permute-start.13 = (bf16[2,8,64,512]{3,2,1,0:T(8,128)(2,1)S(1)}, bf16[2,8,64,512]{3,2,1,0:T(8,128)(2,1)}, u32[]{:S(2)}, u32[]{:S(2)}) collective-permute-start(bf16[2,8,64,512]{3,2,1,0:T(8,128)(2,1)S(1)} %bitcast.146), channel_id=1, source_target_pairs={{0,8},{8,0},{1,9},{9,1},{2,10},{10,2},{3,11},{11,3},{4,12},{12,4},... | collective-permute-start | bytes 3145736 | tf_op jit(solution)/shard_map/ppermute | solution.py:21
  111.1 2.0 copy-start
  113.2 8.3 %collective-permute-start.16 = (f32[2,8,64,512]{3,2,1,0:T(8,128)S(1)}, f32[2,8,64,512]{3,2,1,0:T(8,128)}, u32[]{:S(2)}, u32[]{:S(2)}) collective-permute-start(f32[2,8,64,512]{3,2,1,0:T(8,128)S(1)} %dynamic-slice_bitcast_fusion), channel_id=1, source_target_pairs={{0,8},{8,0},{1,9},{9,1},{2,10},{10,2},{3,11},{11,3},{4,12},{12,4},... | collective-permute-start | bytes 6291464 | tf_op jit(solution)/shard_map/ppermute | solution.py:21
  116.8 4.7 %copy-start.1 = (f32[2,8,2,64,512]{4,3,2,1,0:T(8,128)S(1)}, f32[2,8,2,64,512]{4,3,2,1,0:T(8,128)}, u32[]{:S(2)}) copy-start(f32[2,8,2,64,512]{4,3,2,1,0:T(8,128)} %copy-done) | copy-start | bytes 12582916
  121.5 17.2 %copy-start.2 = (f32[1024,512]{1,0:T(8,128)}, f32[1024,512]{1,0:T(8,128)S(1)}, u32[]{:S(2)}) copy-start(f32[1024,512]{1,0:T(8,128)S(1)} %fusion.14) | copy-start | bytes 6291460
  121.5 22.2 %copy-start.6 = (f32[256]{0:T(256)S(1)}, f32[256]{0:T(256)}, u32[]{:S(2)}) copy-start(f32[256]{0:T(256)} %param.10) | copy-start | bytes 3076
  125.1 36.8 %collective-permute-start.23 = (bf16[2,64,512]{2,1,0:T(8,128)(2,1)S(1)}, bf16[2,64,512]{2,1,0:T(8,128)(2,1)}, u32[]{:S(2)}, u32[]{:S(2)}) collective-permute-start(bf16[2,64,512]{2,1,0:T(8,128)(2,1)S(1)} %get-tuple-element.17), channel_id=1, source_target_pairs={{0,64},{16,80},{32,96},{48,112},{64,0},{80,16},{96,32},{112,48},{1... | collective-permute-start | bytes 393224 | tf_op jit(solution)/shard_map/ppermute | solution.py:17
  131.0 34.3 %collective-permute-start.22 = (bf16[2,64,512]{2,1,0:T(8,128)(2,1)S(1)}, bf16[2,64,512]{2,1,0:T(8,128)(2,1)}, u32[]{:S(2)}, u32[]{:S(2)}) collective-permute-start(bf16[2,64,512]{2,1,0:T(8,128)(2,1)S(1)} %get-tuple-element.18), channel_id=1, source_target_pairs={{0,80},{16,96},{32,112},{48,0},{64,16},{80,32},{96,48},{112,64},{1... | collective-permute-start | bytes 393224 | tf_op jit(solution)/shard_map/ppermute | solution.py:17
  135.0 34.3 %collective-permute-start.21 = (bf16[2,64,512]{2,1,0:T(8,128)(2,1)S(1)}, bf16[2,64,512]{2,1,0:T(8,128)(2,1)S(1)}, u32[]{:S(2)}, u32[]{:S(2)}) collective-permute-start(bf16[2,64,512]{2,1,0:T(8,128)(2,1)S(1)} %get-tuple-element.19), channel_id=1, source_target_pairs={{0,48},{16,64},{32,80},{48,96},{64,112},{80,0},{96,16},{112,32},{1... | collective-permute-start | bytes 393224 | tf_op jit(solution)/shard_map/ppermute | solution.py:17
  138.8 78.6 %collective-permute-start.14 = (bf16[1024,256]{1,0:T(8,128)(2,1)S(1)}, bf16[1024,256]{1,0:T(8,128)(2,1)S(1)}, u32[]{:S(2)}, u32[]{:S(2)}) collective-permute-start(bf16[1024,256]{1,0:T(8,128)(2,1)S(1)} %dynamic-slice_convert_fusion), channel_id=1, source_target_pairs={{0,1},{1,0},{2,3},{3,2},{4,5},{5,4},{6,7},{7,6},{8,9},{9,8},{10,11... | collective-permute-start | bytes 1572872 | tf_op jit(solution)/shard_map/ppermute | solution.py:21
  143.7 14.4 %collective-permute-start.29 = (f32[256]{0:T(256)S(1)}, f32[256]{0:T(256)S(1)}, u32[]{:S(2)}, u32[]{:S(2)}) collective-permute-start(f32[256]{0:T(256)S(1)} %copy-done.6), channel_id=1, source_target_pairs={{0,1},{1,0},{2,3},{3,2},{4,5},{5,4},{6,7},{7,6},{8,9},{9,8},{10,11... | collective-permute-start | bytes 3080 | tf_op jit(solution)/shard_map/ppermute | solution.py:21
  158.1 14.0 %collective-permute-start.20 = (bf16[2,64,512]{2,1,0:T(8,128)(2,1)}, bf16[2,64,512]{2,1,0:T(8,128)(2,1)}, u32[]{:S(2)}, u32[]{:S(2)}) collective-permute-start(bf16[2,64,512]{2,1,0:T(8,128)(2,1)} %get-tuple-element.20), channel_id=1, source_target_pairs={{0,96},{16,112},{32,0},{48,16},{64,32},{80,48},{96,64},{112,80},{1... | collective-permute-start | bytes 393224 | tf_op jit(solution)/shard_map/ppermute | solution.py:17
  161.9 11.6 %collective-permute-start.19 = (bf16[2,64,512]{2,1,0:T(8,128)(2,1)S(1)}, bf16[2,64,512]{2,1,0:T(8,128)(2,1)}, u32[]{:S(2)}, u32[]{:S(2)}) collective-permute-start(bf16[2,64,512]{2,1,0:T(8,128)(2,1)S(1)} %get-tuple-element.21), channel_id=1, source_target_pairs={{0,32},{16,48},{32,64},{48,80},{64,96},{80,112},{96,0},{112,16},{1... | collective-permute-start | bytes 393224 | tf_op jit(solution)/shard_map/ppermute | solution.py:17
  165.3 8.1 %collective-permute-start.18 = (bf16[2,64,512]{2,1,0:T(8,128)(2,1)S(1)}, bf16[2,64,512]{2,1,0:T(8,128)(2,1)}, u32[]{:S(2)}, u32[]{:S(2)}) collective-permute-start(bf16[2,64,512]{2,1,0:T(8,128)(2,1)S(1)} %get-tuple-element.22), channel_id=1, source_target_pairs={{0,112},{16,0},{32,16},{48,32},{64,48},{80,64},{96,80},{112,96},{1... | collective-permute-start | bytes 393224 | tf_op jit(solution)/shard_map/ppermute | solution.py:17
  169.3 0.6 copy-start.4
  170.0 8.2 %collective-permute-start.17 = (bf16[2,64,512]{2,1,0:T(8,128)(2,1)S(1)}, bf16[2,64,512]{2,1,0:T(8,128)(2,1)}, u32[]{:S(2)}, u32[]{:S(2)}) collective-permute-start(bf16[2,64,512]{2,1,0:T(8,128)(2,1)S(1)} %get-tuple-element.16), channel_id=1, source_target_pairs={{0,16},{16,32},{32,48},{48,64},{64,80},{80,96},{96,112},{112,0},{1... | collective-permute-start | bytes 393224 | tf_op jit(solution)/shard_map/ppermute | solution.py:17
  172.2 60.0 %collective-permute-start.30 = (f32[64]{0:T(128)}, f32[64]{0:T(128)S(1)}, u32[]{:S(2)}, u32[]{:S(2)}) collective-permute-start(f32[64]{0:T(128)} %param.11), channel_id=1, source_target_pairs={{0,0},{1,256},{256,1},{257,257},{2,2},{3,258},{258,3},{259,259},{4... | collective-permute-start | bytes 776 | tf_op jit(solution)/shard_map/ppermute | solution.py:35
  179.6 40.0 %collective-permute-start.26 = (f32[32,512]{1,0:T(8,128)S(1)}, f32[32,512]{1,0:T(8,128)S(1)}, u32[]{:S(2)}, u32[]{:S(2)}) collective-permute-start(f32[32,512]{1,0:T(8,128)S(1)} %get-tuple-element.30), channel_id=1, source_target_pairs={{0,256},{128,384},{256,0},{384,128},{1,257},{129,385},{257,1},{385... | collective-permute-start | bytes 196616 | tf_op jit(solution)/shard_map/ppermute | solution.py:25
  211.5 8.0 %collective-permute-start.25 = (f32[32,512]{1,0:T(8,128)S(1)}, f32[32,512]{1,0:T(8,128)S(1)}, u32[]{:S(2)}, u32[]{:S(2)}) collective-permute-start(f32[32,512]{1,0:T(8,128)S(1)} %get-tuple-element.31), channel_id=1, source_target_pairs={{0,384},{128,0},{256,128},{384,256},{1,385},{129,1},{257,129},{385... | collective-permute-start | bytes 196616 | tf_op jit(solution)/shard_map/ppermute | solution.py:25
  214.6 8.0 %collective-permute-start.24 = (f32[32,512]{1,0:T(8,128)S(1)}, f32[32,512]{1,0:T(8,128)S(1)}, u32[]{:S(2)}, u32[]{:S(2)}) collective-permute-start(f32[32,512]{1,0:T(8,128)S(1)} %get-tuple-element.29), channel_id=1, source_target_pairs={{0,128},{128,256},{256,384},{384,0},{1,129},{129,257},{257,385},{3... | collective-permute-start | bytes 196616 | tf_op jit(solution)/shard_map/ppermute | solution.py:25
  272.4 23.9 %collective-permute-start.27 = (f32[32,256]{1,0:T(8,128)S(1)}, f32[32,256]{1,0:T(8,128)S(1)}, u32[]{:S(2)}, u32[]{:S(2)}) collective-permute-start(f32[32,256]{1,0:T(8,128)S(1)} %bitcast.156), channel_id=1, source_target_pairs={{0,0},{1,256},{256,1},{257,257},{2,2},{3,258},{258,3},{259,259},{4... | collective-permute-start | bytes 98312 | tf_op jit(solution)/shard_map/ppermute | solution.py:35
  273.1 23.2 %collective-permute-start.28 = (f32[32,256]{1,0:T(8,128)S(1)}, f32[32,256]{1,0:T(8,128)S(1)}, u32[]{:S(2)}, u32[]{:S(2)}) collective-permute-start(f32[32,256]{1,0:T(8,128)S(1)} %bitcast.157), channel_id=1, source_target_pairs={{0,1},{1,257},{256,0},{257,256},{2,3},{3,259},{258,2},{259,258},{4... | collective-permute-start | bytes 98312 | tf_op jit(solution)/shard_map/ppermute | solution.py:35
  283.9 13.1 %copy-start.5 = (f32[1,256]{1,0:T(1,128)}, f32[1,256]{1,0:T(1,128)S(1)}, u32[]{:S(2)}) copy-start(f32[1,256]{1,0:T(1,128)S(1)} %constant_dynamic-slice_fusion.1) | copy-start | bytes 3076
  296.3 0.8 copy-start.7

commit v3 on v2

v3 whole, which is shorter than its diff:
```python
import jax
import jax.numpy as jnp
from jax import lax
from jax.experimental import pallas as pl
from jax.experimental.pallas import tpu as pltpu
from jax.sharding import Mesh, PartitionSpec as P


decay_rate = 0.9
square_eps = 1e-30

SPLIT = (("zb", 2), ("za", 2), ("y", 8), ("c", 2), ("x", 4), ("zh", 2))
SIZE = dict(SPLIT)
DP = ("zb", "za", "y", "c")
MP = ("x", "zh")
X_STEPS = (1, 3, 2)
Y_STEPS = (4, 3, 5, 2, 6, 1, 7)
Z_STEPS = (2, 1, 3)


def shift(value, axes, step):
    size = 4 if axes == ("zb", "za") else SIZE[axes]
    return lax.ppermute(value, axes, [(i, (i + step) % size) for i in range(size)])


def flip(value, axis, mask=1):
    return lax.ppermute(value, axis, [(i, i ^ mask) for i in range(SIZE[axis])])


def turn(value, to):
    pairs = []
    for a in range(2):
        for b in range(2):
            p, q = to(a, b)
            pairs.append((2 * a + b, 2 * p + q))
    return lax.ppermute(value, ("zb", "zh"), pairs)


def rotate(value, back):
    pairs = []
    for a in range(2):
        for b in range(2):
            for d in range(2):
                p, q, r = (b, d, a) if back else (d, a, b)
                pairs.append((4 * a + 2 * b + d, 4 * p + 2 * q + r))
    return lax.ppermute(value, ("zb", "c", "zh"), pairs)


def pick(value, index, axis=0):
    return lax.dynamic_index_in_dim(value, index, axis, keepdims=False)


def slot(value, index, count):
    here = lax.broadcasted_iota(jnp.int32, (count, 1), 0) == index
    return jnp.where(here, value[None], jnp.zeros((), value.dtype)).reshape(-1)


def arrange_kernel(info_ref, own_ref, other_ref, out_ref):
    count, tokens, heads = own_ref.shape
    own_at = pl.multiple_of(info_ref[count] * heads, heads)
    other_at = pl.multiple_of((1 - info_ref[count]) * heads, heads)
    for i in range(count):
        at = info_ref[i]
        span = slice(i * tokens, (i + 1) * tokens)
        out_ref[pl.ds(own_at, heads), span] = own_ref[at].T
        out_ref[pl.ds(other_at, heads), span] = other_ref[at].T


def grad_kernel(ctx_ref, *refs):
    blocks, (keep_ref, send_ref) = refs[:-2], refs[-2:]
    tile = jnp.concatenate([ref[...] for ref in blocks], axis=0)
    got = jnp.dot(ctx_ref[...], tile, preferred_element_type=jnp.float32)
    rows = keep_ref.shape[2]
    for k in range(2):
        span = slice(k * 128, (k + 1) * 128)
        send_ref[k, 0] = got[:rows, span].astype(send_ref.dtype)
        keep_ref[k, 0] = got[rows:, span]


def back_kernel(info_ref, a0_ref, a1_ref, b0_ref, b1_ref, *refs):
    blocks, (own_ref, other_ref, acc_ref) = refs[:-3], refs[-3:]
    count, tokens, heads = own_ref.shape
    step = pl.program_id(0)
    first = info_ref[count + 3] == 0
    rows = []
    for a_ref, b_ref in ((a0_ref, b0_ref), (a1_ref, b1_ref)):
        mine, came = a_ref[0], b_ref[0]
        rows += [jnp.where(first, mine, came), jnp.where(first, came, mine)]
    tile = jnp.concatenate([ref[...] for ref in blocks], axis=0)
    got = jnp.dot(tile, jnp.concatenate(rows, axis=0), preferred_element_type=jnp.float32)

    @pl.when(step == 0)
    def _():
        acc_ref[...] = got

    @pl.when(step > 0)
    def _():
        acc_ref[...] += got

    @pl.when(step == pl.num_programs(0) - 1)
    def _():
        straight = info_ref[count + 4] == 0
        for i in range(count):
            at = info_ref[i]
            left = acc_ref[i * tokens : (i + 1) * tokens, :heads]
            right = acc_ref[i * tokens : (i + 1) * tokens, heads:]
            own_ref[at] = jnp.where(straight, left, right)
            other_ref[at] = jnp.where(straight, right, left).astype(other_ref.dtype)


def total_kernel(mine_ref, *refs):
    came, out_ref = refs[:-1], refs[-1]
    cols = out_ref.shape[1]
    for za in range(2):
        total = mine_ref[za]
        for ref in came:
            total = total + ref[za].astype(jnp.float32)
        turned = total.T
        for zb in range(2):
            out_ref[2 * zb + za] = turned[zb * cols : (zb + 1) * cols]


def arrange(info, own, other):
    count, tokens, heads = own.shape
    full = pl.BlockSpec(own.shape, lambda i, p: (0, 0, 0))
    return pl.pallas_call(
        arrange_kernel,
        grid_spec=pltpu.PrefetchScalarGridSpec(
            num_scalar_prefetch=1,
            grid=(1,),
            in_specs=[full, full],
            out_specs=pl.BlockSpec((2 * heads, count * tokens), lambda i, p: (0, 0)),
        ),
        out_shape=jax.ShapeDtypeStruct((2 * heads, count * tokens), own.dtype),
        name="arrange",
    )(info, own, other)


def grad_of(ctx, blocks):
    twice, rows_in = ctx.shape
    tokens, half = blocks[0].shape
    tile = 256
    per_za = half // SIZE["za"] // tile
    shape = (SIZE["y"], SIZE["za"], twice // 2, 128)
    out = pl.BlockSpec((2, 1) + shape[2:], lambda t: (t % per_za, t // per_za, 0, 0))
    return pl.pallas_call(
        grad_kernel,
        grid=(half // tile,),
        in_specs=[pl.BlockSpec(ctx.shape, lambda t: (0, 0))]
        + [pl.BlockSpec((tokens, tile), lambda t: (0, t))] * len(blocks),
        out_specs=[out, out],
        out_shape=[
            jax.ShapeDtypeStruct(shape, jnp.float32),
            jax.ShapeDtypeStruct(shape, jnp.bfloat16),
        ],
        cost_estimate=pl.CostEstimate(
            flops=2 * twice * rows_in * half, transcendentals=0, bytes_accessed=9 << 20
        ),
        name="grad",
    )(ctx, *blocks)


def back_of(info, mine, came, blocks):
    _, cols, twice = mine.shape
    tokens, half = blocks[0].shape
    count = len(blocks)
    tile = 4 * cols
    per_za = half // SIZE["za"] // tile
    shape = (count, tokens, twice // 2)
    full = pl.BlockSpec(shape, lambda k, p: (0, 0, 0))

    def weights(low):
        def index(k, p):
            z = (k // per_za) ^ p[count + 1]
            y = ((k % per_za) * 2 + low) ^ p[count + 2]
            return ((y & 1) * 8 + ((y >> 1) & 1) * 4 + ((y >> 2) & 1) * 2 + z, 0, 0)

        return pl.BlockSpec((1, cols, twice), index)

    return pl.pallas_call(
        back_kernel,
        grid_spec=pltpu.PrefetchScalarGridSpec(
            num_scalar_prefetch=1,
            grid=(half // tile,),
            in_specs=[weights(0), weights(1), weights(0), weights(1)]
            + [pl.BlockSpec((tokens, tile), lambda k, p: (0, k))] * count,
            out_specs=[full, full],
            scratch_shapes=[pltpu.VMEM((count * tokens, twice), jnp.float32)],
        ),
        out_shape=[
            jax.ShapeDtypeStruct(shape, jnp.float32),
            jax.ShapeDtypeStruct(shape, jnp.bfloat16),
        ],
        cost_estimate=pl.CostEstimate(
            flops=2 * twice * count * tokens * half, transcendentals=0, bytes_accessed=8 << 20
        ),
        name="back",
    )(info, mine, mine, came, came, *blocks)


def total_of(mine, came, cols):
    return pl.pallas_call(
        total_kernel,
        out_shape=jax.ShapeDtypeStruct((4, cols, mine.shape[1]), jnp.float32),
        name="total",
    )(mine, *came)


def per_device(context, cotangent, lengths, weight, row_stat, col_stat):
    groups = SIZE["zb"] * SIZE["za"] * SIZE["y"] * SIZE["c"]
    zb, za, y, c, x, zh = (lax.axis_index(name) for name, _ in SPLIT)
    seq_here = lengths.shape[0]
    tokens, width = cotangent.shape
    target_len = tokens // seq_here
    heads = context.shape[1]
    half = width // 2
    cols = width // groups
    position = jnp.arange(target_len, dtype=jnp.int32)
    inside = position[None, :] < lengths[:, None]
    shaped = cotangent.reshape(seq_here, target_len, width)
    masked = jnp.where(inside[:, :, None], shaped, jnp.zeros((), cotangent.dtype)).reshape(
        tokens, width
    )

    left, right = masked[:, :half], masked[:, half:]
    theirs = flip(jnp.where(zh == 0, right, left), "zh")
    mine = jnp.where(zh == 0, left, right)
    blocks = [mine] + [shift(mine, "x", s) for s in X_STEPS]
    blocks += [theirs] + [shift(theirs, "x", s) for s in X_STEPS]
    info = [((x - s) & (SIZE["x"] - 1)) * 2 + z for z in (zh, 1 - zh) for s in (0,) + X_STEPS]
    info = jnp.stack(info + [1 - (c ^ zh), za, y, c, zb ^ zh]).astype(jnp.int32)
    context_other = flip(context, "zh")
    by_block = (len(blocks), tokens, heads)
    ctx = arrange(info, context.reshape(by_block), context_other.reshape(by_block))

    slim = weight.T.astype(jnp.bfloat16)
    w_a = turn(slim, lambda a, b: (b, a))
    w_b = turn(slim, lambda a, b: (1 - b, a))
    w = jnp.concatenate([w_a, w_b], axis=1)[None]
    w = jnp.concatenate([w, flip(w, "za")], axis=0)
    for bit in (2, 1, 0):
        w = jnp.concatenate([w, flip(w, "y", 1 << bit)], axis=0)
    w_came = flip(w, "c")

    stats = rotate(jnp.concatenate([row_stat, col_stat]), True)
    row_held, col_held = stats[:heads], stats[heads:]

    kept, sent = grad_of(ctx, blocks)
    parts = kept + flip(sent, "c").astype(jnp.float32)

    own, other = back_of(info, w, w_came, blocks)
    context_grad = (own + flip(other, "zh").astype(jnp.float32)).astype(jnp.bfloat16)
    context_grad = context_grad.reshape(context.shape)

    narrow = parts.astype(jnp.bfloat16)
    last = SIZE["y"] - 1
    came = [shift(pick(narrow, (y + s) & last), "y", s) for s in Y_STEPS]
    pieces = total_of(pick(parts, y), came, cols)
    zl = zb * 2 + za
    part = pick(pieces, zl)
    for s in Z_STEPS:
        part = part + shift(pick(pieces, (zl + s) & 3), ("zb", "za"), s)
    grad = part / groups
    grad_own = rotate(grad, False)

    square = grad * grad + square_eps
    inner_total = heads * SIZE["x"] * SIZE["zh"]
    col_all = lax.psum(jnp.sum(square, axis=1), "c")
    col_all = lax.psum(col_all, "x")
    col_here = decay_rate * col_held + (1.0 - decay_rate) * (col_all / inner_total)
    scaled = grad * grad / col_here[:, None]
    rows = jnp.concatenate([jnp.sum(square, axis=0), jnp.sum(scaled, axis=0)])
    rows = lax.psum(rows, "y")
    rows = lax.psum(jnp.concatenate([rows, slot(col_here, zl, 4)]), ("zb", "za"))
    slots = slot(rows[2 * heads :], zh, 2)
    rows = lax.psum(jnp.concatenate([rows[: 2 * heads], slots]), "zh")
    slots = rows[2 * heads :].reshape(8, cols)
    col_new = pick(slots, zb * 4 + c * 2 + za)
    row_here = decay_rate * row_held + (1.0 - decay_rate) * (rows[:heads] / width)
    square_sum = jnp.sum(rows[heads : 2 * heads] / row_here)
    tail = jnp.broadcast_to(square_sum, (128,))
    sums = lax.psum(jnp.concatenate([slot(row_here, c, 2), tail]), "c")
    row_new = pick(sums[: 2 * heads].reshape(2, heads), zh)
    square_sum = lax.psum(sums[2 * heads], "x")
    raw_update = grad_own / jnp.sqrt(row_new[None, :] * col_new[:, None])
    update_rms = jnp.sqrt(square_sum / (inner_total * width))
    update = (raw_update / jnp.maximum(1.0, update_rms)).T
    return (context_grad, update, row_new, col_new)


def solution(mesh):
    names = tuple(name for name, _ in SPLIT)
    fine = Mesh(mesh.devices.reshape(tuple(size for _, size in SPLIT)), names)
    in_specs = (P(DP, MP), P(DP + MP, None), P(DP + MP), P(MP, DP), P(MP), P(DP))
    out_specs = (P(DP, MP), P(MP, DP), P(MP), P(DP))
    return jax.shard_map(
        per_device, mesh=fine, in_specs=in_specs, out_specs=out_specs, check_vma=False
    )
```

time: 299 us -> 298 us (level)
  the two profiles are of different devices: /device:TPU:2 before, /device:TPU:1 now
where the time goes in v3:
time: 298 us; the launch traced here: 295 us
  starting transfers between devices  147 us (49%)
  blocking collectives  60.4 us (20%)
  waiting for transfers between devices  44.2 us (15%)
  Pallas kernels  23.8 us (8%)
  other arithmetic  9.37 us (3%)
  local copies, waits for them, and re-layouts  7.87 us (3%)
    ppermute x9, starting transfers between devices, flip(): return lax.ppermute(value, axis, [(i, i ^ mask) for i in range(SIZE[axis])])  66 us
    ppermute x16, starting transfers between devices, shift(): lax.ppermute(value, axes, [(i, (i + step) % size) for i in range(size)])  61.9 us
    ppermute x2, waiting for transfers between devices, turn(): return lax.ppermute(value, ('zb', 'zh'), pairs)  16.1 us
    ppermute x9, waiting for transfers between devices, flip(): return lax.ppermute(value, axis, [(i, i ^ mask) for i in range(SIZE[axis])])  14.6 us
    ppermute x2, starting transfers between devices, rotate(): return lax.ppermute(value, ('zb', 'c', 'zh'), pairs)  14.5 us
    psum x1, blocking collectives, per_device(): col_all = lax.psum(col_all, 'x')  13.5 us
    ppermute x16, waiting for transfers between devices, shift(): lax.ppermute(value, axes, [(i, (i + step) % size) for i in range(size)])  13.5 us
    psum x1, blocking collectives, per_device(): rows = lax.psum(rows, 'y')  10.7 us
  transfers between devices with their start and end apart: 29, of which 6 were waited for; matrix products, arithmetic and copies ran while one was open for 3% of the time, Pallas kernels for 8%

profile of v3, /device:TPU:1, one launch (start us, length us, event | category | flops | bytes accessed | tf_op | source)
XLA Modules:
  0.0 294.9 jit_solution(18219745760229377081)
XLA Ops:
  0.6 0.7 iota_compare_fusion
  1.5 1.4 broadcast_select_fusion
  3.0 3.9 %collective-permute-start.7 = (bf16[128,2048]{1,0:T(8,128)(2,1)S(1)}, bf16[128,2048]{1,0:T(8,128)(2,1)S(1)}, u32[]{:S(2)}, u32[]{:S(2)}) collective-permute-start(bf16[128,2048]{1,0:T(8,128)(2,1)S(1)} %get-tuple-element.28.refs_0_), channel_id=1, source_target_pairs={{0,2},{2,4},{4,6},{6,0},{1,3},{3,5},{5,7},{7,1},{8,10},{10,12},{12... | collective-permute-start | bytes 1572872 | tf_op jit(solution)/shard_map/ppermute | solution.py:23
  6.9 10.6 %collective-permute-start.10 = (bf16[128,2048]{1,0:T(8,128)(2,1)S(1)}, bf16[128,2048]{1,0:T(8,128)(2,1)S(1)}, u32[]{:S(2)}, u32[]{:S(2)}) collective-permute-start(bf16[128,2048]{1,0:T(8,128)(2,1)S(1)} %get-tuple-element.27), channel_id=1, source_target_pairs={{0,1},{1,0},{2,3},{3,2},{4,5},{5,4},{6,7},{7,6},{8,9},{9,8},{10,11... | collective-permute-start | bytes 1572872 | tf_op jit(solution)/shard_map/ppermute | solution.py:27
  17.6 1.9 collective-permute-start.15
  19.5 4.0 %collective-permute-start.1 = (bf16[64,256]{1,0:T(8,128)(2,1)S(1)}, bf16[64,256]{1,0:T(8,128)(2,1)S(1)}, u32[]{:S(2)}, u32[]{:S(2)}) collective-permute-start(bf16[64,256]{1,0:T(8,128)(2,1)S(1)} %convert_bitcast_fusion), channel_id=1, source_target_pairs={{0,256},{1,0},{256,257},{257,1},{2,258},{3,2},{258,259},{259,3},{4... | collective-permute-start | bytes 98312 | tf_op jit(solution)/shard_map/ppermute | solution.py:36
  23.6 0.7 collective-permute-start
  24.2 16.1 %collective-permute-done.1 = bf16[64,256]{1,0:T(8,128)(2,1)S(1)} collective-permute-done((bf16[64,256]{1,0:T(8,128)(2,1)S(1)}, bf16[64,256]{1,0:T(8,128)(2,1)S(1)}, u32[]{:S(2)}, u32[]{:S(2)}) %collective-permute-start.1) | collective-permute-done | bytes 32800 | tf_op jit(solution)/shard_map/ppermute | solution.py:36
  40.3 26.9 %collective-permute-start.2 = (bf16[1,64,512]{2,1,0:T(8,128)(2,1)S(1)}, bf16[1,64,512]{2,1,0:T(8,128)(2,1)S(1)}, u32[]{:S(2)}, u32[]{:S(2)}) collective-permute-start(bf16[1,64,512]{2,1,0:T(8,128)(2,1)S(1)} %maximum_bitcast_fusion), channel_id=1, source_target_pairs={{0,128},{128,0},{1,129},{129,1},{2,130},{130,2},{3,131},{131,3},{4... | collective-permute-start | bytes 196616 | tf_op jit(solution)/shard_map/ppermute | solution.py:27
  67.3 1.6 collective-permute-done.2
  68.9 7.5 %collective-permute-start.3 = (bf16[2,64,512]{2,1,0:T(8,128)(2,1)S(1)}, bf16[2,64,512]{2,1,0:T(8,128)(2,1)S(1)}, u32[]{:S(2)}, u32[]{:S(2)}) collective-permute-start(bf16[2,64,512]{2,1,0:T(8,128)(2,1)S(1)} %pad_maximum_fusion.2), channel_id=1, source_target_pairs={{0,64},{16,80},{32,96},{48,112},{64,0},{80,16},{96,32},{112,48},{1... | collective-permute-start | bytes 393224 | tf_op jit(solution)/shard_map/ppermute | solution.py:27
  76.4 3.4 %collective-permute-start.8 = (bf16[128,2048]{1,0:T(8,128)(2,1)S(1)}, bf16[128,2048]{1,0:T(8,128)(2,1)S(1)}, u32[]{:S(2)}, u32[]{:S(2)}) collective-permute-start(bf16[128,2048]{1,0:T(8,128)(2,1)S(1)} %get-tuple-element.28.refs_0_), channel_id=1, source_target_pairs={{0,6},{2,0},{4,2},{6,4},{1,7},{3,1},{5,3},{7,5},{8,14},{10,8},{12,... | collective-permute-start | bytes 1572872 | tf_op jit(solution)/shard_map/ppermute | solution.py:23
  79.8 3.4 %collective-permute-start.9 = (bf16[128,2048]{1,0:T(8,128)(2,1)S(1)}, bf16[128,2048]{1,0:T(8,128)(2,1)}, u32[]{:S(2)}, u32[]{:S(2)}) collective-permute-start(bf16[128,2048]{1,0:T(8,128)(2,1)S(1)} %get-tuple-element.28.refs_0_), channel_id=1, source_target_pairs={{0,4},{2,6},{4,0},{6,2},{1,5},{3,7},{5,1},{7,3},{8,12},{10,14},{12... | collective-permute-start | bytes 1572872 | tf_op jit(solution)/shard_map/ppermute | solution.py:23
  83.2 2.2 collective-permute-start.11
  85.5 4.3 %collective-permute-start.12 = (bf16[128,2048]{1,0:T(8,128)(2,1)S(1)}, bf16[128,2048]{1,0:T(8,128)(2,1)}, u32[]{:S(2)}, u32[]{:S(2)}) collective-permute-start(bf16[128,2048]{1,0:T(8,128)(2,1)S(1)} %collective-permute-done.10.refs_4_), channel_id=1, source_target_pairs={{0,6},{2,0},{4,2},{6,4},{1,7},{3,1},{5,3},{7,5},{8,14},{10,8},{12,... | collective-permute-start | bytes 1572872 | tf_op jit(solution)/shard_map/ppermute | solution.py:23
  89.8 0.8 copy-done.8
  90.6 2.1 collective-permute-start.13
  92.7 0.6 stack.55.info_ref
  93.4 3.2 %arrange.1.ctx_ref = bf16[512,1024]{1,0:T(8,128)(2,1)} custom-call(s32[13]{0:T(128)} %stack.55.info_ref, bf16[8,128,256]{2,1,0:T(8,128)(2,1)} %bitcast.65, bf16[8,128,256]{2,1,0:T(8,128)(2,1)} %bitcast.66), custom_call_target="tpu_custom_call" | custom-call | tf_op jit(solution)/shard_map/arrange/pallas_call | solution.py:126
  96.6 5.1 %collective-permute-start.4 = (bf16[4,64,512]{2,1,0:T(8,128)(2,1)S(1)}, bf16[4,64,512]{2,1,0:T(8,128)(2,1)S(1)}, u32[]{:S(2)}, u32[]{:S(2)}) collective-permute-start(bf16[4,64,512]{2,1,0:T(8,128)(2,1)S(1)} %pad_maximum_fusion.1), channel_id=1, source_target_pairs={{0,32},{16,48},{32,0},{48,16},{64,96},{80,112},{96,64},{112,80},{1... | collective-permute-start | bytes 786440 | tf_op jit(solution)/shard_map/ppermute | solution.py:27
  101.7 8.9 %collective-permute-done.11.refs_5_ = bf16[128,2048]{1,0:T(8,128)(2,1)} collective-permute-done((bf16[128,2048]{1,0:T(8,128)(2,1)S(1)}, bf16[128,2048]{1,0:T(8,128)(2,1)}, u32[]{:S(2)}, u32[]{:S(2)}) %collective-permute-start.11) | collective-permute-done | bytes 524320 | tf_op jit(solution)/shard_map/ppermute | solution.py:23
  110.7 1.5 collective-permute-done.12.refs_6_
  112.2 3.0 %collective-permute-done.13.refs_7_ = bf16[128,2048]{1,0:T(8,128)(2,1)} collective-permute-done((bf16[128,2048]{1,0:T(8,128)(2,1)S(1)}, bf16[128,2048]{1,0:T(8,128)(2,1)}, u32[]{:S(2)}, u32[]{:S(2)}) %collective-permute-start.13) | collective-permute-done | bytes 524320 | tf_op jit(solution)/shard_map/ppermute | solution.py:23
  115.2 8.4 %grad.1 = (f32[8,2,256,128]{3,2,1,0:T(8,128)}, bf16[8,2,256,128]{3,2,1,0:T(8,128)(2,1)}) custom-call(bf16[512,1024]{1,0:T(8,128)(2,1)} %arrange.1.ctx_ref, bf16[128,2048]{1,0:T(8,128)(2,1)} %copy-done.3, bf16[128,2048]{1,0:T(8,128)(2,1)} %copy-done.5, bf16[128,2048]{1,0:T(8,128)(2,1)} %copy-done.7, bf16[128,2048]{1,0:T(8,128)(2,1)} %collective-permute-done.9.refs_3_, ...), custom_call_target="tpu_custom_call" | custom-call | flops 2147483648 | bytes 9437184 | tf_op jit(solution)/shard_map/grad/pallas_call | solution.py:146
  123.6 6.8 %collective-permute-start.16 = (bf16[8,2,256,128]{3,2,1,0:T(8,128)(2,1)}, bf16[8,2,256,128]{3,2,1,0:T(8,128)(2,1)S(1)}, u32[]{:S(2)}, u32[]{:S(2)}) collective-permute-start(bf16[8,2,256,128]{3,2,1,0:T(8,128)(2,1)} %get-tuple-element.11), channel_id=1, source_target_pairs={{0,8},{8,0},{1,9},{9,1},{2,10},{10,2},{3,11},{11,3},{4,12},{12,4},... | collective-permute-start | bytes 3145736 | tf_op jit(solution)/shard_map/ppermute | solution.py:27
  130.5 2.4 collective-permute-start.5
  133.0 13.0 %collective-permute-done.5 = bf16[8,64,512]{2,1,0:T(8,128)(2,1)S(1)} collective-permute-done((bf16[8,64,512]{2,1,0:T(8,128)(2,1)S(1)}, bf16[8,64,512]{2,1,0:T(8,128)(2,1)S(1)}, u32[]{:S(2)}, u32[]{:S(2)}) %collective-permute-start.5) | collective-permute-done | bytes 524320 | tf_op jit(solution)/shard_map/ppermute | solution.py:27
  146.0 2.8 collective-permute-start.6
  148.9 1.7 fusion.6
  150.7 7.7 %collective-permute-start.17 = (bf16[2,256,128]{2,1,0:T(8,128)(2,1)S(1)}, bf16[2,256,128]{2,1,0:T(8,128)(2,1)S(1)}, u32[]{:S(2)}, u32[]{:S(2)}) collective-permute-start(bf16[2,256,128]{2,1,0:T(8,128)(2,1)S(1)} %get-tuple-element.26), channel_id=1, source_target_pairs={{0,64},{16,80},{32,96},{48,112},{64,0},{80,16},{96,32},{112,48},{1... | collective-permute-start | bytes 393224 | tf_op jit(solution)/shard_map/ppermute | solution.py:23
  158.4 2.5 collective-permute-start.18
  160.8 5.8 %collective-permute-start.19 = (bf16[2,256,128]{2,1,0:T(8,128)(2,1)S(1)}, bf16[2,256,128]{2,1,0:T(8,128)(2,1)S(1)}, u32[]{:S(2)}, u32[]{:S(2)}) collective-permute-start(bf16[2,256,128]{2,1,0:T(8,128)(2,1)S(1)} %get-tuple-element.24), channel_id=1, source_target_pairs={{0,80},{16,96},{32,112},{48,0},{64,16},{80,32},{96,48},{112,64},{1... | collective-permute-start | bytes 393224 | tf_op jit(solution)/shard_map/ppermute | solution.py:23
  166.7 1.9 collective-permute-start.20
  168.7 5.5 %collective-permute-start.21 = (bf16[2,256,128]{2,1,0:T(8,128)(2,1)S(1)}, bf16[2,256,128]{2,1,0:T(8,128)(2,1)S(1)}, u32[]{:S(2)}, u32[]{:S(2)}) collective-permute-start(bf16[2,256,128]{2,1,0:T(8,128)(2,1)S(1)} %get-tuple-element.22), channel_id=1, source_target_pairs={{0,96},{16,112},{32,0},{48,16},{64,32},{80,48},{96,64},{112,80},{1... | collective-permute-start | bytes 393224 | tf_op jit(solution)/shard_map/ppermute | solution.py:23
  174.2 2.3 collective-permute-start.22
  176.5 4.6 %collective-permute-start.23 = (bf16[2,256,128]{2,1,0:T(8,128)(2,1)S(1)}, bf16[2,256,128]{2,1,0:T(8,128)(2,1)S(1)}, u32[]{:S(2)}, u32[]{:S(2)}) collective-permute-start(bf16[2,256,128]{2,1,0:T(8,128)(2,1)S(1)} %get-tuple-element.20), channel_id=1, source_target_pairs={{0,112},{16,0},{32,16},{48,32},{64,48},{80,64},{96,80},{112,96},{1... | collective-permute-start | bytes 393224 | tf_op jit(solution)/shard_map/ppermute | solution.py:23
  181.0 0.5 iota_compare_fusion.2
  181.6 1.7 dynamic-slice_bitcast_fusion.mine_ref
  183.2 6.7 %collective-permute-start.28 = (f32[320]{0:T(512)S(1)}, f32[320]{0:T(512)S(1)}, u32[]{:S(2)}, u32[]{:S(2)}) collective-permute-start(f32[320]{0:T(512)S(1)} %pad_maximum_fusion.5), channel_id=1, source_target_pairs={{0,0},{1,8},{8,256},{9,264},{256,1},{257,9},{264,257},{265,265},{2... | collective-permute-start | bytes 3848 | tf_op jit(solution)/shard_map/ppermute | solution.py:46
  190.0 0.6 copy-done.13
  190.6 0.6 copy-done.15
  191.3 2.2 total.1
  193.4 0.9 dynamic-slice_bitcast_fusion.10
  194.4 6.7 %collective-permute-start.26 = (f32[64,256]{1,0:T(8,128)S(1)}, f32[64,256]{1,0:T(8,128)S(1)}, u32[]{:S(2)}, u32[]{:S(2)}) collective-permute-start(f32[64,256]{1,0:T(8,128)S(1)} %get-tuple-element.30), channel_id=1, source_target_pairs={{0,384},{128,0},{256,128},{384,256},{1,385},{129,1},{257,129},{385... | collective-permute-start | bytes 196616 | tf_op jit(solution)/shard_map/ppermute | solution.py:23
  201.1 1.9 collective-permute-start.25
  203.0 3.7 %collective-permute-start.24 = (f32[64,256]{1,0:T(8,128)S(1)}, f32[64,256]{1,0:T(8,128)S(1)}, u32[]{:S(2)}, u32[]{:S(2)}) collective-permute-start(f32[64,256]{1,0:T(8,128)S(1)} %get-tuple-element.29), channel_id=1, source_target_pairs={{0,256},{128,384},{256,0},{384,128},{1,257},{129,385},{257,1},{385... | collective-permute-start | bytes 196616 | tf_op jit(solution)/shard_map/ppermute | solution.py:23
  206.7 0.9 copy-done.1
  207.7 10.1 %back.1 = (f32[8,128,256]{2,1,0:T(8,128)}, bf16[8,128,256]{2,1,0:T(8,128)(2,1)}) custom-call(s32[13]{0:T(128)} %stack.55.info_ref, bf16[16,64,512]{2,1,0:T(8,128)(2,1)} %copy-done, bf16[16,64,512]{2,1,0:T(8,128)(2,1)} %copy-done, bf16[16,64,512]{2,1,0:T(8,128)(2,1)} %copy-done.1, bf16[16,64,512]{2,1,0:T(8,128)(2,1)} %copy-done.1, ...), custom_call_target="tpu_custom_call" | custom-call | flops 2147483648 | bytes 8388608 | tf_op jit(solution)/shard_map/back/pallas_call | solution.py:180
  217.7 1.9 collective-permute-start.14
  219.7 1.0 add_reduce_fusion
  220.7 7.8 %collective-permute-start.27 = (f32[64,256]{1,0:T(8,128)S(1)}, f32[64,256]{1,0:T(8,128)S(1)}, u32[]{:S(2)}, u32[]{:S(2)}) collective-permute-start(f32[64,256]{1,0:T(8,128)S(1)} %get-tuple-element.17), channel_id=1, source_target_pairs={{0,0},{1,256},{8,1},{9,257},{256,8},{257,264},{264,9},{265,265},{2... | collective-permute-start | bytes 196616 | tf_op jit(solution)/shard_map/ppermute | solution.py:46
  228.5 2.5 psum.49
  231.0 13.5 %psum.50 = f32[64]{0:T(128)S(1)} all-reduce(f32[64]{0:T(128)S(1)} %psum.49), channel_id=1, replica_groups=mesh['zb'=2,'za'=2,'y'=8,'c'=2,'x'=4,'zh'=2] {'x'}, use_global_device_ids=true, to_apply=%region_3.4 | all-reduce | flops 64 | bytes 512 | tf_op jit(solution)/shard_map/psum | solution.py:269
  244.6 0.1 add_reduce_fusion.1
  244.8 10.7 %psum.51 = f32[512]{0:T(512)S(1)} all-reduce(f32[512]{0:T(512)S(1)} %pad_maximum_fusion.6), channel_id=1, replica_groups=mesh['zb'=2,'za'=2,'y'=8,'c'=2,'x'=4,'zh'=2] {'y'}, use_global_device_ids=true, to_apply=%region_5.6 | all-reduce | flops 512 | bytes 4096 | tf_op jit(solution)/shard_map/psum | solution.py:273
  255.5 9.0 %psum.52 = f32[768]{0:T(1024)S(1)} all-reduce(f32[768]{0:T(1024)S(1)} %pad_maximum_fusion.3), channel_id=1, replica_groups=mesh['zb'=2,'za'=2,'y'=8,'c'=2,'x'=4,'zh'=2] {'zb','za'}, use_global_device_ids=true, to_apply=%region_6.7 | all-reduce | flops 768 | bytes 6144 | tf_op jit(solution)/shard_map/psum | solution.py:274
  264.6 7.7 %psum.53 = f32[1024]{0:T(1024)S(1)} all-reduce(f32[1024]{0:T(1024)S(1)} %pad_maximum_fusion.4), channel_id=1, replica_groups=mesh['zb'=2,'za'=2,'y'=8,'c'=2,'x'=4,'zh'=2] {'zh'}, use_global_device_ids=true, to_apply=%region_7.8 | all-reduce | flops 1024 | bytes 8192 | tf_op jit(solution)/shard_map/psum | solution.py:276
  272.3 0.6 fusion.3
  273.0 0.6 concatenate.42
  273.6 10.4 %psum.54 = f32[640]{0:T(1024)S(1)} all-reduce(f32[640]{0:T(1024)S(1)} %concatenate.42), channel_id=1, replica_groups=mesh['zb'=2,'za'=2,'y'=8,'c'=2,'x'=4,'zh'=2] {'c'}, use_global_device_ids=true, to_apply=%region_9.10 | all-reduce | flops 640 | bytes 5120 | tf_op jit(solution)/shard_map/psum | solution.py:282
  284.0 0.5 slice.51
  284.5 6.7 %psum.55 = f32[]{:T(128)} all-reduce(f32[]{:T(128)} %bitcast.32), channel_id=1, replica_groups=mesh['zb'=2,'za'=2,'y'=8,'c'=2,'x'=4,'zh'=2] {'x'}, use_global_device_ids=true, to_apply=%region_10.11 | all-reduce | flops 1 | bytes 8 | tf_op jit(solution)/shard_map/psum | solution.py:284
  292.1 0.7 divide_bitcast_fusion
  292.8 2.1 add_convert_fusion
  (97 shorter events, 1.1 us)
Async XLA Ops:
  1.5 16.1 %copy-start.4 = (bf16[1024,256]{1,0:T(8,128)(2,1)S(1)}, bf16[1024,256]{1,0:T(8,128)(2,1)}, u32[]{:S(2)}) copy-start(bf16[1024,256]{1,0:T(8,128)(2,1)} %param.6) | copy-start | bytes 1572868
  1.5 18.1 %copy-start.16 = (f32[256,64]{0,1:T(8,128)S(1)}, f32[256,64]{0,1:T(8,128)}, u32[]{:S(2)}) copy-start(f32[256,64]{0,1:T(8,128)} %param.9) | copy-start | bytes 196612
  3.0 112.2 %copy-start.3 = (bf16[128,2048]{1,0:T(8,128)(2,1)}, bf16[128,2048]{1,0:T(8,128)(2,1)S(1)}, u32[]{:S(2)}) copy-start(bf16[128,2048]{1,0:T(8,128)(2,1)S(1)} %get-tuple-element.28.refs_0_) | copy-start | bytes 1572868
  3.0 82.5 %collective-permute-start.7 = (bf16[128,2048]{1,0:T(8,128)(2,1)S(1)}, bf16[128,2048]{1,0:T(8,128)(2,1)S(1)}, u32[]{:S(2)}, u32[]{:S(2)}) collective-permute-start(bf16[128,2048]{1,0:T(8,128)(2,1)S(1)} %get-tuple-element.28.refs_0_), channel_id=1, source_target_pairs={{0,2},{2,4},{4,6},{6,0},{1,3},{3,5},{5,7},{7,1},{8,10},{10,12},{12... | collective-permute-start | bytes 1572872 | tf_op jit(solution)/shard_map/ppermute | solution.py:23
  6.9 76.3 %collective-permute-start.10 = (bf16[128,2048]{1,0:T(8,128)(2,1)S(1)}, bf16[128,2048]{1,0:T(8,128)(2,1)S(1)}, u32[]{:S(2)}, u32[]{:S(2)}) collective-permute-start(bf16[128,2048]{1,0:T(8,128)(2,1)S(1)} %get-tuple-element.27), channel_id=1, source_target_pairs={{0,1},{1,0},{2,3},{3,2},{4,5},{5,4},{6,7},{7,6},{8,9},{9,8},{10,11... | collective-permute-start | bytes 1572872 | tf_op jit(solution)/shard_map/ppermute | solution.py:27
  17.6 72.2 %collective-permute-start.15 = (bf16[1024,256]{1,0:T(8,128)(2,1)S(1)}, bf16[1024,256]{1,0:T(8,128)(2,1)S(1)}, u32[]{:S(2)}, u32[]{:S(2)}) collective-permute-start(bf16[1024,256]{1,0:T(8,128)(2,1)S(1)} %copy-done.4), channel_id=1, source_target_pairs={{0,1},{1,0},{2,3},{3,2},{4,5},{5,4},{6,7},{7,6},{8,9},{9,8},{10,11... | collective-permute-start | bytes 1572872 | tf_op jit(solution)/shard_map/ppermute | solution.py:27
  19.5 20.8 %collective-permute-start.1 = (bf16[64,256]{1,0:T(8,128)(2,1)S(1)}, bf16[64,256]{1,0:T(8,128)(2,1)S(1)}, u32[]{:S(2)}, u32[]{:S(2)}) collective-permute-start(bf16[64,256]{1,0:T(8,128)(2,1)S(1)} %convert_bitcast_fusion), channel_id=1, source_target_pairs={{0,256},{1,0},{256,257},{257,1},{2,258},{3,2},{258,259},{259,3},{4... | collective-permute-start | bytes 98312 | tf_op jit(solution)/shard_map/ppermute | solution.py:36
  23.6 16.8 %collective-permute-start = (bf16[64,256]{1,0:T(8,128)(2,1)S(1)}, bf16[64,256]{1,0:T(8,128)(2,1)S(1)}, u32[]{:S(2)}, u32[]{:S(2)}) collective-permute-start(bf16[64,256]{1,0:T(8,128)(2,1)S(1)} %convert_bitcast_fusion), channel_id=1, source_target_pairs={{0,0},{1,256},{256,1},{257,257},{2,2},{3,258},{258,3},{259,259},{4... | collective-permute-start | bytes 98312 | tf_op jit(solution)/shard_map/ppermute | solution.py:36
  40.3 28.6 %collective-permute-start.2 = (bf16[1,64,512]{2,1,0:T(8,128)(2,1)S(1)}, bf16[1,64,512]{2,1,0:T(8,128)(2,1)S(1)}, u32[]{:S(2)}, u32[]{:S(2)}) collective-permute-start(bf16[1,64,512]{2,1,0:T(8,128)(2,1)S(1)} %maximum_bitcast_fusion), channel_id=1, source_target_pairs={{0,128},{128,0},{1,129},{129,1},{2,130},{130,2},{3,131},{131,3},{4... | collective-permute-start | bytes 196616 | tf_op jit(solution)/shard_map/ppermute | solution.py:27
  68.9 10.8 %collective-permute-start.3 = (bf16[2,64,512]{2,1,0:T(8,128)(2,1)S(1)}, bf16[2,64,512]{2,1,0:T(8,128)(2,1)S(1)}, u32[]{:S(2)}, u32[]{:S(2)}) collective-permute-start(bf16[2,64,512]{2,1,0:T(8,128)(2,1)S(1)} %pad_maximum_fusion.2), channel_id=1, source_target_pairs={{0,64},{16,80},{32,96},{48,112},{64,0},{80,16},{96,32},{112,48},{1... | collective-permute-start | bytes 393224 | tf_op jit(solution)/shard_map/ppermute | solution.py:27
  76.4 20.2 %collective-permute-start.8 = (bf16[128,2048]{1,0:T(8,128)(2,1)S(1)}, bf16[128,2048]{1,0:T(8,128)(2,1)S(1)}, u32[]{:S(2)}, u32[]{:S(2)}) collective-permute-start(bf16[128,2048]{1,0:T(8,128)(2,1)S(1)} %get-tuple-element.28.refs_0_), channel_id=1, source_target_pairs={{0,6},{2,0},{4,2},{6,4},{1,7},{3,1},{5,3},{7,5},{8,14},{10,8},{12,... | collective-permute-start | bytes 1572872 | tf_op jit(solution)/shard_map/ppermute | solution.py:23
  79.8 22.0 %collective-permute-start.9 = (bf16[128,2048]{1,0:T(8,128)(2,1)S(1)}, bf16[128,2048]{1,0:T(8,128)(2,1)}, u32[]{:S(2)}, u32[]{:S(2)}) collective-permute-start(bf16[128,2048]{1,0:T(8,128)(2,1)S(1)} %get-tuple-element.28.refs_0_), channel_id=1, source_target_pairs={{0,4},{2,6},{4,0},{6,2},{1,5},{3,7},{5,1},{7,3},{8,12},{10,14},{12... | collective-permute-start | bytes 1572872 | tf_op jit(solution)/shard_map/ppermute | solution.py:23
  83.2 32.0 %copy-start.6 = (bf16[128,2048]{1,0:T(8,128)(2,1)}, bf16[128,2048]{1,0:T(8,128)(2,1)S(1)}, u32[]{:S(2)}) copy-start(bf16[128,2048]{1,0:T(8,128)(2,1)S(1)} %collective-permute-done.10.refs_4_) | copy-start | bytes 1572868
  83.2 27.4 %collective-permute-start.11 = (bf16[128,2048]{1,0:T(8,128)(2,1)S(1)}, bf16[128,2048]{1,0:T(8,128)(2,1)}, u32[]{:S(2)}, u32[]{:S(2)}) collective-permute-start(bf16[128,2048]{1,0:T(8,128)(2,1)S(1)} %collective-permute-done.10.refs_4_), channel_id=1, source_target_pairs={{0,2},{2,4},{4,6},{6,0},{1,3},{3,5},{5,7},{7,1},{8,10},{10,12},{12... | collective-permute-start | bytes 1572872 | tf_op jit(solution)/shard_map/ppermute | solution.py:23
  85.5 29.7 %copy-start.5 = (bf16[128,2048]{1,0:T(8,128)(2,1)}, bf16[128,2048]{1,0:T(8,128)(2,1)S(1)}, u32[]{:S(2)}) copy-start(bf16[128,2048]{1,0:T(8,128)(2,1)S(1)} %collective-permute-done.7.refs_1_) | copy-start | bytes 1572868
  85.5 26.7 %collective-permute-start.12 = (bf16[128,2048]{1,0:T(8,128)(2,1)S(1)}, bf16[128,2048]{1,0:T(8,128)(2,1)}, u32[]{:S(2)}, u32[]{:S(2)}) collective-permute-start(bf16[128,2048]{1,0:T(8,128)(2,1)S(1)} %collective-permute-done.10.refs_4_), channel_id=1, source_target_pairs={{0,6},{2,0},{4,2},{6,4},{1,7},{3,1},{5,3},{7,5},{8,14},{10,8},{12,... | collective-permute-start | bytes 1572872 | tf_op jit(solution)/shard_map/ppermute | solution.py:23
  89.8 0.8 copy-start.8
  90.6 24.6 %collective-permute-start.13 = (bf16[128,2048]{1,0:T(8,128)(2,1)S(1)}, bf16[128,2048]{1,0:T(8,128)(2,1)}, u32[]{:S(2)}, u32[]{:S(2)}) collective-permute-start(bf16[128,2048]{1,0:T(8,128)(2,1)S(1)} %collective-permute-done.10.refs_4_), channel_id=1, source_target_pairs={{0,4},{2,6},{4,0},{6,2},{1,5},{3,7},{5,1},{7,3},{8,12},{10,14},{12... | collective-permute-start | bytes 1572872 | tf_op jit(solution)/shard_map/ppermute | solution.py:23
  96.6 18.6 %copy-start.7 = (bf16[128,2048]{1,0:T(8,128)(2,1)}, bf16[128,2048]{1,0:T(8,128)(2,1)S(1)}, u32[]{:S(2)}) copy-start(bf16[128,2048]{1,0:T(8,128)(2,1)S(1)} %collective-permute-done.8.refs_2_) | copy-start | bytes 1572868
  96.6 33.8 %collective-permute-start.4 = (bf16[4,64,512]{2,1,0:T(8,128)(2,1)S(1)}, bf16[4,64,512]{2,1,0:T(8,128)(2,1)S(1)}, u32[]{:S(2)}, u32[]{:S(2)}) collective-permute-start(bf16[4,64,512]{2,1,0:T(8,128)(2,1)S(1)} %pad_maximum_fusion.1), channel_id=1, source_target_pairs={{0,32},{16,48},{32,0},{48,16},{64,96},{80,112},{96,64},{112,80},{1... | collective-permute-start | bytes 786440 | tf_op jit(solution)/shard_map/ppermute | solution.py:27
  123.6 25.3 %collective-permute-start.16 = (bf16[8,2,256,128]{3,2,1,0:T(8,128)(2,1)}, bf16[8,2,256,128]{3,2,1,0:T(8,128)(2,1)S(1)}, u32[]{:S(2)}, u32[]{:S(2)}) collective-permute-start(bf16[8,2,256,128]{3,2,1,0:T(8,128)(2,1)} %get-tuple-element.11), channel_id=1, source_target_pairs={{0,8},{8,0},{1,9},{9,1},{2,10},{10,2},{3,11},{11,3},{4,12},{12,4},... | collective-permute-start | bytes 3145736 | tf_op jit(solution)/shard_map/ppermute | solution.py:27
  130.4 18.4 %copy-start.2 = (f32[8,2,256,128]{3,2,1,0:T(8,128)S(1)}, f32[8,2,256,128]{3,2,1,0:T(8,128)}, u32[]{:S(2)}) copy-start(f32[8,2,256,128]{3,2,1,0:T(8,128)} %get-tuple-element.10) | copy-start | bytes 6291460
  130.5 15.5 %collective-permute-start.5 = (bf16[8,64,512]{2,1,0:T(8,128)(2,1)S(1)}, bf16[8,64,512]{2,1,0:T(8,128)(2,1)S(1)}, u32[]{:S(2)}, u32[]{:S(2)}) collective-permute-start(bf16[8,64,512]{2,1,0:T(8,128)(2,1)S(1)} %pad_maximum_fusion), channel_id=1, source_target_pairs={{0,16},{16,0},{32,48},{48,32},{64,80},{80,64},{96,112},{112,96},{1... | collective-permute-start | bytes 1572872 | tf_op jit(solution)/shard_map/ppermute | solution.py:27
  146.0 4.6 %copy-start = (bf16[16,64,512]{2,1,0:T(8,128)(2,1)}, bf16[16,64,512]{2,1,0:T(8,128)(2,1)S(1)}, u32[]{:S(2)}) copy-start(bf16[16,64,512]{2,1,0:T(8,128)(2,1)S(1)} %constant_dynamic-update-slice_fusion.a0_ref.a1_ref) | copy-start | bytes 3145732
  146.0 60.7 %collective-permute-start.6 = (bf16[16,64,512]{2,1,0:T(8,128)(2,1)S(1)}, bf16[16,64,512]{2,1,0:T(8,128)(2,1)S(1)}, u32[]{:S(2)}, u32[]{:S(2)}) collective-permute-start(bf16[16,64,512]{2,1,0:T(8,128)(2,1)S(1)} %constant_dynamic-update-slice_fusion.a0_ref.a1_ref), channel_id=1, source_target_pairs={{0,8},{8,0},{1,9},{9,1},{2,10},{10,2},{3,11},{11,3},{4,12},{12,4},... | collective-permute-start | bytes 3145736 | tf_op jit(solution)/shard_map/ppermute | solution.py:27
  148.9 17.8 %copy-start.18 = (f32[256]{0:T(256)S(1)}, f32[256]{0:T(256)}, u32[]{:S(2)}) copy-start(f32[256]{0:T(256)} %param.10) | copy-start | bytes 3076
  148.9 17.8 %copy-start.20 = (f32[64]{0:T(128)S(1)}, f32[64]{0:T(128)}, u32[]{:S(2)}) copy-start(f32[64]{0:T(128)} %param.11) | copy-start | bytes 772
  150.7 18.0 %collective-permute-start.17 = (bf16[2,256,128]{2,1,0:T(8,128)(2,1)S(1)}, bf16[2,256,128]{2,1,0:T(8,128)(2,1)S(1)}, u32[]{:S(2)}, u32[]{:S(2)}) collective-permute-start(bf16[2,256,128]{2,1,0:T(8,128)(2,1)S(1)} %get-tuple-element.26), channel_id=1, source_target_pairs={{0,64},{16,80},{32,96},{48,112},{64,0},{80,16},{96,32},{112,48},{1... | collective-permute-start | bytes 393224 | tf_op jit(solution)/shard_map/ppermute | solution.py:23
  158.4 15.8 %collective-permute-start.18 = (bf16[2,256,128]{2,1,0:T(8,128)(2,1)S(1)}, bf16[2,256,128]{2,1,0:T(8,128)(2,1)S(1)}, u32[]{:S(2)}, u32[]{:S(2)}) collective-permute-start(bf16[2,256,128]{2,1,0:T(8,128)(2,1)S(1)} %get-tuple-element.25), channel_id=1, source_target_pairs={{0,48},{16,64},{32,80},{48,96},{64,112},{80,0},{96,16},{112,32},{1... | collective-permute-start | bytes 393224 | tf_op jit(solution)/shard_map/ppermute | solution.py:23
  160.8 15.6 %collective-permute-start.19 = (bf16[2,256,128]{2,1,0:T(8,128)(2,1)S(1)}, bf16[2,256,128]{2,1,0:T(8,128)(2,1)S(1)}, u32[]{:S(2)}, u32[]{:S(2)}) collective-permute-start(bf16[2,256,128]{2,1,0:T(8,128)(2,1)S(1)} %get-tuple-element.24), channel_id=1, source_target_pairs={{0,80},{16,96},{32,112},{48,0},{64,16},{80,32},{96,48},{112,64},{1... | collective-permute-start | bytes 393224 | tf_op jit(solution)/shard_map/ppermute | solution.py:23
  166.7 16.5 %collective-permute-start.20 = (bf16[2,256,128]{2,1,0:T(8,128)(2,1)S(1)}, bf16[2,256,128]{2,1,0:T(8,128)(2,1)S(1)}, u32[]{:S(2)}, u32[]{:S(2)}) collective-permute-start(bf16[2,256,128]{2,1,0:T(8,128)(2,1)S(1)} %get-tuple-element.23), channel_id=1, source_target_pairs={{0,32},{16,48},{32,64},{48,80},{64,96},{80,112},{96,0},{112,16},{1... | collective-permute-start | bytes 393224 | tf_op jit(solution)/shard_map/ppermute | solution.py:23
  168.7 21.3 %copy-start.9 = (bf16[2,256,128]{2,1,0:T(8,128)(2,1)}, bf16[2,256,128]{2,1,0:T(8,128)(2,1)S(1)}, u32[]{:S(2)}) copy-start(bf16[2,256,128]{2,1,0:T(8,128)(2,1)S(1)} %collective-permute-done.17.refs_0_) | copy-start | bytes 393220
  168.7 21.2 %collective-permute-start.21 = (bf16[2,256,128]{2,1,0:T(8,128)(2,1)S(1)}, bf16[2,256,128]{2,1,0:T(8,128)(2,1)S(1)}, u32[]{:S(2)}, u32[]{:S(2)}) collective-permute-start(bf16[2,256,128]{2,1,0:T(8,128)(2,1)S(1)} %get-tuple-element.22), channel_id=1, source_target_pairs={{0,96},{16,112},{32,0},{48,16},{64,32},{80,48},{96,64},{112,80},{1... | collective-permute-start | bytes 393224 | tf_op jit(solution)/shard_map/ppermute | solution.py:23
  174.2 15.8 %copy-start.10 = (bf16[2,256,128]{2,1,0:T(8,128)(2,1)}, bf16[2,256,128]{2,1,0:T(8,128)(2,1)S(1)}, u32[]{:S(2)}) copy-start(bf16[2,256,128]{2,1,0:T(8,128)(2,1)S(1)} %collective-permute-done.18.refs_1_) | copy-start | bytes 393220
  174.2 15.8 %collective-permute-start.22 = (bf16[2,256,128]{2,1,0:T(8,128)(2,1)S(1)}, bf16[2,256,128]{2,1,0:T(8,128)(2,1)S(1)}, u32[]{:S(2)}, u32[]{:S(2)}) collective-permute-start(bf16[2,256,128]{2,1,0:T(8,128)(2,1)S(1)} %get-tuple-element.21), channel_id=1, source_target_pairs={{0,16},{16,32},{32,48},{48,64},{64,80},{80,96},{96,112},{112,0},{1... | collective-permute-start | bytes 393224 | tf_op jit(solution)/shard_map/ppermute | solution.py:23
  176.5 13.5 %copy-start.11 = (bf16[2,256,128]{2,1,0:T(8,128)(2,1)}, bf16[2,256,128]{2,1,0:T(8,128)(2,1)S(1)}, u32[]{:S(2)}) copy-start(bf16[2,256,128]{2,1,0:T(8,128)(2,1)S(1)} %collective-permute-done.19.refs_2_) | copy-start | bytes 393220
  176.5 13.5 %collective-permute-start.23 = (bf16[2,256,128]{2,1,0:T(8,128)(2,1)S(1)}, bf16[2,256,128]{2,1,0:T(8,128)(2,1)S(1)}, u32[]{:S(2)}, u32[]{:S(2)}) collective-permute-start(bf16[2,256,128]{2,1,0:T(8,128)(2,1)S(1)} %get-tuple-element.20), channel_id=1, source_target_pairs={{0,112},{16,0},{32,16},{48,32},{64,48},{80,64},{96,80},{112,96},{1... | collective-permute-start | bytes 393224 | tf_op jit(solution)/shard_map/ppermute | solution.py:23
  183.2 6.8 %copy-start.12 = (bf16[2,256,128]{2,1,0:T(8,128)(2,1)}, bf16[2,256,128]{2,1,0:T(8,128)(2,1)S(1)}, u32[]{:S(2)}) copy-start(bf16[2,256,128]{2,1,0:T(8,128)(2,1)S(1)} %collective-permute-done.20.refs_3_) | copy-start | bytes 393220
  183.2 61.3 %collective-permute-start.28 = (f32[320]{0:T(512)S(1)}, f32[320]{0:T(512)S(1)}, u32[]{:S(2)}, u32[]{:S(2)}) collective-permute-start(f32[320]{0:T(512)S(1)} %pad_maximum_fusion.5), channel_id=1, source_target_pairs={{0,0},{1,8},{8,256},{9,264},{256,1},{257,9},{264,257},{265,265},{2... | collective-permute-start | bytes 3848 | tf_op jit(solution)/shard_map/ppermute | solution.py:46
  189.9 0.6 copy-start.13
  189.9 0.7 copy-start.14
  190.6 0.6 copy-start.15
  194.4 25.3 %collective-permute-start.26 = (f32[64,256]{1,0:T(8,128)S(1)}, f32[64,256]{1,0:T(8,128)S(1)}, u32[]{:S(2)}, u32[]{:S(2)}) collective-permute-start(f32[64,256]{1,0:T(8,128)S(1)} %get-tuple-element.30), channel_id=1, source_target_pairs={{0,384},{128,0},{256,128},{384,256},{1,385},{129,1},{257,129},{385... | collective-permute-start | bytes 196616 | tf_op jit(solution)/shard_map/ppermute | solution.py:23
  201.1 18.6 %collective-permute-start.25 = (f32[64,256]{1,0:T(8,128)S(1)}, f32[64,256]{1,0:T(8,128)S(1)}, u32[]{:S(2)}, u32[]{:S(2)}) collective-permute-start(f32[64,256]{1,0:T(8,128)S(1)} %get-tuple-element.31), channel_id=1, source_target_pairs={{0,128},{128,256},{256,384},{384,0},{1,129},{129,257},{257,385},{3... | collective-permute-start | bytes 196616 | tf_op jit(solution)/shard_map/ppermute | solution.py:23
  203.0 41.7 %copy-start.21 = (pred[4]{0:T(512)(128)(4,1)S(1)}, pred[4]{0:T(512)(128)(4,1)}, u32[]{:S(2)}) copy-start(pred[4]{0:T(512)(128)(4,1)} %iota_compare_fusion.2) | copy-start | bytes 16
  203.0 16.7 %collective-permute-start.24 = (f32[64,256]{1,0:T(8,128)S(1)}, f32[64,256]{1,0:T(8,128)S(1)}, u32[]{:S(2)}, u32[]{:S(2)}) collective-permute-start(f32[64,256]{1,0:T(8,128)S(1)} %get-tuple-element.29), channel_id=1, source_target_pairs={{0,256},{128,384},{256,0},{384,128},{1,257},{129,385},{257,1},{385... | collective-permute-start | bytes 196616 | tf_op jit(solution)/shard_map/ppermute | solution.py:23
  206.7 0.9 copy-start.1
  217.7 75.0 %collective-permute-start.14 = (bf16[8,128,256]{2,1,0:T(8,128)(2,1)}, bf16[8,128,256]{2,1,0:T(8,128)(2,1)S(1)}, u32[]{:S(2)}, u32[]{:S(2)}) collective-permute-start(bf16[8,128,256]{2,1,0:T(8,128)(2,1)} %get-tuple-element.9), channel_id=1, source_target_pairs={{0,1},{1,0},{2,3},{3,2},{4,5},{5,4},{6,7},{7,6},{8,9},{9,8},{10,11... | collective-permute-start | bytes 1572872 | tf_op jit(solution)/shard_map/ppermute | solution.py:27
  220.7 71.4 %collective-permute-start.27 = (f32[64,256]{1,0:T(8,128)S(1)}, f32[64,256]{1,0:T(8,128)S(1)}, u32[]{:S(2)}, u32[]{:S(2)}) collective-permute-start(f32[64,256]{1,0:T(8,128)S(1)} %get-tuple-element.17), channel_id=1, source_target_pairs={{0,0},{1,256},{8,1},{9,257},{256,8},{257,264},{264,9},{265,265},{2... | collective-permute-start | bytes 196616 | tf_op jit(solution)/shard_map/ppermute | solution.py:46
  292.0 2.9 copy-start.17
  292.0 2.9 copy-start.19

commit v4 on v3

--- a/solution.py
+++ b/solution.py
@@ -70,21 +70,23 @@
     blocks, (keep_ref, send_ref) = refs[:-2], refs[-2:]
     tile = jnp.concatenate([ref[...] for ref in blocks], axis=0)
     got = jnp.dot(ctx_ref[...], tile, preferred_element_type=jnp.float32)
-    rows = keep_ref.shape[2]
-    for k in range(2):
-        span = slice(k * 128, (k + 1) * 128)
+    rows, cols = keep_ref.shape[2:]
+    for k in range(keep_ref.shape[0]):
+        span = slice(k * cols, (k + 1) * cols)
         send_ref[k, 0] = got[:rows, span].astype(send_ref.dtype)
         keep_ref[k, 0] = got[rows:, span]
 
 
-def back_kernel(info_ref, a0_ref, a1_ref, b0_ref, b1_ref, *refs):
-    blocks, (own_ref, other_ref, acc_ref) = refs[:-3], refs[-3:]
+def back_kernel(info_ref, *refs):
+    y_count = SIZE["y"]
+    mine_refs, came_refs = refs[:y_count], refs[y_count : 2 * y_count]
+    blocks, (own_ref, other_ref, acc_ref) = refs[2 * y_count : -3], refs[-3:]
     count, tokens, heads = own_ref.shape
     step = pl.program_id(0)
     first = info_ref[count + 3] == 0
     rows = []
-    for a_ref, b_ref in ((a0_ref, b0_ref), (a1_ref, b1_ref)):
-        mine, came = a_ref[0], b_ref[0]
+    for mine_ref, came_ref in zip(mine_refs, came_refs):
+        mine, came = mine_ref[0], came_ref[0]
         rows += [jnp.where(first, mine, came), jnp.where(first, came, mine)]
     tile = jnp.concatenate([ref[...] for ref in blocks], axis=0)
     got = jnp.dot(tile, jnp.concatenate(rows, axis=0), preferred_element_type=jnp.float32)
@@ -139,10 +141,9 @@
 def grad_of(ctx, blocks):
     twice, rows_in = ctx.shape
     tokens, half = blocks[0].shape
-    tile = 256
-    per_za = half // SIZE["za"] // tile
-    shape = (SIZE["y"], SIZE["za"], twice // 2, 128)
-    out = pl.BlockSpec((2, 1) + shape[2:], lambda t: (t % per_za, t // per_za, 0, 0))
+    tile = half // SIZE["za"]
+    shape = (SIZE["y"], SIZE["za"], twice // 2, tile // SIZE["y"])
+    out = pl.BlockSpec((SIZE["y"], 1) + shape[2:], lambda t: (0, t, 0, 0))
     return pl.pallas_call(
         grad_kernel,
         grid=(half // tile,),
@@ -164,15 +165,14 @@
     _, cols, twice = mine.shape
     tokens, half = blocks[0].shape
     count = len(blocks)
-    tile = 4 * cols
-    per_za = half // SIZE["za"] // tile
+    tile = half // SIZE["za"]
     shape = (count, tokens, twice // 2)
     full = pl.BlockSpec(shape, lambda k, p: (0, 0, 0))
 
-    def weights(low):
+    def weights(place):
         def index(k, p):
-            z = (k // per_za) ^ p[count + 1]
-            y = ((k % per_za) * 2 + low) ^ p[count + 2]
+            z = k ^ p[count + 1]
+            y = place ^ p[count + 2]
             return ((y & 1) * 8 + ((y >> 1) & 1) * 4 + ((y >> 2) & 1) * 2 + z, 0, 0)
 
         return pl.BlockSpec((1, cols, twice), index)
@@ -182,7 +182,7 @@
         grid_spec=pltpu.PrefetchScalarGridSpec(
             num_scalar_prefetch=1,
             grid=(half // tile,),
-            in_specs=[weights(0), weights(1), weights(0), weights(1)]
+            in_specs=[weights(y) for y in range(SIZE["y"])] * 2
             + [pl.BlockSpec((tokens, tile), lambda k, p: (0, k))] * count,
             out_specs=[full, full],
             scratch_shapes=[pltpu.VMEM((count * tokens, twice), jnp.float32)],
@@ -195,7 +195,7 @@
             flops=2 * twice * count * tokens * half, transcendentals=0, bytes_accessed=8 << 20
         ),
         name="back",
-    )(info, mine, mine, came, came, *blocks)
+    )(info, *([mine] * SIZE["y"] + [came] * SIZE["y"]), *blocks)
 
 
 def total_of(mine, came, cols):
@@ -239,7 +239,8 @@
     w = jnp.concatenate([w_a, w_b], axis=1)[None]
     w = jnp.concatenate([w, flip(w, "za")], axis=0)
     for bit in (2, 1, 0):
-        w = jnp.concatenate([w, flip(w, "y", 1 << bit)], axis=0)
+        other = flip(w, "y", 1 << bit)
+        w = jnp.concatenate([w, other], axis=0)
     w_came = flip(w, "c")
 
     stats = rotate(jnp.concatenate([row_stat, col_stat]), True)

time: 298 us -> 293 us (0.983)
  Pallas kernels: 23.8 us -> 18.6 us
  transfers between devices with their start and end apart: 29 -> 29, of which waited for: 6 -> 6; matrix products, arithmetic and copies ran while one was open for 3% -> 3% of each run, Pallas kernels for 8% -> 6%
where the time goes in v4:
time: 293 us; the launch traced here: 290 us
  starting transfers between devices  147 us (50%)
  blocking collectives  60.5 us (21%)
  waiting for transfers between devices  44.2 us (15%)
  Pallas kernels  18.6 us (6%)
  other arithmetic  9.37 us (3%)
  local copies, waits for them, and re-layouts  7.87 us (3%)
    ppermute x9, starting transfers between devices, flip(): return lax.ppermute(value, axis, [(i, i ^ mask) for i in range(SIZE[axis])])  66 us
    ppermute x16, starting transfers between devices, shift(): lax.ppermute(value, axes, [(i, (i + step) % size) for i in range(size)])  62 us
    ppermute x2, waiting for transfers between devices, turn(): return lax.ppermute(value, ('zb', 'zh'), pairs)  16.1 us
    ppermute x9, waiting for transfers between devices, flip(): return lax.ppermute(value, axis, [(i, i ^ mask) for i in range(SIZE[axis])])  14.6 us
    ppermute x2, starting transfers between devices, rotate(): return lax.ppermute(value, ('zb', 'c', 'zh'), pairs)  14.4 us
    psum x1, blocking collectives, per_device(): col_all = lax.psum(col_all, 'x')  13.6 us
    ppermute x16, waiting for transfers between devices, shift(): lax.ppermute(value, axes, [(i, (i + step) % size) for i in range(size)])  13.5 us
    psum x1, blocking collectives, per_device(): rows = lax.psum(rows, 'y')  10.7 us
  transfers between devices with their start and end apart: 29, of which 6 were waited for; matrix products, arithmetic and copies ran while one was open for 3% of the time, Pallas kernels for 6%

profile of v4, /device:TPU:1, one launch (start us, length us, event | category | flops | bytes accessed | tf_op | source)
XLA Modules:
  0.0 289.7 jit_solution(7495968116546510975)
XLA Ops:
  0.6 0.7 iota_compare_fusion
  1.5 1.4 broadcast_select_fusion
  3.0 3.9 %collective-permute-start.7 = (bf16[128,2048]{1,0:T(8,128)(2,1)S(1)}, bf16[128,2048]{1,0:T(8,128)(2,1)S(1)}, u32[]{:S(2)}, u32[]{:S(2)}) collective-permute-start(bf16[128,2048]{1,0:T(8,128)(2,1)S(1)} %get-tuple-element.28.refs_16_.refs_0_), channel_id=1, source_target_pairs={{0,2},{2,4},{4,6},{6,0},{1,3},{3,5},{5,7},{7,1},{8,10},{10,12},{12... | collective-permute-start | bytes 1572872 | tf_op jit(solution)/shard_map/ppermute | solution.py:23
  6.9 10.6 %collective-permute-start.10 = (bf16[128,2048]{1,0:T(8,128)(2,1)S(1)}, bf16[128,2048]{1,0:T(8,128)(2,1)S(1)}, u32[]{:S(2)}, u32[]{:S(2)}) collective-permute-start(bf16[128,2048]{1,0:T(8,128)(2,1)S(1)} %get-tuple-element.27), channel_id=1, source_target_pairs={{0,1},{1,0},{2,3},{3,2},{4,5},{5,4},{6,7},{7,6},{8,9},{9,8},{10,11... | collective-permute-start | bytes 1572872 | tf_op jit(solution)/shard_map/ppermute | solution.py:27
  17.6 1.9 collective-permute-start.15
  19.5 4.0 %collective-permute-start.1 = (bf16[64,256]{1,0:T(8,128)(2,1)S(1)}, bf16[64,256]{1,0:T(8,128)(2,1)S(1)}, u32[]{:S(2)}, u32[]{:S(2)}) collective-permute-start(bf16[64,256]{1,0:T(8,128)(2,1)S(1)} %convert_bitcast_fusion), channel_id=1, source_target_pairs={{0,256},{1,0},{256,257},{257,1},{2,258},{3,2},{258,259},{259,3},{4... | collective-permute-start | bytes 98312 | tf_op jit(solution)/shard_map/ppermute | solution.py:36
  23.6 0.7 collective-permute-start
  24.2 16.1 %collective-permute-done.1 = bf16[64,256]{1,0:T(8,128)(2,1)S(1)} collective-permute-done((bf16[64,256]{1,0:T(8,128)(2,1)S(1)}, bf16[64,256]{1,0:T(8,128)(2,1)S(1)}, u32[]{:S(2)}, u32[]{:S(2)}) %collective-permute-start.1) | collective-permute-done | bytes 32800 | tf_op jit(solution)/shard_map/ppermute | solution.py:36
  40.3 26.9 %collective-permute-start.2 = (bf16[1,64,512]{2,1,0:T(8,128)(2,1)S(1)}, bf16[1,64,512]{2,1,0:T(8,128)(2,1)S(1)}, u32[]{:S(2)}, u32[]{:S(2)}) collective-permute-start(bf16[1,64,512]{2,1,0:T(8,128)(2,1)S(1)} %maximum_bitcast_fusion), channel_id=1, source_target_pairs={{0,128},{128,0},{1,129},{129,1},{2,130},{130,2},{3,131},{131,3},{4... | collective-permute-start | bytes 196616 | tf_op jit(solution)/shard_map/ppermute | solution.py:27
  67.3 1.6 collective-permute-done.2
  68.9 7.5 %collective-permute-start.3 = (bf16[2,64,512]{2,1,0:T(8,128)(2,1)S(1)}, bf16[2,64,512]{2,1,0:T(8,128)(2,1)S(1)}, u32[]{:S(2)}, u32[]{:S(2)}) collective-permute-start(bf16[2,64,512]{2,1,0:T(8,128)(2,1)S(1)} %pad_maximum_fusion.2), channel_id=1, source_target_pairs={{0,64},{16,80},{32,96},{48,112},{64,0},{80,16},{96,32},{112,48},{1... | collective-permute-start | bytes 393224 | tf_op jit(solution)/shard_map/ppermute | solution.py:27
  76.4 3.4 %collective-permute-start.8 = (bf16[128,2048]{1,0:T(8,128)(2,1)S(1)}, bf16[128,2048]{1,0:T(8,128)(2,1)S(1)}, u32[]{:S(2)}, u32[]{:S(2)}) collective-permute-start(bf16[128,2048]{1,0:T(8,128)(2,1)S(1)} %get-tuple-element.28.refs_16_.refs_0_), channel_id=1, source_target_pairs={{0,6},{2,0},{4,2},{6,4},{1,7},{3,1},{5,3},{7,5},{8,14},{10,8},{12,... | collective-permute-start | bytes 1572872 | tf_op jit(solution)/shard_map/ppermute | solution.py:23
  79.8 3.4 %collective-permute-start.9 = (bf16[128,2048]{1,0:T(8,128)(2,1)S(1)}, bf16[128,2048]{1,0:T(8,128)(2,1)}, u32[]{:S(2)}, u32[]{:S(2)}) collective-permute-start(bf16[128,2048]{1,0:T(8,128)(2,1)S(1)} %get-tuple-element.28.refs_16_.refs_0_), channel_id=1, source_target_pairs={{0,4},{2,6},{4,0},{6,2},{1,5},{3,7},{5,1},{7,3},{8,12},{10,14},{12... | collective-permute-start | bytes 1572872 | tf_op jit(solution)/shard_map/ppermute | solution.py:23
  83.2 2.2 collective-permute-start.11
  85.5 4.3 %collective-permute-start.12 = (bf16[128,2048]{1,0:T(8,128)(2,1)S(1)}, bf16[128,2048]{1,0:T(8,128)(2,1)}, u32[]{:S(2)}, u32[]{:S(2)}) collective-permute-start(bf16[128,2048]{1,0:T(8,128)(2,1)S(1)} %collective-permute-done.10.refs_20_.refs_4_), channel_id=1, source_target_pairs={{0,6},{2,0},{4,2},{6,4},{1,7},{3,1},{5,3},{7,5},{8,14},{10,8},{12,... | collective-permute-start | bytes 1572872 | tf_op jit(solution)/shard_map/ppermute | solution.py:23
  89.8 0.8 copy-done.8
  90.6 2.1 collective-permute-start.13
  92.7 0.6 stack.55.info_ref
  93.4 3.2 %arrange.1.ctx_ref = bf16[512,1024]{1,0:T(8,128)(2,1)} custom-call(s32[13]{0:T(128)} %stack.55.info_ref, bf16[8,128,256]{2,1,0:T(8,128)(2,1)} %bitcast.65, bf16[8,128,256]{2,1,0:T(8,128)(2,1)} %bitcast.66), custom_call_target="tpu_custom_call" | custom-call | tf_op jit(solution)/shard_map/arrange/pallas_call | solution.py:128
  96.6 5.1 %collective-permute-start.4 = (bf16[4,64,512]{2,1,0:T(8,128)(2,1)S(1)}, bf16[4,64,512]{2,1,0:T(8,128)(2,1)S(1)}, u32[]{:S(2)}, u32[]{:S(2)}) collective-permute-start(bf16[4,64,512]{2,1,0:T(8,128)(2,1)S(1)} %pad_maximum_fusion.1), channel_id=1, source_target_pairs={{0,32},{16,48},{32,0},{48,16},{64,96},{80,112},{96,64},{112,80},{1... | collective-permute-start | bytes 786440 | tf_op jit(solution)/shard_map/ppermute | solution.py:27
  101.7 8.9 %collective-permute-done.11.refs_21_.refs_5_ = bf16[128,2048]{1,0:T(8,128)(2,1)} collective-permute-done((bf16[128,2048]{1,0:T(8,128)(2,1)S(1)}, bf16[128,2048]{1,0:T(8,128)(2,1)}, u32[]{:S(2)}, u32[]{:S(2)}) %collective-permute-start.11) | collective-permute-done | bytes 524320 | tf_op jit(solution)/shard_map/ppermute | solution.py:23
  110.7 1.5 collective-permute-done.12.refs_22_.refs_6_
  112.2 3.0 %collective-permute-done.13.refs_23_.refs_7_ = bf16[128,2048]{1,0:T(8,128)(2,1)} collective-permute-done((bf16[128,2048]{1,0:T(8,128)(2,1)S(1)}, bf16[128,2048]{1,0:T(8,128)(2,1)}, u32[]{:S(2)}, u32[]{:S(2)}) %collective-permute-start.13) | collective-permute-done | bytes 524320 | tf_op jit(solution)/shard_map/ppermute | solution.py:23
  115.2 6.1 %grad.1 = (f32[8,2,256,128]{3,2,1,0:T(8,128)}, bf16[8,2,256,128]{3,2,1,0:T(8,128)(2,1)}) custom-call(bf16[512,1024]{1,0:T(8,128)(2,1)} %arrange.1.ctx_ref, bf16[128,2048]{1,0:T(8,128)(2,1)} %copy-done.3, bf16[128,2048]{1,0:T(8,128)(2,1)} %copy-done.5, bf16[128,2048]{1,0:T(8,128)(2,1)} %copy-done.7, ...), custom_call_target="tpu_custom_call" | custom-call | flops 2147483648 | bytes 9437184 | tf_op jit(solution)/shard_map/grad/pallas_call | solution.py:147
  121.2 6.8 %collective-permute-start.16 = (bf16[8,2,256,128]{3,2,1,0:T(8,128)(2,1)}, bf16[8,2,256,128]{3,2,1,0:T(8,128)(2,1)S(1)}, u32[]{:S(2)}, u32[]{:S(2)}) collective-permute-start(bf16[8,2,256,128]{3,2,1,0:T(8,128)(2,1)} %get-tuple-element.11), channel_id=1, source_target_pairs={{0,8},{8,0},{1,9},{9,1},{2,10},{10,2},{3,11},{11,3},{4,12},{12,4},... | collective-permute-start | bytes 3145736 | tf_op jit(solution)/shard_map/ppermute | solution.py:27
  128.2 2.4 collective-permute-start.5
  130.7 13.0 %collective-permute-done.5 = bf16[8,64,512]{2,1,0:T(8,128)(2,1)S(1)} collective-permute-done((bf16[8,64,512]{2,1,0:T(8,128)(2,1)S(1)}, bf16[8,64,512]{2,1,0:T(8,128)(2,1)S(1)}, u32[]{:S(2)}, u32[]{:S(2)}) %collective-permute-start.5) | collective-permute-done | bytes 524320 | tf_op jit(solution)/shard_map/ppermute | solution.py:27
  143.7 2.8 collective-permute-start.6
  146.6 1.7 fusion.6
  148.4 7.7 %collective-permute-start.17 = (bf16[2,256,128]{2,1,0:T(8,128)(2,1)S(1)}, bf16[2,256,128]{2,1,0:T(8,128)(2,1)S(1)}, u32[]{:S(2)}, u32[]{:S(2)}) collective-permute-start(bf16[2,256,128]{2,1,0:T(8,128)(2,1)S(1)} %get-tuple-element.26), channel_id=1, source_target_pairs={{0,64},{16,80},{32,96},{48,112},{64,0},{80,16},{96,32},{112,48},{1... | collective-permute-start | bytes 393224 | tf_op jit(solution)/shard_map/ppermute | solution.py:23
  156.1 2.5 collective-permute-start.18
  158.5 5.8 %collective-permute-start.19 = (bf16[2,256,128]{2,1,0:T(8,128)(2,1)S(1)}, bf16[2,256,128]{2,1,0:T(8,128)(2,1)S(1)}, u32[]{:S(2)}, u32[]{:S(2)}) collective-permute-start(bf16[2,256,128]{2,1,0:T(8,128)(2,1)S(1)} %get-tuple-element.24), channel_id=1, source_target_pairs={{0,80},{16,96},{32,112},{48,0},{64,16},{80,32},{96,48},{112,64},{1... | collective-permute-start | bytes 393224 | tf_op jit(solution)/shard_map/ppermute | solution.py:23
  164.4 1.9 collective-permute-start.20
  166.4 5.5 %collective-permute-start.21 = (bf16[2,256,128]{2,1,0:T(8,128)(2,1)S(1)}, bf16[2,256,128]{2,1,0:T(8,128)(2,1)S(1)}, u32[]{:S(2)}, u32[]{:S(2)}) collective-permute-start(bf16[2,256,128]{2,1,0:T(8,128)(2,1)S(1)} %get-tuple-element.22), channel_id=1, source_target_pairs={{0,96},{16,112},{32,0},{48,16},{64,32},{80,48},{96,64},{112,80},{1... | collective-permute-start | bytes 393224 | tf_op jit(solution)/shard_map/ppermute | solution.py:23
  171.9 2.3 collective-permute-start.22
  174.2 4.6 %collective-permute-start.23 = (bf16[2,256,128]{2,1,0:T(8,128)(2,1)S(1)}, bf16[2,256,128]{2,1,0:T(8,128)(2,1)S(1)}, u32[]{:S(2)}, u32[]{:S(2)}) collective-permute-start(bf16[2,256,128]{2,1,0:T(8,128)(2,1)S(1)} %get-tuple-element.20), channel_id=1, source_target_pairs={{0,112},{16,0},{32,16},{48,32},{64,48},{80,64},{96,80},{112,96},{1... | collective-permute-start | bytes 393224 | tf_op jit(solution)/shard_map/ppermute | solution.py:23
  178.7 0.5 iota_compare_fusion.2
  179.3 1.7 dynamic-slice_bitcast_fusion.mine_ref
  180.9 6.6 %collective-permute-start.28 = (f32[320]{0:T(512)S(1)}, f32[320]{0:T(512)S(1)}, u32[]{:S(2)}, u32[]{:S(2)}) collective-permute-start(f32[320]{0:T(512)S(1)} %pad_maximum_fusion.5), channel_id=1, source_target_pairs={{0,0},{1,8},{8,256},{9,264},{256,1},{257,9},{264,257},{265,265},{2... | collective-permute-start | bytes 3848 | tf_op jit(solution)/shard_map/ppermute | solution.py:46
  187.6 0.6 copy-done.13
  188.2 0.6 copy-done.15
  188.9 2.2 total.1
  191.1 0.9 dynamic-slice_bitcast_fusion.10
  192.0 6.8 %collective-permute-start.26 = (f32[64,256]{1,0:T(8,128)S(1)}, f32[64,256]{1,0:T(8,128)S(1)}, u32[]{:S(2)}, u32[]{:S(2)}) collective-permute-start(f32[64,256]{1,0:T(8,128)S(1)} %get-tuple-element.30), channel_id=1, source_target_pairs={{0,384},{128,0},{256,128},{384,256},{1,385},{129,1},{257,129},{385... | collective-permute-start | bytes 196616 | tf_op jit(solution)/shard_map/ppermute | solution.py:23
  198.8 1.9 collective-permute-start.25
  200.7 3.7 %collective-permute-start.24 = (f32[64,256]{1,0:T(8,128)S(1)}, f32[64,256]{1,0:T(8,128)S(1)}, u32[]{:S(2)}, u32[]{:S(2)}) collective-permute-start(f32[64,256]{1,0:T(8,128)S(1)} %get-tuple-element.29), channel_id=1, source_target_pairs={{0,256},{128,384},{256,0},{384,128},{1,257},{129,385},{257,1},{385... | collective-permute-start | bytes 196616 | tf_op jit(solution)/shard_map/ppermute | solution.py:23
  204.4 0.9 copy-done.1
  205.4 7.2 %back.1 = (f32[8,128,256]{2,1,0:T(8,128)}, bf16[8,128,256]{2,1,0:T(8,128)(2,1)}) custom-call(s32[13]{0:T(128)} %stack.55.info_ref, bf16[16,64,512]{2,1,0:T(8,128)(2,1)} %copy-done, bf16[16,64,512]{2,1,0:T(8,128)(2,1)} %copy-done, bf16[16,64,512]{2,1,0:T(8,128)(2,1)} %copy-done, bf16[16,64,512]{2,1,0:T(8,128)(2,1)} %copy-done, bf16[16,64,512]{2,1,0:T(8,128)(2,1)} %copy-done, ...), custom_call_target="tpu_custom_call" | custom-call | flops 2147483648 | bytes 8388608 | tf_op jit(solution)/shard_map/back/pallas_call | solution.py:180
  212.5 1.9 collective-permute-start.14
  214.5 1.0 add_reduce_fusion
  215.5 7.8 %collective-permute-start.27 = (f32[64,256]{1,0:T(8,128)S(1)}, f32[64,256]{1,0:T(8,128)S(1)}, u32[]{:S(2)}, u32[]{:S(2)}) collective-permute-start(f32[64,256]{1,0:T(8,128)S(1)} %get-tuple-element.17), channel_id=1, source_target_pairs={{0,0},{1,256},{8,1},{9,257},{256,8},{257,264},{264,9},{265,265},{2... | collective-permute-start | bytes 196616 | tf_op jit(solution)/shard_map/ppermute | solution.py:46
  223.2 2.5 psum.49
  225.7 13.6 %psum.50 = f32[64]{0:T(128)S(1)} all-reduce(f32[64]{0:T(128)S(1)} %psum.49), channel_id=1, replica_groups=mesh['zb'=2,'za'=2,'y'=8,'c'=2,'x'=4,'zh'=2] {'x'}, use_global_device_ids=true, to_apply=%region_3.4 | all-reduce | flops 64 | bytes 512 | tf_op jit(solution)/shard_map/psum | solution.py:270
  239.3 0.1 add_reduce_fusion.1
  239.6 10.7 %psum.51 = f32[512]{0:T(512)S(1)} all-reduce(f32[512]{0:T(512)S(1)} %pad_maximum_fusion.6), channel_id=1, replica_groups=mesh['zb'=2,'za'=2,'y'=8,'c'=2,'x'=4,'zh'=2] {'y'}, use_global_device_ids=true, to_apply=%region_5.6 | all-reduce | flops 512 | bytes 4096 | tf_op jit(solution)/shard_map/psum | solution.py:274
  250.3 9.0 %psum.52 = f32[768]{0:T(1024)S(1)} all-reduce(f32[768]{0:T(1024)S(1)} %pad_maximum_fusion.3), channel_id=1, replica_groups=mesh['zb'=2,'za'=2,'y'=8,'c'=2,'x'=4,'zh'=2] {'zb','za'}, use_global_device_ids=true, to_apply=%region_6.7 | all-reduce | flops 768 | bytes 6144 | tf_op jit(solution)/shard_map/psum | solution.py:275
  259.4 7.7 %psum.53 = f32[1024]{0:T(1024)S(1)} all-reduce(f32[1024]{0:T(1024)S(1)} %pad_maximum_fusion.4), channel_id=1, replica_groups=mesh['zb'=2,'za'=2,'y'=8,'c'=2,'x'=4,'zh'=2] {'zh'}, use_global_device_ids=true, to_apply=%region_7.8 | all-reduce | flops 1024 | bytes 8192 | tf_op jit(solution)/shard_map/psum | solution.py:277
  267.1 0.6 fusion.3
  267.8 0.6 concatenate.42
  268.4 10.4 %psum.54 = f32[640]{0:T(1024)S(1)} all-reduce(f32[640]{0:T(1024)S(1)} %concatenate.42), channel_id=1, replica_groups=mesh['zb'=2,'za'=2,'y'=8,'c'=2,'x'=4,'zh'=2] {'c'}, use_global_device_ids=true, to_apply=%region_9.10 | all-reduce | flops 640 | bytes 5120 | tf_op jit(solution)/shard_map/psum | solution.py:283
  278.8 0.5 slice.51
  279.3 6.7 %psum.55 = f32[]{:T(128)} all-reduce(f32[]{:T(128)} %bitcast.32), channel_id=1, replica_groups=mesh['zb'=2,'za'=2,'y'=8,'c'=2,'x'=4,'zh'=2] {'x'}, use_global_device_ids=true, to_apply=%region_10.11 | all-reduce | flops 1 | bytes 8 | tf_op jit(solution)/shard_map/psum | solution.py:285
  286.9 0.7 divide_bitcast_fusion
  287.6 2.1 add_convert_fusion
  (97 shorter events, 1.1 us)
Async XLA Ops:
  1.5 16.1 %copy-start.4 = (bf16[1024,256]{1,0:T(8,128)(2,1)S(1)}, bf16[1024,256]{1,0:T(8,128)(2,1)}, u32[]{:S(2)}) copy-start(bf16[1024,256]{1,0:T(8,128)(2,1)} %param.6) | copy-start | bytes 1572868
  1.5 18.1 %copy-start.16 = (f32[256,64]{0,1:T(8,128)S(1)}, f32[256,64]{0,1:T(8,128)}, u32[]{:S(2)}) copy-start(f32[256,64]{0,1:T(8,128)} %param.9) | copy-start | bytes 196612
  3.0 112.2 %copy-start.3 = (bf16[128,2048]{1,0:T(8,128)(2,1)}, bf16[128,2048]{1,0:T(8,128)(2,1)S(1)}, u32[]{:S(2)}) copy-start(bf16[128,2048]{1,0:T(8,128)(2,1)S(1)} %get-tuple-element.28.refs_16_.refs_0_) | copy-start | bytes 1572868
  3.0 82.5 %collective-permute-start.7 = (bf16[128,2048]{1,0:T(8,128)(2,1)S(1)}, bf16[128,2048]{1,0:T(8,128)(2,1)S(1)}, u32[]{:S(2)}, u32[]{:S(2)}) collective-permute-start(bf16[128,2048]{1,0:T(8,128)(2,1)S(1)} %get-tuple-element.28.refs_16_.refs_0_), channel_id=1, source_target_pairs={{0,2},{2,4},{4,6},{6,0},{1,3},{3,5},{5,7},{7,1},{8,10},{10,12},{12... | collective-permute-start | bytes 1572872 | tf_op jit(solution)/shard_map/ppermute | solution.py:23
  6.9 76.3 %collective-permute-start.10 = (bf16[128,2048]{1,0:T(8,128)(2,1)S(1)}, bf16[128,2048]{1,0:T(8,128)(2,1)S(1)}, u32[]{:S(2)}, u32[]{:S(2)}) collective-permute-start(bf16[128,2048]{1,0:T(8,128)(2,1)S(1)} %get-tuple-element.27), channel_id=1, source_target_pairs={{0,1},{1,0},{2,3},{3,2},{4,5},{5,4},{6,7},{7,6},{8,9},{9,8},{10,11... | collective-permute-start | bytes 1572872 | tf_op jit(solution)/shard_map/ppermute | solution.py:27
  17.6 72.2 %collective-permute-start.15 = (bf16[1024,256]{1,0:T(8,128)(2,1)S(1)}, bf16[1024,256]{1,0:T(8,128)(2,1)S(1)}, u32[]{:S(2)}, u32[]{:S(2)}) collective-permute-start(bf16[1024,256]{1,0:T(8,128)(2,1)S(1)} %copy-done.4), channel_id=1, source_target_pairs={{0,1},{1,0},{2,3},{3,2},{4,5},{5,4},{6,7},{7,6},{8,9},{9,8},{10,11... | collective-permute-start | bytes 1572872 | tf_op jit(solution)/shard_map/ppermute | solution.py:27
  19.5 20.8 %collective-permute-start.1 = (bf16[64,256]{1,0:T(8,128)(2,1)S(1)}, bf16[64,256]{1,0:T(8,128)(2,1)S(1)}, u32[]{:S(2)}, u32[]{:S(2)}) collective-permute-start(bf16[64,256]{1,0:T(8,128)(2,1)S(1)} %convert_bitcast_fusion), channel_id=1, source_target_pairs={{0,256},{1,0},{256,257},{257,1},{2,258},{3,2},{258,259},{259,3},{4... | collective-permute-start | bytes 98312 | tf_op jit(solution)/shard_map/ppermute | solution.py:36
  23.6 16.8 %collective-permute-start = (bf16[64,256]{1,0:T(8,128)(2,1)S(1)}, bf16[64,256]{1,0:T(8,128)(2,1)S(1)}, u32[]{:S(2)}, u32[]{:S(2)}) collective-permute-start(bf16[64,256]{1,0:T(8,128)(2,1)S(1)} %convert_bitcast_fusion), channel_id=1, source_target_pairs={{0,0},{1,256},{256,1},{257,257},{2,2},{3,258},{258,3},{259,259},{4... | collective-permute-start | bytes 98312 | tf_op jit(solution)/shard_map/ppermute | solution.py:36
  40.3 28.6 %collective-permute-start.2 = (bf16[1,64,512]{2,1,0:T(8,128)(2,1)S(1)}, bf16[1,64,512]{2,1,0:T(8,128)(2,1)S(1)}, u32[]{:S(2)}, u32[]{:S(2)}) collective-permute-start(bf16[1,64,512]{2,1,0:T(8,128)(2,1)S(1)} %maximum_bitcast_fusion), channel_id=1, source_target_pairs={{0,128},{128,0},{1,129},{129,1},{2,130},{130,2},{3,131},{131,3},{4... | collective-permute-start | bytes 196616 | tf_op jit(solution)/shard_map/ppermute | solution.py:27
  68.9 10.8 %collective-permute-start.3 = (bf16[2,64,512]{2,1,0:T(8,128)(2,1)S(1)}, bf16[2,64,512]{2,1,0:T(8,128)(2,1)S(1)}, u32[]{:S(2)}, u32[]{:S(2)}) collective-permute-start(bf16[2,64,512]{2,1,0:T(8,128)(2,1)S(1)} %pad_maximum_fusion.2), channel_id=1, source_target_pairs={{0,64},{16,80},{32,96},{48,112},{64,0},{80,16},{96,32},{112,48},{1... | collective-permute-start | bytes 393224 | tf_op jit(solution)/shard_map/ppermute | solution.py:27
  76.4 20.2 %collective-permute-start.8 = (bf16[128,2048]{1,0:T(8,128)(2,1)S(1)}, bf16[128,2048]{1,0:T(8,128)(2,1)S(1)}, u32[]{:S(2)}, u32[]{:S(2)}) collective-permute-start(bf16[128,2048]{1,0:T(8,128)(2,1)S(1)} %get-tuple-element.28.refs_16_.refs_0_), channel_id=1, source_target_pairs={{0,6},{2,0},{4,2},{6,4},{1,7},{3,1},{5,3},{7,5},{8,14},{10,8},{12,... | collective-permute-start | bytes 1572872 | tf_op jit(solution)/shard_map/ppermute | solution.py:23
  79.8 22.0 %collective-permute-start.9 = (bf16[128,2048]{1,0:T(8,128)(2,1)S(1)}, bf16[128,2048]{1,0:T(8,128)(2,1)}, u32[]{:S(2)}, u32[]{:S(2)}) collective-permute-start(bf16[128,2048]{1,0:T(8,128)(2,1)S(1)} %get-tuple-element.28.refs_16_.refs_0_), channel_id=1, source_target_pairs={{0,4},{2,6},{4,0},{6,2},{1,5},{3,7},{5,1},{7,3},{8,12},{10,14},{12... | collective-permute-start | bytes 1572872 | tf_op jit(solution)/shard_map/ppermute | solution.py:23
  83.2 32.0 %copy-start.6 = (bf16[128,2048]{1,0:T(8,128)(2,1)}, bf16[128,2048]{1,0:T(8,128)(2,1)S(1)}, u32[]{:S(2)}) copy-start(bf16[128,2048]{1,0:T(8,128)(2,1)S(1)} %collective-permute-done.10.refs_20_.refs_4_) | copy-start | bytes 1572868
  83.2 27.4 %collective-permute-start.11 = (bf16[128,2048]{1,0:T(8,128)(2,1)S(1)}, bf16[128,2048]{1,0:T(8,128)(2,1)}, u32[]{:S(2)}, u32[]{:S(2)}) collective-permute-start(bf16[128,2048]{1,0:T(8,128)(2,1)S(1)} %collective-permute-done.10.refs_20_.refs_4_), channel_id=1, source_target_pairs={{0,2},{2,4},{4,6},{6,0},{1,3},{3,5},{5,7},{7,1},{8,10},{10,12},{12... | collective-permute-start | bytes 1572872 | tf_op jit(solution)/shard_map/ppermute | solution.py:23
  85.5 29.7 %copy-start.5 = (bf16[128,2048]{1,0:T(8,128)(2,1)}, bf16[128,2048]{1,0:T(8,128)(2,1)S(1)}, u32[]{:S(2)}) copy-start(bf16[128,2048]{1,0:T(8,128)(2,1)S(1)} %collective-permute-done.7.refs_17_.refs_1_) | copy-start | bytes 1572868
  85.5 26.7 %collective-permute-start.12 = (bf16[128,2048]{1,0:T(8,128)(2,1)S(1)}, bf16[128,2048]{1,0:T(8,128)(2,1)}, u32[]{:S(2)}, u32[]{:S(2)}) collective-permute-start(bf16[128,2048]{1,0:T(8,128)(2,1)S(1)} %collective-permute-done.10.refs_20_.refs_4_), channel_id=1, source_target_pairs={{0,6},{2,0},{4,2},{6,4},{1,7},{3,1},{5,3},{7,5},{8,14},{10,8},{12,... | collective-permute-start | bytes 1572872 | tf_op jit(solution)/shard_map/ppermute | solution.py:23
  89.8 0.8 copy-start.8
  90.6 24.6 %collective-permute-start.13 = (bf16[128,2048]{1,0:T(8,128)(2,1)S(1)}, bf16[128,2048]{1,0:T(8,128)(2,1)}, u32[]{:S(2)}, u32[]{:S(2)}) collective-permute-start(bf16[128,2048]{1,0:T(8,128)(2,1)S(1)} %collective-permute-done.10.refs_20_.refs_4_), channel_id=1, source_target_pairs={{0,4},{2,6},{4,0},{6,2},{1,5},{3,7},{5,1},{7,3},{8,12},{10,14},{12... | collective-permute-start | bytes 1572872 | tf_op jit(solution)/shard_map/ppermute | solution.py:23
  96.6 18.6 %copy-start.7 = (bf16[128,2048]{1,0:T(8,128)(2,1)}, bf16[128,2048]{1,0:T(8,128)(2,1)S(1)}, u32[]{:S(2)}) copy-start(bf16[128,2048]{1,0:T(8,128)(2,1)S(1)} %collective-permute-done.8.refs_18_.refs_2_) | copy-start | bytes 1572868
  96.6 31.5 %collective-permute-start.4 = (bf16[4,64,512]{2,1,0:T(8,128)(2,1)S(1)}, bf16[4,64,512]{2,1,0:T(8,128)(2,1)S(1)}, u32[]{:S(2)}, u32[]{:S(2)}) collective-permute-start(bf16[4,64,512]{2,1,0:T(8,128)(2,1)S(1)} %pad_maximum_fusion.1), channel_id=1, source_target_pairs={{0,32},{16,48},{32,0},{48,16},{64,96},{80,112},{96,64},{112,80},{1... | collective-permute-start | bytes 786440 | tf_op jit(solution)/shard_map/ppermute | solution.py:27
  121.2 25.3 %collective-permute-start.16 = (bf16[8,2,256,128]{3,2,1,0:T(8,128)(2,1)}, bf16[8,2,256,128]{3,2,1,0:T(8,128)(2,1)S(1)}, u32[]{:S(2)}, u32[]{:S(2)}) collective-permute-start(bf16[8,2,256,128]{3,2,1,0:T(8,128)(2,1)} %get-tuple-element.11), channel_id=1, source_target_pairs={{0,8},{8,0},{1,9},{9,1},{2,10},{10,2},{3,11},{11,3},{4,12},{12,4},... | collective-permute-start | bytes 3145736 | tf_op jit(solution)/shard_map/ppermute | solution.py:27
  128.1 18.4 %copy-start.2 = (f32[8,2,256,128]{3,2,1,0:T(8,128)S(1)}, f32[8,2,256,128]{3,2,1,0:T(8,128)}, u32[]{:S(2)}) copy-start(f32[8,2,256,128]{3,2,1,0:T(8,128)} %get-tuple-element.10) | copy-start | bytes 6291460
  128.2 15.5 %collective-permute-start.5 = (bf16[8,64,512]{2,1,0:T(8,128)(2,1)S(1)}, bf16[8,64,512]{2,1,0:T(8,128)(2,1)S(1)}, u32[]{:S(2)}, u32[]{:S(2)}) collective-permute-start(bf16[8,64,512]{2,1,0:T(8,128)(2,1)S(1)} %pad_maximum_fusion), channel_id=1, source_target_pairs={{0,16},{16,0},{32,48},{48,32},{64,80},{80,64},{96,112},{112,96},{1... | collective-permute-start | bytes 1572872 | tf_op jit(solution)/shard_map/ppermute | solution.py:27
  143.7 4.6 %copy-start = (bf16[16,64,512]{2,1,0:T(8,128)(2,1)}, bf16[16,64,512]{2,1,0:T(8,128)(2,1)S(1)}, u32[]{:S(2)}) copy-start(bf16[16,64,512]{2,1,0:T(8,128)(2,1)S(1)} %constant_dynamic-update-slice_fusion.refs_0_.refs_1_.refs_2_.refs_3_.refs_4_.refs_5_.refs_6_.refs_7_) | copy-start | bytes 3145732
  143.7 60.7 %collective-permute-start.6 = (bf16[16,64,512]{2,1,0:T(8,128)(2,1)S(1)}, bf16[16,64,512]{2,1,0:T(8,128)(2,1)S(1)}, u32[]{:S(2)}, u32[]{:S(2)}) collective-permute-start(bf16[16,64,512]{2,1,0:T(8,128)(2,1)S(1)} %constant_dynamic-update-slice_fusion.refs_0_.refs_1_.refs_2_.refs_3_.refs_4_.refs_5_.refs_6_.refs_7_), channel_id=1, source_target_pairs={{0,8},{8,0},{1,9},{9,1},{2,10},{10,2},{3,11},{11,3},{4,12},{12,4},... | collective-permute-start | bytes 3145736 | tf_op jit(solution)/shard_map/ppermute | solution.py:27
  146.5 17.8 %copy-start.18 = (f32[256]{0:T(256)S(1)}, f32[256]{0:T(256)}, u32[]{:S(2)}) copy-start(f32[256]{0:T(256)} %param.10) | copy-start | bytes 3076
  146.6 17.8 %copy-start.20 = (f32[64]{0:T(128)S(1)}, f32[64]{0:T(128)}, u32[]{:S(2)}) copy-start(f32[64]{0:T(128)} %param.11) | copy-start | bytes 772
  148.4 18.0 %collective-permute-start.17 = (bf16[2,256,128]{2,1,0:T(8,128)(2,1)S(1)}, bf16[2,256,128]{2,1,0:T(8,128)(2,1)S(1)}, u32[]{:S(2)}, u32[]{:S(2)}) collective-permute-start(bf16[2,256,128]{2,1,0:T(8,128)(2,1)S(1)} %get-tuple-element.26), channel_id=1, source_target_pairs={{0,64},{16,80},{32,96},{48,112},{64,0},{80,16},{96,32},{112,48},{1... | collective-permute-start | bytes 393224 | tf_op jit(solution)/shard_map/ppermute | solution.py:23
  156.1 15.8 %collective-permute-start.18 = (bf16[2,256,128]{2,1,0:T(8,128)(2,1)S(1)}, bf16[2,256,128]{2,1,0:T(8,128)(2,1)S(1)}, u32[]{:S(2)}, u32[]{:S(2)}) collective-permute-start(bf16[2,256,128]{2,1,0:T(8,128)(2,1)S(1)} %get-tuple-element.25), channel_id=1, source_target_pairs={{0,48},{16,64},{32,80},{48,96},{64,112},{80,0},{96,16},{112,32},{1... | collective-permute-start | bytes 393224 | tf_op jit(solution)/shard_map/ppermute | solution.py:23
  158.5 15.6 %collective-permute-start.19 = (bf16[2,256,128]{2,1,0:T(8,128)(2,1)S(1)}, bf16[2,256,128]{2,1,0:T(8,128)(2,1)S(1)}, u32[]{:S(2)}, u32[]{:S(2)}) collective-permute-start(bf16[2,256,128]{2,1,0:T(8,128)(2,1)S(1)} %get-tuple-element.24), channel_id=1, source_target_pairs={{0,80},{16,96},{32,112},{48,0},{64,16},{80,32},{96,48},{112,64},{1... | collective-permute-start | bytes 393224 | tf_op jit(solution)/shard_map/ppermute | solution.py:23
  164.4 16.5 %collective-permute-start.20 = (bf16[2,256,128]{2,1,0:T(8,128)(2,1)S(1)}, bf16[2,256,128]{2,1,0:T(8,128)(2,1)S(1)}, u32[]{:S(2)}, u32[]{:S(2)}) collective-permute-start(bf16[2,256,128]{2,1,0:T(8,128)(2,1)S(1)} %get-tuple-element.23), channel_id=1, source_target_pairs={{0,32},{16,48},{32,64},{48,80},{64,96},{80,112},{96,0},{112,16},{1... | collective-permute-start | bytes 393224 | tf_op jit(solution)/shard_map/ppermute | solution.py:23
  166.4 21.2 %copy-start.9 = (bf16[2,256,128]{2,1,0:T(8,128)(2,1)}, bf16[2,256,128]{2,1,0:T(8,128)(2,1)S(1)}, u32[]{:S(2)}) copy-start(bf16[2,256,128]{2,1,0:T(8,128)(2,1)S(1)} %collective-permute-done.17.refs_0_) | copy-start | bytes 393220
  166.4 21.2 %collective-permute-start.21 = (bf16[2,256,128]{2,1,0:T(8,128)(2,1)S(1)}, bf16[2,256,128]{2,1,0:T(8,128)(2,1)S(1)}, u32[]{:S(2)}, u32[]{:S(2)}) collective-permute-start(bf16[2,256,128]{2,1,0:T(8,128)(2,1)S(1)} %get-tuple-element.22), channel_id=1, source_target_pairs={{0,96},{16,112},{32,0},{48,16},{64,32},{80,48},{96,64},{112,80},{1... | collective-permute-start | bytes 393224 | tf_op jit(solution)/shard_map/ppermute | solution.py:23
  171.9 15.7 %copy-start.10 = (bf16[2,256,128]{2,1,0:T(8,128)(2,1)}, bf16[2,256,128]{2,1,0:T(8,128)(2,1)S(1)}, u32[]{:S(2)}) copy-start(bf16[2,256,128]{2,1,0:T(8,128)(2,1)S(1)} %collective-permute-done.18.refs_1_) | copy-start | bytes 393220
  171.9 15.7 %collective-permute-start.22 = (bf16[2,256,128]{2,1,0:T(8,128)(2,1)S(1)}, bf16[2,256,128]{2,1,0:T(8,128)(2,1)S(1)}, u32[]{:S(2)}, u32[]{:S(2)}) collective-permute-start(bf16[2,256,128]{2,1,0:T(8,128)(2,1)S(1)} %get-tuple-element.21), channel_id=1, source_target_pairs={{0,16},{16,32},{32,48},{48,64},{64,80},{80,96},{96,112},{112,0},{1... | collective-permute-start | bytes 393224 | tf_op jit(solution)/shard_map/ppermute | solution.py:23
  174.1 13.5 %copy-start.11 = (bf16[2,256,128]{2,1,0:T(8,128)(2,1)}, bf16[2,256,128]{2,1,0:T(8,128)(2,1)S(1)}, u32[]{:S(2)}) copy-start(bf16[2,256,128]{2,1,0:T(8,128)(2,1)S(1)} %collective-permute-done.19.refs_2_) | copy-start | bytes 393220
  174.2 13.4 %collective-permute-start.23 = (bf16[2,256,128]{2,1,0:T(8,128)(2,1)S(1)}, bf16[2,256,128]{2,1,0:T(8,128)(2,1)S(1)}, u32[]{:S(2)}, u32[]{:S(2)}) collective-permute-start(bf16[2,256,128]{2,1,0:T(8,128)(2,1)S(1)} %get-tuple-element.20), channel_id=1, source_target_pairs={{0,112},{16,0},{32,16},{48,32},{64,48},{80,64},{96,80},{112,96},{1... | collective-permute-start | bytes 393224 | tf_op jit(solution)/shard_map/ppermute | solution.py:23
  180.9 6.7 %copy-start.12 = (bf16[2,256,128]{2,1,0:T(8,128)(2,1)}, bf16[2,256,128]{2,1,0:T(8,128)(2,1)S(1)}, u32[]{:S(2)}) copy-start(bf16[2,256,128]{2,1,0:T(8,128)(2,1)S(1)} %collective-permute-done.20.refs_3_) | copy-start | bytes 393220
  180.9 58.4 %collective-permute-start.28 = (f32[320]{0:T(512)S(1)}, f32[320]{0:T(512)S(1)}, u32[]{:S(2)}, u32[]{:S(2)}) collective-permute-start(f32[320]{0:T(512)S(1)} %pad_maximum_fusion.5), channel_id=1, source_target_pairs={{0,0},{1,8},{8,256},{9,264},{256,1},{257,9},{264,257},{265,265},{2... | collective-permute-start | bytes 3848 | tf_op jit(solution)/shard_map/ppermute | solution.py:46
  187.5 0.6 copy-start.13
  187.6 0.7 copy-start.14
  188.2 0.6 copy-start.15
  192.0 22.5 %collective-permute-start.26 = (f32[64,256]{1,0:T(8,128)S(1)}, f32[64,256]{1,0:T(8,128)S(1)}, u32[]{:S(2)}, u32[]{:S(2)}) collective-permute-start(f32[64,256]{1,0:T(8,128)S(1)} %get-tuple-element.30), channel_id=1, source_target_pairs={{0,384},{128,0},{256,128},{384,256},{1,385},{129,1},{257,129},{385... | collective-permute-start | bytes 196616 | tf_op jit(solution)/shard_map/ppermute | solution.py:23
  198.8 15.7 %collective-permute-start.25 = (f32[64,256]{1,0:T(8,128)S(1)}, f32[64,256]{1,0:T(8,128)S(1)}, u32[]{:S(2)}, u32[]{:S(2)}) collective-permute-start(f32[64,256]{1,0:T(8,128)S(1)} %get-tuple-element.31), channel_id=1, source_target_pairs={{0,128},{128,256},{256,384},{384,0},{1,129},{129,257},{257,385},{3... | collective-permute-start | bytes 196616 | tf_op jit(solution)/shard_map/ppermute | solution.py:23
  200.7 38.8 %copy-start.21 = (pred[4]{0:T(512)(128)(4,1)S(1)}, pred[4]{0:T(512)(128)(4,1)}, u32[]{:S(2)}) copy-start(pred[4]{0:T(512)(128)(4,1)} %iota_compare_fusion.2) | copy-start | bytes 16
  200.7 13.8 %collective-permute-start.24 = (f32[64,256]{1,0:T(8,128)S(1)}, f32[64,256]{1,0:T(8,128)S(1)}, u32[]{:S(2)}, u32[]{:S(2)}) collective-permute-start(f32[64,256]{1,0:T(8,128)S(1)} %get-tuple-element.29), channel_id=1, source_target_pairs={{0,256},{128,384},{256,0},{384,128},{1,257},{129,385},{257,1},{385... | collective-permute-start | bytes 196616 | tf_op jit(solution)/shard_map/ppermute | solution.py:23
  204.4 0.9 copy-start.1
  212.5 75.1 %collective-permute-start.14 = (bf16[8,128,256]{2,1,0:T(8,128)(2,1)}, bf16[8,128,256]{2,1,0:T(8,128)(2,1)S(1)}, u32[]{:S(2)}, u32[]{:S(2)}) collective-permute-start(bf16[8,128,256]{2,1,0:T(8,128)(2,1)} %get-tuple-element.9), channel_id=1, source_target_pairs={{0,1},{1,0},{2,3},{3,2},{4,5},{5,4},{6,7},{7,6},{8,9},{9,8},{10,11... | collective-permute-start | bytes 1572872 | tf_op jit(solution)/shard_map/ppermute | solution.py:27
  215.5 71.4 %collective-permute-start.27 = (f32[64,256]{1,0:T(8,128)S(1)}, f32[64,256]{1,0:T(8,128)S(1)}, u32[]{:S(2)}, u32[]{:S(2)}) collective-permute-start(f32[64,256]{1,0:T(8,128)S(1)} %get-tuple-element.17), channel_id=1, source_target_pairs={{0,0},{1,256},{8,1},{9,257},{256,8},{257,264},{264,9},{265,265},{2... | collective-permute-start | bytes 196616 | tf_op jit(solution)/shard_map/ppermute | solution.py:46
  286.8 2.9 %copy-start.17 = (f32[1,256]{1,0:T(1,128)}, f32[1,256]{1,0:T(1,128)S(1)}, u32[]{:S(2)}) copy-start(f32[1,256]{1,0:T(1,128)S(1)} %constant_dynamic-slice_fusion.1) | copy-start | bytes 3076
  286.9 2.9 copy-start.19

commit v5 on v4

--- a/solution.py
+++ b/solution.py
@@ -173,7 +173,7 @@
         def index(k, p):
             z = k ^ p[count + 1]
             y = place ^ p[count + 2]
-            return ((y & 1) * 8 + ((y >> 1) & 1) * 4 + ((y >> 2) & 1) * 2 + z, 0, 0)
+            return (z * 8 + (y & 1) * 4 + ((y >> 1) & 1) * 2 + ((y >> 2) & 1), 0, 0)
 
         return pl.BlockSpec((1, cols, twice), index)
 
@@ -233,14 +233,15 @@
     by_block = (len(blocks), tokens, heads)
     ctx = arrange(info, context.reshape(by_block), context_other.reshape(by_block))
 
-    slim = weight.T.astype(jnp.bfloat16)
-    w_a = turn(slim, lambda a, b: (b, a))
-    w_b = turn(slim, lambda a, b: (1 - b, a))
-    w = jnp.concatenate([w_a, w_b], axis=1)[None]
-    w = jnp.concatenate([w, flip(w, "za")], axis=0)
+    w = weight.T.astype(jnp.bfloat16)[None]
     for bit in (2, 1, 0):
         other = flip(w, "y", 1 << bit)
         w = jnp.concatenate([w, other], axis=0)
+    w_a = turn(w, lambda a, b: (b, a))
+    w_b = turn(w, lambda a, b: (1 - b, a))
+    w = jnp.concatenate([w_a, w_b], axis=2)
+    other = flip(w, "za")
+    w = jnp.concatenate([w, other], axis=0)
     w_came = flip(w, "c")
 
     stats = rotate(jnp.concatenate([row_stat, col_stat]), True)

time: 293 us -> 274 us (0.935)
  starting transfers between devices: 147 us -> 125 us
  blocking collectives: 60.5 us -> 65.1 us
  waiting for transfers between devices: 44.2 us -> 40.7 us
    ppermute x9, starting transfers between devices: 66 us -> 43.9 us  [flip(): return lax.ppermute(value, axis, [(i, i ^ mask) for i in range(SIZE[axis])])]
    ppermute x2, waiting for transfers between devices: 16.1 us -> 7.98 us  [turn(): return lax.ppermute(value, ('zb', 'zh'), pairs)]
    ppermute x2, starting transfers between devices: 14.4 us -> 9.62 us  [rotate(): return lax.ppermute(value, ('zb', 'c', 'zh'), pairs)]
    ppermute x16, starting transfers between devices: 62 us -> 65.7 us  [shift(): lax.ppermute(value, axes, [(i, (i + step) % size) for i in range(size)])]
  transfers between devices with their start and end apart: 29 -> 29, of which waited for: 6 -> 8; matrix products, arithmetic and copies ran while one was open for 3% -> 4% of each run, Pallas kernels for 6% -> 7%
where the time goes in v5:
time: 274 us; the launch traced here: 271 us
  starting transfers between devices  125 us (46%)
  blocking collectives  65.1 us (24%)
  waiting for transfers between devices  40.7 us (15%)
  Pallas kernels  18.6 us (7%)
  other arithmetic  9.85 us (4%)
  local copies, waits for them, and re-layouts  9.72 us (4%)
    ppermute x16, starting transfers between devices, shift(): lax.ppermute(value, axes, [(i, (i + step) % size) for i in range(size)])  65.7 us
    ppermute x9, starting transfers between devices, flip(): return lax.ppermute(value, axis, [(i, i ^ mask) for i in range(SIZE[axis])])  43.9 us
    ppermute x9, waiting for transfers between devices, flip(): return lax.ppermute(value, axis, [(i, i ^ mask) for i in range(SIZE[axis])])  17.4 us
    ppermute x16, waiting for transfers between devices, shift(): lax.ppermute(value, axes, [(i, (i + step) % size) for i in range(size)])  15.3 us
    psum x1, blocking collectives, per_device(): col_all = lax.psum(col_all, 'x')  15.2 us
    psum x1, blocking collectives, per_device(): rows = lax.psum(rows, 'y')  11 us
    psum x1, blocking collectives, per_device(): lax.psum(jnp.concatenate([rows, slot(col_here, zl, 4)]), ('zb', 'za'))  11 us
    psum x1, blocking collectives, per_device(): sums = lax.psum(jnp.concatenate([slot(row_here, c, 2), tail]), 'c')  11 us
  transfers between devices with their start and end apart: 29, of which 8 were waited for; matrix products, arithmetic and copies ran while one was open for 4% of the time, Pallas kernels for 7%

profile of v5, /device:TPU:1, one launch (start us, length us, event | category | flops | bytes accessed | tf_op | source)
XLA Modules:
  0.0 271.3 jit_solution(746059803476197571)
XLA Ops:
  0.6 0.7 iota_compare_fusion
  1.5 1.4 broadcast_select_fusion
  3.0 3.9 %collective-permute-start.7 = (bf16[128,2048]{1,0:T(8,128)(2,1)S(1)}, bf16[128,2048]{1,0:T(8,128)(2,1)S(1)}, u32[]{:S(2)}, u32[]{:S(2)}) collective-permute-start(bf16[128,2048]{1,0:T(8,128)(2,1)S(1)} %get-tuple-element.28.refs_16_.refs_0_), channel_id=1, source_target_pairs={{0,2},{2,4},{4,6},{6,0},{1,3},{3,5},{5,7},{7,1},{8,10},{10,12},{12... | collective-permute-start | bytes 1572872 | tf_op jit(solution)/shard_map/ppermute | solution.py:23
  6.9 10.6 %collective-permute-start.10 = (bf16[128,2048]{1,0:T(8,128)(2,1)S(1)}, bf16[128,2048]{1,0:T(8,128)(2,1)S(1)}, u32[]{:S(2)}, u32[]{:S(2)}) collective-permute-start(bf16[128,2048]{1,0:T(8,128)(2,1)S(1)} %get-tuple-element.27), channel_id=1, source_target_pairs={{0,1},{1,0},{2,3},{3,2},{4,5},{5,4},{6,7},{7,6},{8,9},{9,8},{10,11... | collective-permute-start | bytes 1572872 | tf_op jit(solution)/shard_map/ppermute | solution.py:27
  17.6 1.9 collective-permute-start.15
  19.5 7.5 %collective-permute-start = (bf16[1,64,256]{2,1,0:T(8,128)(2,1)S(1)}, bf16[1,64,256]{2,1,0:T(8,128)(2,1)S(1)}, u32[]{:S(2)}, u32[]{:S(2)}) collective-permute-start(bf16[1,64,256]{2,1,0:T(8,128)(2,1)S(1)} %convert_bitcast_fusion), channel_id=1, source_target_pairs={{0,64},{16,80},{32,96},{48,112},{64,0},{80,16},{96,32},{112,48},{1... | collective-permute-start | bytes 98312 | tf_op jit(solution)/shard_map/ppermute | solution.py:27
  27.0 1.6 collective-permute-done
  28.6 4.3 %collective-permute-start.1 = (bf16[2,64,256]{2,1,0:T(8,128)(2,1)S(1)}, bf16[2,64,256]{2,1,0:T(8,128)(2,1)S(1)}, u32[]{:S(2)}, u32[]{:S(2)}) collective-permute-start(bf16[2,64,256]{2,1,0:T(8,128)(2,1)S(1)} %pad_maximum_fusion.3), channel_id=1, source_target_pairs={{0,32},{16,48},{32,0},{48,16},{64,96},{80,112},{96,64},{112,80},{1... | collective-permute-start | bytes 196616 | tf_op jit(solution)/shard_map/ppermute | solution.py:27
  32.9 1.9 collective-permute-done.1
  34.9 2.9 %collective-permute-start.2 = (bf16[4,64,256]{2,1,0:T(8,128)(2,1)S(1)}, bf16[4,64,256]{2,1,0:T(8,128)(2,1)}, u32[]{:S(2)}, u32[]{:S(2)}) collective-permute-start(bf16[4,64,256]{2,1,0:T(8,128)(2,1)S(1)} %pad_maximum_fusion.2), channel_id=1, source_target_pairs={{0,16},{16,0},{32,48},{48,32},{64,80},{80,64},{96,112},{112,96},{1... | collective-permute-start | bytes 393224 | tf_op jit(solution)/shard_map/ppermute | solution.py:27
  37.8 3.4 %collective-permute-start.8 = (bf16[128,2048]{1,0:T(8,128)(2,1)S(1)}, bf16[128,2048]{1,0:T(8,128)(2,1)S(1)}, u32[]{:S(2)}, u32[]{:S(2)}) collective-permute-start(bf16[128,2048]{1,0:T(8,128)(2,1)S(1)} %get-tuple-element.28.refs_16_.refs_0_), channel_id=1, source_target_pairs={{0,6},{2,0},{4,2},{6,4},{1,7},{3,1},{5,3},{7,5},{8,14},{10,8},{12,... | collective-permute-start | bytes 1572872 | tf_op jit(solution)/shard_map/ppermute | solution.py:23
  41.2 4.0 %collective-permute-start.9 = (bf16[128,2048]{1,0:T(8,128)(2,1)S(1)}, bf16[128,2048]{1,0:T(8,128)(2,1)S(1)}, u32[]{:S(2)}, u32[]{:S(2)}) collective-permute-start(bf16[128,2048]{1,0:T(8,128)(2,1)S(1)} %get-tuple-element.28.refs_16_.refs_0_), channel_id=1, source_target_pairs={{0,4},{2,6},{4,0},{6,2},{1,5},{3,7},{5,1},{7,3},{8,12},{10,14},{12... | collective-permute-start | bytes 1572872 | tf_op jit(solution)/shard_map/ppermute | solution.py:23
  45.3 1.9 collective-permute-start.11
  47.2 4.6 %collective-permute-start.12 = (bf16[128,2048]{1,0:T(8,128)(2,1)S(1)}, bf16[128,2048]{1,0:T(8,128)(2,1)}, u32[]{:S(2)}, u32[]{:S(2)}) collective-permute-start(bf16[128,2048]{1,0:T(8,128)(2,1)S(1)} %collective-permute-done.10.refs_20_.refs_4_), channel_id=1, source_target_pairs={{0,6},{2,0},{4,2},{6,4},{1,7},{3,1},{5,3},{7,5},{8,14},{10,8},{12,... | collective-permute-start | bytes 1572872 | tf_op jit(solution)/shard_map/ppermute | solution.py:23
  51.8 0.8 copy-done.10
  52.6 1.9 collective-permute-start.13
  54.6 0.7 stack.55.info_ref
  55.3 0.9 pad_maximum_fusion.1
  56.2 3.2 %arrange.1.ctx_ref = bf16[512,1024]{1,0:T(8,128)(2,1)} custom-call(s32[13]{0:T(128)} %stack.55.info_ref, bf16[8,128,256]{2,1,0:T(8,128)(2,1)} %bitcast.63, bf16[8,128,256]{2,1,0:T(8,128)(2,1)} %bitcast.64), custom_call_target="tpu_custom_call" | custom-call | tf_op jit(solution)/shard_map/arrange/pallas_call | solution.py:128
  59.4 1.4 collective-permute-start.3
  60.8 12.1 %collective-permute-done.11.refs_21_.refs_5_ = bf16[128,2048]{1,0:T(8,128)(2,1)} collective-permute-done((bf16[128,2048]{1,0:T(8,128)(2,1)S(1)}, bf16[128,2048]{1,0:T(8,128)(2,1)}, u32[]{:S(2)}, u32[]{:S(2)}) %collective-permute-start.11) | collective-permute-done | bytes 524320 | tf_op jit(solution)/shard_map/ppermute | solution.py:23
  72.9 1.3 collective-permute-done.12.refs_22_.refs_6_
  74.2 1.6 collective-permute-done.13.refs_23_.refs_7_
  75.9 0.8 copy-done.9
  76.7 6.0 %grad.1 = (f32[8,2,256,128]{3,2,1,0:T(8,128)}, bf16[8,2,256,128]{3,2,1,0:T(8,128)(2,1)}) custom-call(bf16[512,1024]{1,0:T(8,128)(2,1)} %arrange.1.ctx_ref, bf16[128,2048]{1,0:T(8,128)(2,1)} %copy-done.3, bf16[128,2048]{1,0:T(8,128)(2,1)} %copy-done.5, bf16[128,2048]{1,0:T(8,128)(2,1)} %copy-done.7, bf16[128,2048]{1,0:T(8,128)(2,1)} %copy-done.8, ...), custom_call_target="tpu_custom_call" | custom-call | flops 2147483648 | bytes 9437184 | tf_op jit(solution)/shard_map/grad/pallas_call | solution.py:147
  82.7 7.5 %collective-permute-start.16 = (bf16[8,2,256,128]{3,2,1,0:T(8,128)(2,1)}, bf16[8,2,256,128]{3,2,1,0:T(8,128)(2,1)S(1)}, u32[]{:S(2)}, u32[]{:S(2)}) collective-permute-start(bf16[8,2,256,128]{3,2,1,0:T(8,128)(2,1)} %get-tuple-element.11), channel_id=1, source_target_pairs={{0,8},{8,0},{1,9},{9,1},{2,10},{10,2},{3,11},{11,3},{4,12},{12,4},... | collective-permute-start | bytes 3145736 | tf_op jit(solution)/shard_map/ppermute | solution.py:27
  90.2 4.7 %collective-permute-start.4 = (bf16[8,64,256]{2,1,0:T(8,128)(2,1)S(1)}, bf16[8,64,256]{2,1,0:T(8,128)(2,1)S(1)}, u32[]{:S(2)}, u32[]{:S(2)}) collective-permute-start(bf16[8,64,256]{2,1,0:T(8,128)(2,1)S(1)} %pad_maximum_fusion.1), channel_id=1, source_target_pairs={{0,256},{1,0},{256,257},{257,1},{2,258},{3,2},{258,259},{259,3},{4... | collective-permute-start | bytes 786440 | tf_op jit(solution)/shard_map/ppermute | solution.py:36
  94.9 1.0 constant_dynamic-update-slice_fusion.1
  95.9 8.0 %collective-permute-done.4 = bf16[8,64,256]{2,1,0:T(8,128)(2,1)S(1)} collective-permute-done((bf16[8,64,256]{2,1,0:T(8,128)(2,1)S(1)}, bf16[8,64,256]{2,1,0:T(8,128)(2,1)S(1)}, u32[]{:S(2)}, u32[]{:S(2)}) %collective-permute-start.4) | collective-permute-done | bytes 262176 | tf_op jit(solution)/shard_map/ppermute | solution.py:36
  103.9 4.8 %collective-permute-start.5 = (bf16[8,64,512]{2,1,0:T(8,128)(2,1)S(1)}, bf16[8,64,512]{2,1,0:T(8,128)(2,1)S(1)}, u32[]{:S(2)}, u32[]{:S(2)}) collective-permute-start(bf16[8,64,512]{2,1,0:T(8,128)(2,1)S(1)} %constant_dynamic-update-slice_fusion), channel_id=1, source_target_pairs={{0,128},{128,0},{1,129},{129,1},{2,130},{130,2},{3,131},{131,3},{4... | collective-permute-start | bytes 1572872 | tf_op jit(solution)/shard_map/ppermute | solution.py:27
  108.7 13.9 %collective-permute-done.5 = bf16[8,64,512]{2,1,0:T(8,128)(2,1)S(1)} collective-permute-done((bf16[8,64,512]{2,1,0:T(8,128)(2,1)S(1)}, bf16[8,64,512]{2,1,0:T(8,128)(2,1)S(1)}, u32[]{:S(2)}, u32[]{:S(2)}) %collective-permute-start.5) | collective-permute-done | bytes 524320 | tf_op jit(solution)/shard_map/ppermute | solution.py:27
  122.7 2.4 collective-permute-start.6
  125.2 1.7 fusion.6
  126.9 8.1 %collective-permute-start.17 = (bf16[2,256,128]{2,1,0:T(8,128)(2,1)S(1)}, bf16[2,256,128]{2,1,0:T(8,128)(2,1)S(1)}, u32[]{:S(2)}, u32[]{:S(2)}) collective-permute-start(bf16[2,256,128]{2,1,0:T(8,128)(2,1)S(1)} %get-tuple-element.26), channel_id=1, source_target_pairs={{0,64},{16,80},{32,96},{48,112},{64,0},{80,16},{96,32},{112,48},{1... | collective-permute-start | bytes 393224 | tf_op jit(solution)/shard_map/ppermute | solution.py:23
  135.1 2.6 collective-permute-start.18
  137.7 8.1 %collective-permute-start.19 = (bf16[2,256,128]{2,1,0:T(8,128)(2,1)S(1)}, bf16[2,256,128]{2,1,0:T(8,128)(2,1)S(1)}, u32[]{:S(2)}, u32[]{:S(2)}) collective-permute-start(bf16[2,256,128]{2,1,0:T(8,128)(2,1)S(1)} %get-tuple-element.24), channel_id=1, source_target_pairs={{0,80},{16,96},{32,112},{48,0},{64,16},{80,32},{96,48},{112,64},{1... | collective-permute-start | bytes 393224 | tf_op jit(solution)/shard_map/ppermute | solution.py:23
  145.8 3.1 %collective-permute-start.20 = (bf16[2,256,128]{2,1,0:T(8,128)(2,1)S(1)}, bf16[2,256,128]{2,1,0:T(8,128)(2,1)S(1)}, u32[]{:S(2)}, u32[]{:S(2)}) collective-permute-start(bf16[2,256,128]{2,1,0:T(8,128)(2,1)S(1)} %get-tuple-element.23), channel_id=1, source_target_pairs={{0,32},{16,48},{32,64},{48,80},{64,96},{80,112},{96,0},{112,16},{1... | collective-permute-start | bytes 393224 | tf_op jit(solution)/shard_map/ppermute | solution.py:23
  148.9 4.3 %collective-permute-start.21 = (bf16[2,256,128]{2,1,0:T(8,128)(2,1)S(1)}, bf16[2,256,128]{2,1,0:T(8,128)(2,1)S(1)}, u32[]{:S(2)}, u32[]{:S(2)}) collective-permute-start(bf16[2,256,128]{2,1,0:T(8,128)(2,1)S(1)} %get-tuple-element.22), channel_id=1, source_target_pairs={{0,96},{16,112},{32,0},{48,16},{64,32},{80,48},{96,64},{112,80},{1... | collective-permute-start | bytes 393224 | tf_op jit(solution)/shard_map/ppermute | solution.py:23
  153.5 1.9 collective-permute-start.22
  155.5 4.5 %collective-permute-start.23 = (bf16[2,256,128]{2,1,0:T(8,128)(2,1)S(1)}, bf16[2,256,128]{2,1,0:T(8,128)(2,1)S(1)}, u32[]{:S(2)}, u32[]{:S(2)}) collective-permute-start(bf16[2,256,128]{2,1,0:T(8,128)(2,1)S(1)} %get-tuple-element.20), channel_id=1, source_target_pairs={{0,112},{16,0},{32,16},{48,32},{64,48},{80,64},{96,80},{112,96},{1... | collective-permute-start | bytes 393224 | tf_op jit(solution)/shard_map/ppermute | solution.py:23
  160.0 1.7 dynamic-slice_bitcast_fusion.mine_ref
  161.7 4.7 %collective-permute-start.28 = (f32[320]{0:T(512)S(1)}, f32[320]{0:T(512)S(1)}, u32[]{:S(2)}, u32[]{:S(2)}) collective-permute-start(f32[320]{0:T(512)S(1)} %pad_maximum_fusion.6), channel_id=1, source_target_pairs={{0,0},{1,8},{8,256},{9,264},{256,1},{257,9},{264,257},{265,265},{2... | collective-permute-start | bytes 3848 | tf_op jit(solution)/shard_map/ppermute | solution.py:46
  167.2 0.6 copy-done.17
  167.8 2.2 total.1
  170.0 0.9 dynamic-slice_bitcast_fusion.10
  170.9 8.1 %collective-permute-start.26 = (f32[64,256]{1,0:T(8,128)S(1)}, f32[64,256]{1,0:T(8,128)S(1)}, u32[]{:S(2)}, u32[]{:S(2)}) collective-permute-start(f32[64,256]{1,0:T(8,128)S(1)} %get-tuple-element.30), channel_id=1, source_target_pairs={{0,384},{128,0},{256,128},{384,256},{1,385},{129,1},{257,129},{385... | collective-permute-start | bytes 196616 | tf_op jit(solution)/shard_map/ppermute | solution.py:23
  179.0 1.9 collective-permute-start.25
  180.9 3.3 %collective-permute-start.24 = (f32[64,256]{1,0:T(8,128)S(1)}, f32[64,256]{1,0:T(8,128)S(1)}, u32[]{:S(2)}, u32[]{:S(2)}) collective-permute-start(f32[64,256]{1,0:T(8,128)S(1)} %get-tuple-element.29), channel_id=1, source_target_pairs={{0,256},{128,384},{256,0},{384,128},{1,257},{129,385},{257,1},{385... | collective-permute-start | bytes 196616 | tf_op jit(solution)/shard_map/ppermute | solution.py:23
  184.2 0.9 copy-done.1
  185.2 7.2 %back.1 = (f32[8,128,256]{2,1,0:T(8,128)}, bf16[8,128,256]{2,1,0:T(8,128)(2,1)}) custom-call(s32[13]{0:T(128)} %stack.55.info_ref, bf16[16,64,512]{2,1,0:T(8,128)(2,1)} %copy-done, bf16[16,64,512]{2,1,0:T(8,128)(2,1)} %copy-done, bf16[16,64,512]{2,1,0:T(8,128)(2,1)} %copy-done, bf16[16,64,512]{2,1,0:T(8,128)(2,1)} %copy-done, bf16[16,64,512]{2,1,0:T(8,128)(2,1)} %copy-done, ...), custom_call_target="tpu_custom_call" | custom-call | flops 2147483648 | bytes 8388608 | tf_op jit(solution)/shard_map/back/pallas_call | solution.py:180
  192.4 1.9 collective-permute-start.14
  194.3 1.0 add_reduce_fusion
  195.3 4.9 %collective-permute-start.27 = (f32[64,256]{1,0:T(8,128)S(1)}, f32[64,256]{1,0:T(8,128)S(1)}, u32[]{:S(2)}, u32[]{:S(2)}) collective-permute-start(f32[64,256]{1,0:T(8,128)S(1)} %get-tuple-element.17), channel_id=1, source_target_pairs={{0,0},{1,256},{8,1},{9,257},{256,8},{257,264},{264,9},{265,265},{2... | collective-permute-start | bytes 196616 | tf_op jit(solution)/shard_map/ppermute | solution.py:46
  200.2 2.5 psum.49
  202.7 15.2 %psum.50 = f32[64]{0:T(128)S(1)} all-reduce(f32[64]{0:T(128)S(1)} %psum.49), channel_id=1, replica_groups=mesh['zb'=2,'za'=2,'y'=8,'c'=2,'x'=4,'zh'=2] {'x'}, use_global_device_ids=true, to_apply=%region_3.4 | all-reduce | flops 64 | bytes 512 | tf_op jit(solution)/shard_map/psum | solution.py:271
  218.2 11.0 %psum.51 = f32[512]{0:T(512)S(1)} all-reduce(f32[512]{0:T(512)S(1)} %pad_maximum_fusion.7), channel_id=1, replica_groups=mesh['zb'=2,'za'=2,'y'=8,'c'=2,'x'=4,'zh'=2] {'y'}, use_global_device_ids=true, to_apply=%region_5.6 | all-reduce | flops 512 | bytes 4096 | tf_op jit(solution)/shard_map/psum | solution.py:275
  229.2 11.0 %psum.52 = f32[768]{0:T(1024)S(1)} all-reduce(f32[768]{0:T(1024)S(1)} %pad_maximum_fusion.4), channel_id=1, replica_groups=mesh['zb'=2,'za'=2,'y'=8,'c'=2,'x'=4,'zh'=2] {'zb','za'}, use_global_device_ids=true, to_apply=%region_6.7 | all-reduce | flops 768 | bytes 6144 | tf_op jit(solution)/shard_map/psum | solution.py:276
  240.3 7.7 %psum.53 = f32[1024]{0:T(1024)S(1)} all-reduce(f32[1024]{0:T(1024)S(1)} %pad_maximum_fusion.5), channel_id=1, replica_groups=mesh['zb'=2,'za'=2,'y'=8,'c'=2,'x'=4,'zh'=2] {'zh'}, use_global_device_ids=true, to_apply=%region_7.8 | all-reduce | flops 1024 | bytes 8192 | tf_op jit(solution)/shard_map/psum | solution.py:278
  248.0 0.6 fusion.3
  248.7 0.6 concatenate.41
  249.4 11.0 %psum.54 = f32[640]{0:T(1024)S(1)} all-reduce(f32[640]{0:T(1024)S(1)} %concatenate.41), channel_id=1, replica_groups=mesh['zb'=2,'za'=2,'y'=8,'c'=2,'x'=4,'zh'=2] {'c'}, use_global_device_ids=true, to_apply=%region_9.10 | all-reduce | flops 640 | bytes 5120 | tf_op jit(solution)/shard_map/psum | solution.py:284
  260.9 6.7 %psum.55 = f32[]{:T(128)} all-reduce(f32[]{:T(128)} %bitcast.33), channel_id=1, replica_groups=mesh['zb'=2,'za'=2,'y'=8,'c'=2,'x'=4,'zh'=2] {'x'}, use_global_device_ids=true, to_apply=%region_10.11 | all-reduce | flops 1 | bytes 8 | tf_op jit(solution)/shard_map/psum | solution.py:286
  268.4 0.7 divide_bitcast_fusion
  269.1 2.2 add_convert_fusion
  (96 shorter events, 2.5 us)
Async XLA Ops:
  1.5 16.1 %copy-start.4 = (bf16[1024,256]{1,0:T(8,128)(2,1)S(1)}, bf16[1024,256]{1,0:T(8,128)(2,1)}, u32[]{:S(2)}) copy-start(bf16[1024,256]{1,0:T(8,128)(2,1)} %param.6) | copy-start | bytes 1572868
  1.5 18.1 %copy-start.18 = (f32[256,64]{0,1:T(8,128)S(1)}, f32[256,64]{0,1:T(8,128)}, u32[]{:S(2)}) copy-start(f32[256,64]{0,1:T(8,128)} %param.9) | copy-start | bytes 196612
  3.0 72.9 %copy-start.3 = (bf16[128,2048]{1,0:T(8,128)(2,1)}, bf16[128,2048]{1,0:T(8,128)(2,1)S(1)}, u32[]{:S(2)}) copy-start(bf16[128,2048]{1,0:T(8,128)(2,1)S(1)} %get-tuple-element.28.refs_16_.refs_0_) | copy-start | bytes 1572868
  3.0 44.2 %collective-permute-start.7 = (bf16[128,2048]{1,0:T(8,128)(2,1)S(1)}, bf16[128,2048]{1,0:T(8,128)(2,1)S(1)}, u32[]{:S(2)}, u32[]{:S(2)}) collective-permute-start(bf16[128,2048]{1,0:T(8,128)(2,1)S(1)} %get-tuple-element.28.refs_16_.refs_0_), channel_id=1, source_target_pairs={{0,2},{2,4},{4,6},{6,0},{1,3},{3,5},{5,7},{7,1},{8,10},{10,12},{12... | collective-permute-start | bytes 1572872 | tf_op jit(solution)/shard_map/ppermute | solution.py:23
  6.9 38.3 %collective-permute-start.10 = (bf16[128,2048]{1,0:T(8,128)(2,1)S(1)}, bf16[128,2048]{1,0:T(8,128)(2,1)S(1)}, u32[]{:S(2)}, u32[]{:S(2)}) collective-permute-start(bf16[128,2048]{1,0:T(8,128)(2,1)S(1)} %get-tuple-element.27), channel_id=1, source_target_pairs={{0,1},{1,0},{2,3},{3,2},{4,5},{5,4},{6,7},{7,6},{8,9},{9,8},{10,11... | collective-permute-start | bytes 1572872 | tf_op jit(solution)/shard_map/ppermute | solution.py:27
  17.6 34.2 %collective-permute-start.15 = (bf16[1024,256]{1,0:T(8,128)(2,1)S(1)}, bf16[1024,256]{1,0:T(8,128)(2,1)S(1)}, u32[]{:S(2)}, u32[]{:S(2)}) collective-permute-start(bf16[1024,256]{1,0:T(8,128)(2,1)S(1)} %copy-done.4), channel_id=1, source_target_pairs={{0,1},{1,0},{2,3},{3,2},{4,5},{5,4},{6,7},{7,6},{8,9},{9,8},{10,11... | collective-permute-start | bytes 1572872 | tf_op jit(solution)/shard_map/ppermute | solution.py:27
  19.5 9.0 %collective-permute-start = (bf16[1,64,256]{2,1,0:T(8,128)(2,1)S(1)}, bf16[1,64,256]{2,1,0:T(8,128)(2,1)S(1)}, u32[]{:S(2)}, u32[]{:S(2)}) collective-permute-start(bf16[1,64,256]{2,1,0:T(8,128)(2,1)S(1)} %convert_bitcast_fusion), channel_id=1, source_target_pairs={{0,64},{16,80},{32,96},{48,112},{64,0},{80,16},{96,32},{112,48},{1... | collective-permute-start | bytes 98312 | tf_op jit(solution)/shard_map/ppermute | solution.py:27
  28.6 6.3 %collective-permute-start.1 = (bf16[2,64,256]{2,1,0:T(8,128)(2,1)S(1)}, bf16[2,64,256]{2,1,0:T(8,128)(2,1)S(1)}, u32[]{:S(2)}, u32[]{:S(2)}) collective-permute-start(bf16[2,64,256]{2,1,0:T(8,128)(2,1)S(1)} %pad_maximum_fusion.3), channel_id=1, source_target_pairs={{0,32},{16,48},{32,0},{48,16},{64,96},{80,112},{96,64},{112,80},{1... | collective-permute-start | bytes 196616 | tf_op jit(solution)/shard_map/ppermute | solution.py:27
  34.9 6.3 %collective-permute-start.2 = (bf16[4,64,256]{2,1,0:T(8,128)(2,1)S(1)}, bf16[4,64,256]{2,1,0:T(8,128)(2,1)}, u32[]{:S(2)}, u32[]{:S(2)}) collective-permute-start(bf16[4,64,256]{2,1,0:T(8,128)(2,1)S(1)} %pad_maximum_fusion.2), channel_id=1, source_target_pairs={{0,16},{16,0},{32,48},{48,32},{64,80},{80,64},{96,112},{112,96},{1... | collective-permute-start | bytes 393224 | tf_op jit(solution)/shard_map/ppermute | solution.py:27
  37.8 21.6 %collective-permute-start.8 = (bf16[128,2048]{1,0:T(8,128)(2,1)S(1)}, bf16[128,2048]{1,0:T(8,128)(2,1)S(1)}, u32[]{:S(2)}, u32[]{:S(2)}) collective-permute-start(bf16[128,2048]{1,0:T(8,128)(2,1)S(1)} %get-tuple-element.28.refs_16_.refs_0_), channel_id=1, source_target_pairs={{0,6},{2,0},{4,2},{6,4},{1,7},{3,1},{5,3},{7,5},{8,14},{10,8},{12,... | collective-permute-start | bytes 1572872 | tf_op jit(solution)/shard_map/ppermute | solution.py:23
  41.2 19.6 %collective-permute-start.9 = (bf16[128,2048]{1,0:T(8,128)(2,1)S(1)}, bf16[128,2048]{1,0:T(8,128)(2,1)S(1)}, u32[]{:S(2)}, u32[]{:S(2)}) collective-permute-start(bf16[128,2048]{1,0:T(8,128)(2,1)S(1)} %get-tuple-element.28.refs_16_.refs_0_), channel_id=1, source_target_pairs={{0,4},{2,6},{4,0},{6,2},{1,5},{3,7},{5,1},{7,3},{8,12},{10,14},{12... | collective-permute-start | bytes 1572872 | tf_op jit(solution)/shard_map/ppermute | solution.py:23
  45.3 30.6 %copy-start.6 = (bf16[128,2048]{1,0:T(8,128)(2,1)}, bf16[128,2048]{1,0:T(8,128)(2,1)S(1)}, u32[]{:S(2)}) copy-start(bf16[128,2048]{1,0:T(8,128)(2,1)S(1)} %collective-permute-done.10.refs_20_.refs_4_) | copy-start | bytes 1572868
  45.3 27.6 %collective-permute-start.11 = (bf16[128,2048]{1,0:T(8,128)(2,1)S(1)}, bf16[128,2048]{1,0:T(8,128)(2,1)}, u32[]{:S(2)}, u32[]{:S(2)}) collective-permute-start(bf16[128,2048]{1,0:T(8,128)(2,1)S(1)} %collective-permute-done.10.refs_20_.refs_4_), channel_id=1, source_target_pairs={{0,2},{2,4},{4,6},{6,0},{1,3},{3,5},{5,7},{7,1},{8,10},{10,12},{12... | collective-permute-start | bytes 1572872 | tf_op jit(solution)/shard_map/ppermute | solution.py:23
  47.2 28.6 %copy-start.5 = (bf16[128,2048]{1,0:T(8,128)(2,1)}, bf16[128,2048]{1,0:T(8,128)(2,1)S(1)}, u32[]{:S(2)}) copy-start(bf16[128,2048]{1,0:T(8,128)(2,1)S(1)} %collective-permute-done.7.refs_17_.refs_1_) | copy-start | bytes 1572868
  47.2 27.0 %collective-permute-start.12 = (bf16[128,2048]{1,0:T(8,128)(2,1)S(1)}, bf16[128,2048]{1,0:T(8,128)(2,1)}, u32[]{:S(2)}, u32[]{:S(2)}) collective-permute-start(bf16[128,2048]{1,0:T(8,128)(2,1)S(1)} %collective-permute-done.10.refs_20_.refs_4_), channel_id=1, source_target_pairs={{0,6},{2,0},{4,2},{6,4},{1,7},{3,1},{5,3},{7,5},{8,14},{10,8},{12,... | collective-permute-start | bytes 1572872 | tf_op jit(solution)/shard_map/ppermute | solution.py:23
  51.8 0.8 copy-start.10
  52.6 23.2 %collective-permute-start.13 = (bf16[128,2048]{1,0:T(8,128)(2,1)S(1)}, bf16[128,2048]{1,0:T(8,128)(2,1)S(1)}, u32[]{:S(2)}, u32[]{:S(2)}) collective-permute-start(bf16[128,2048]{1,0:T(8,128)(2,1)S(1)} %collective-permute-done.10.refs_20_.refs_4_), channel_id=1, source_target_pairs={{0,4},{2,6},{4,0},{6,2},{1,5},{3,7},{5,1},{7,3},{8,12},{10,14},{12... | collective-permute-start | bytes 1572872 | tf_op jit(solution)/shard_map/ppermute | solution.py:23
  59.4 16.4 %copy-start.7 = (bf16[128,2048]{1,0:T(8,128)(2,1)}, bf16[128,2048]{1,0:T(8,128)(2,1)S(1)}, u32[]{:S(2)}) copy-start(bf16[128,2048]{1,0:T(8,128)(2,1)S(1)} %collective-permute-done.8.refs_18_.refs_2_) | copy-start | bytes 1572868
  59.4 35.5 %collective-permute-start.3 = (bf16[8,64,256]{2,1,0:T(8,128)(2,1)S(1)}, bf16[8,64,256]{2,1,0:T(8,128)(2,1)}, u32[]{:S(2)}, u32[]{:S(2)}) collective-permute-start(bf16[8,64,256]{2,1,0:T(8,128)(2,1)S(1)} %pad_maximum_fusion.1), channel_id=1, source_target_pairs={{0,0},{1,256},{256,1},{257,257},{2,2},{3,258},{258,3},{259,259},{4... | collective-permute-start | bytes 786440 | tf_op jit(solution)/shard_map/ppermute | solution.py:36
  60.8 15.1 %copy-start.8 = (bf16[128,2048]{1,0:T(8,128)(2,1)}, bf16[128,2048]{1,0:T(8,128)(2,1)S(1)}, u32[]{:S(2)}) copy-start(bf16[128,2048]{1,0:T(8,128)(2,1)S(1)} %collective-permute-done.9.refs_19_.refs_3_) | copy-start | bytes 1572868
  75.9 0.8 copy-start.9
  82.7 42.4 %collective-permute-start.16 = (bf16[8,2,256,128]{3,2,1,0:T(8,128)(2,1)}, bf16[8,2,256,128]{3,2,1,0:T(8,128)(2,1)S(1)}, u32[]{:S(2)}, u32[]{:S(2)}) collective-permute-start(bf16[8,2,256,128]{3,2,1,0:T(8,128)(2,1)} %get-tuple-element.11), channel_id=1, source_target_pairs={{0,8},{8,0},{1,9},{9,1},{2,10},{10,2},{3,11},{11,3},{4,12},{12,4},... | collective-permute-start | bytes 3145736 | tf_op jit(solution)/shard_map/ppermute | solution.py:27
  90.2 13.7 %collective-permute-start.4 = (bf16[8,64,256]{2,1,0:T(8,128)(2,1)S(1)}, bf16[8,64,256]{2,1,0:T(8,128)(2,1)S(1)}, u32[]{:S(2)}, u32[]{:S(2)}) collective-permute-start(bf16[8,64,256]{2,1,0:T(8,128)(2,1)S(1)} %pad_maximum_fusion.1), channel_id=1, source_target_pairs={{0,256},{1,0},{256,257},{257,1},{2,258},{3,2},{258,259},{259,3},{4... | collective-permute-start | bytes 786440 | tf_op jit(solution)/shard_map/ppermute | solution.py:36
  103.9 18.7 %collective-permute-start.5 = (bf16[8,64,512]{2,1,0:T(8,128)(2,1)S(1)}, bf16[8,64,512]{2,1,0:T(8,128)(2,1)S(1)}, u32[]{:S(2)}, u32[]{:S(2)}) collective-permute-start(bf16[8,64,512]{2,1,0:T(8,128)(2,1)S(1)} %constant_dynamic-update-slice_fusion), channel_id=1, source_target_pairs={{0,128},{128,0},{1,129},{129,1},{2,130},{130,2},{3,131},{131,3},{4... | collective-permute-start | bytes 1572872 | tf_op jit(solution)/shard_map/ppermute | solution.py:27
  108.7 16.4 %copy-start.2 = (f32[8,2,256,128]{3,2,1,0:T(8,128)S(1)}, f32[8,2,256,128]{3,2,1,0:T(8,128)}, u32[]{:S(2)}) copy-start(f32[8,2,256,128]{3,2,1,0:T(8,128)} %get-tuple-element.10) | copy-start | bytes 6291460
  122.7 4.2 %copy-start = (bf16[16,64,512]{2,1,0:T(8,128)(2,1)}, bf16[16,64,512]{2,1,0:T(8,128)(2,1)S(1)}, u32[]{:S(2)}) copy-start(bf16[16,64,512]{2,1,0:T(8,128)(2,1)S(1)} %pad_maximum_fusion.refs_0_.refs_1_.refs_2_.refs_3_.refs_4_.refs_5_.refs_6_.refs_7_) | copy-start | bytes 3145732
  122.7 61.5 %collective-permute-start.6 = (bf16[16,64,512]{2,1,0:T(8,128)(2,1)S(1)}, bf16[16,64,512]{2,1,0:T(8,128)(2,1)S(1)}, u32[]{:S(2)}, u32[]{:S(2)}) collective-permute-start(bf16[16,64,512]{2,1,0:T(8,128)(2,1)S(1)} %pad_maximum_fusion.refs_0_.refs_1_.refs_2_.refs_3_.refs_4_.refs_5_.refs_6_.refs_7_), channel_id=1, source_target_pairs={{0,8},{8,0},{1,9},{9,1},{2,10},{10,2},{3,11},{11,3},{4,12},{12,4},... | collective-permute-start | bytes 3145736 | tf_op jit(solution)/shard_map/ppermute | solution.py:27
  125.1 20.6 %copy-start.20 = (f32[256]{0:T(256)S(1)}, f32[256]{0:T(256)}, u32[]{:S(2)}) copy-start(f32[256]{0:T(256)} %param.10) | copy-start | bytes 3076
  125.1 20.6 %copy-start.22 = (f32[64]{0:T(128)S(1)}, f32[64]{0:T(128)}, u32[]{:S(2)}) copy-start(f32[64]{0:T(128)} %param.11) | copy-start | bytes 772
  126.9 22.0 %collective-permute-start.17 = (bf16[2,256,128]{2,1,0:T(8,128)(2,1)S(1)}, bf16[2,256,128]{2,1,0:T(8,128)(2,1)S(1)}, u32[]{:S(2)}, u32[]{:S(2)}) collective-permute-start(bf16[2,256,128]{2,1,0:T(8,128)(2,1)S(1)} %get-tuple-element.26), channel_id=1, source_target_pairs={{0,64},{16,80},{32,96},{48,112},{64,0},{80,16},{96,32},{112,48},{1... | collective-permute-start | bytes 393224 | tf_op jit(solution)/shard_map/ppermute | solution.py:23
  135.1 18.4 %collective-permute-start.18 = (bf16[2,256,128]{2,1,0:T(8,128)(2,1)S(1)}, bf16[2,256,128]{2,1,0:T(8,128)(2,1)S(1)}, u32[]{:S(2)}, u32[]{:S(2)}) collective-permute-start(bf16[2,256,128]{2,1,0:T(8,128)(2,1)S(1)} %get-tuple-element.25), channel_id=1, source_target_pairs={{0,48},{16,64},{32,80},{48,96},{64,112},{80,0},{96,16},{112,32},{1... | collective-permute-start | bytes 393224 | tf_op jit(solution)/shard_map/ppermute | solution.py:23
  137.7 17.8 %collective-permute-start.19 = (bf16[2,256,128]{2,1,0:T(8,128)(2,1)S(1)}, bf16[2,256,128]{2,1,0:T(8,128)(2,1)S(1)}, u32[]{:S(2)}, u32[]{:S(2)}) collective-permute-start(bf16[2,256,128]{2,1,0:T(8,128)(2,1)S(1)} %get-tuple-element.24), channel_id=1, source_target_pairs={{0,80},{16,96},{32,112},{48,0},{64,16},{80,32},{96,48},{112,64},{1... | collective-permute-start | bytes 393224 | tf_op jit(solution)/shard_map/ppermute | solution.py:23
  145.8 15.9 %collective-permute-start.20 = (bf16[2,256,128]{2,1,0:T(8,128)(2,1)S(1)}, bf16[2,256,128]{2,1,0:T(8,128)(2,1)S(1)}, u32[]{:S(2)}, u32[]{:S(2)}) collective-permute-start(bf16[2,256,128]{2,1,0:T(8,128)(2,1)S(1)} %get-tuple-element.23), channel_id=1, source_target_pairs={{0,32},{16,48},{32,64},{48,80},{64,96},{80,112},{96,0},{112,16},{1... | collective-permute-start | bytes 393224 | tf_op jit(solution)/shard_map/ppermute | solution.py:23
  148.9 17.6 %copy-start.11 = (bf16[2,256,128]{2,1,0:T(8,128)(2,1)}, bf16[2,256,128]{2,1,0:T(8,128)(2,1)S(1)}, u32[]{:S(2)}) copy-start(bf16[2,256,128]{2,1,0:T(8,128)(2,1)S(1)} %collective-permute-done.17.refs_0_) | copy-start | bytes 393220
  148.9 17.5 %collective-permute-start.21 = (bf16[2,256,128]{2,1,0:T(8,128)(2,1)S(1)}, bf16[2,256,128]{2,1,0:T(8,128)(2,1)S(1)}, u32[]{:S(2)}, u32[]{:S(2)}) collective-permute-start(bf16[2,256,128]{2,1,0:T(8,128)(2,1)S(1)} %get-tuple-element.22), channel_id=1, source_target_pairs={{0,96},{16,112},{32,0},{48,16},{64,32},{80,48},{96,64},{112,80},{1... | collective-permute-start | bytes 393224 | tf_op jit(solution)/shard_map/ppermute | solution.py:23
  153.5 13.0 %copy-start.12 = (bf16[2,256,128]{2,1,0:T(8,128)(2,1)}, bf16[2,256,128]{2,1,0:T(8,128)(2,1)S(1)}, u32[]{:S(2)}) copy-start(bf16[2,256,128]{2,1,0:T(8,128)(2,1)S(1)} %collective-permute-done.18.refs_1_) | copy-start | bytes 393220
  153.5 12.9 %collective-permute-start.22 = (bf16[2,256,128]{2,1,0:T(8,128)(2,1)S(1)}, bf16[2,256,128]{2,1,0:T(8,128)(2,1)S(1)}, u32[]{:S(2)}, u32[]{:S(2)}) collective-permute-start(bf16[2,256,128]{2,1,0:T(8,128)(2,1)S(1)} %get-tuple-element.21), channel_id=1, source_target_pairs={{0,16},{16,32},{32,48},{48,64},{64,80},{80,96},{96,112},{112,0},{1... | collective-permute-start | bytes 393224 | tf_op jit(solution)/shard_map/ppermute | solution.py:23
  155.5 11.0 %copy-start.13 = (bf16[2,256,128]{2,1,0:T(8,128)(2,1)}, bf16[2,256,128]{2,1,0:T(8,128)(2,1)S(1)}, u32[]{:S(2)}) copy-start(bf16[2,256,128]{2,1,0:T(8,128)(2,1)S(1)} %collective-permute-done.19.refs_2_) | copy-start | bytes 393220
  155.5 11.0 %collective-permute-start.23 = (bf16[2,256,128]{2,1,0:T(8,128)(2,1)S(1)}, bf16[2,256,128]{2,1,0:T(8,128)(2,1)S(1)}, u32[]{:S(2)}, u32[]{:S(2)}) collective-permute-start(bf16[2,256,128]{2,1,0:T(8,128)(2,1)S(1)} %get-tuple-element.20), channel_id=1, source_target_pairs={{0,112},{16,0},{32,16},{48,32},{64,48},{80,64},{96,80},{112,96},{1... | collective-permute-start | bytes 393224 | tf_op jit(solution)/shard_map/ppermute | solution.py:23
  161.7 4.8 %copy-start.14 = (bf16[2,256,128]{2,1,0:T(8,128)(2,1)}, bf16[2,256,128]{2,1,0:T(8,128)(2,1)S(1)}, u32[]{:S(2)}) copy-start(bf16[2,256,128]{2,1,0:T(8,128)(2,1)S(1)} %collective-permute-done.20.refs_3_) | copy-start | bytes 393220
  161.7 56.2 %collective-permute-start.28 = (f32[320]{0:T(512)S(1)}, f32[320]{0:T(512)S(1)}, u32[]{:S(2)}, u32[]{:S(2)}) collective-permute-start(f32[320]{0:T(512)S(1)} %pad_maximum_fusion.6), channel_id=1, source_target_pairs={{0,0},{1,8},{8,256},{9,264},{256,1},{257,9},{264,257},{265,265},{2... | collective-permute-start | bytes 3848 | tf_op jit(solution)/shard_map/ppermute | solution.py:46
  166.4 0.7 copy-start.15
  166.5 0.7 copy-start.16
  167.1 0.7 copy-start.17
  170.9 23.4 %collective-permute-start.26 = (f32[64,256]{1,0:T(8,128)S(1)}, f32[64,256]{1,0:T(8,128)S(1)}, u32[]{:S(2)}, u32[]{:S(2)}) collective-permute-start(f32[64,256]{1,0:T(8,128)S(1)} %get-tuple-element.30), channel_id=1, source_target_pairs={{0,384},{128,0},{256,128},{384,256},{1,385},{129,1},{257,129},{385... | collective-permute-start | bytes 196616 | tf_op jit(solution)/shard_map/ppermute | solution.py:23
  179.0 15.3 %collective-permute-start.25 = (f32[64,256]{1,0:T(8,128)S(1)}, f32[64,256]{1,0:T(8,128)S(1)}, u32[]{:S(2)}, u32[]{:S(2)}) collective-permute-start(f32[64,256]{1,0:T(8,128)S(1)} %get-tuple-element.31), channel_id=1, source_target_pairs={{0,128},{128,256},{256,384},{384,0},{1,129},{129,257},{257,385},{3... | collective-permute-start | bytes 196616 | tf_op jit(solution)/shard_map/ppermute | solution.py:23
  180.9 13.4 %collective-permute-start.24 = (f32[64,256]{1,0:T(8,128)S(1)}, f32[64,256]{1,0:T(8,128)S(1)}, u32[]{:S(2)}, u32[]{:S(2)}) collective-permute-start(f32[64,256]{1,0:T(8,128)S(1)} %get-tuple-element.29), channel_id=1, source_target_pairs={{0,256},{128,384},{256,0},{384,128},{1,257},{129,385},{257,1},{385... | collective-permute-start | bytes 196616 | tf_op jit(solution)/shard_map/ppermute | solution.py:23
  184.2 1.0 copy-start.1
  192.4 76.7 %collective-permute-start.14 = (bf16[8,128,256]{2,1,0:T(8,128)(2,1)}, bf16[8,128,256]{2,1,0:T(8,128)(2,1)S(1)}, u32[]{:S(2)}, u32[]{:S(2)}) collective-permute-start(bf16[8,128,256]{2,1,0:T(8,128)(2,1)} %get-tuple-element.9), channel_id=1, source_target_pairs={{0,1},{1,0},{2,3},{3,2},{4,5},{5,4},{6,7},{7,6},{8,9},{9,8},{10,11... | collective-permute-start | bytes 1572872 | tf_op jit(solution)/shard_map/ppermute | solution.py:27
  195.3 73.1 %collective-permute-start.27 = (f32[64,256]{1,0:T(8,128)S(1)}, f32[64,256]{1,0:T(8,128)S(1)}, u32[]{:S(2)}, u32[]{:S(2)}) collective-permute-start(f32[64,256]{1,0:T(8,128)S(1)} %get-tuple-element.17), channel_id=1, source_target_pairs={{0,0},{1,256},{8,1},{9,257},{256,8},{257,264},{264,9},{265,265},{2... | collective-permute-start | bytes 196616 | tf_op jit(solution)/shard_map/ppermute | solution.py:46
  268.3 3.0 %copy-start.19 = (f32[1,256]{1,0:T(1,128)}, f32[1,256]{1,0:T(1,128)S(1)}, u32[]{:S(2)}) copy-start(f32[1,256]{1,0:T(1,128)S(1)} %constant_dynamic-slice_fusion.1) | copy-start | bytes 3076
  268.4 2.9 %copy-start.21 = (f32[64]{0:T(128)}, f32[64]{0:T(128)S(1)}, u32[]{:S(2)}) copy-start(f32[64]{0:T(128)S(1)} %fusion.4) | copy-start | bytes 772

commit v6 on v5

--- a/solution.py
+++ b/solution.py
@@ -14,7 +14,6 @@
 DP = ("zb", "za", "y", "c")
 MP = ("x", "zh")
 X_STEPS = (1, 3, 2)
-Y_STEPS = (4, 3, 5, 2, 6, 1, 7)
 Z_STEPS = (2, 1, 3)
 
 
@@ -110,16 +109,21 @@
             other_ref[at] = jnp.where(straight, right, left).astype(other_ref.dtype)
 
 
-def total_kernel(mine_ref, *refs):
-    came, out_ref = refs[:-1], refs[-1]
-    cols = out_ref.shape[1]
-    for za in range(2):
-        total = mine_ref[za]
-        for ref in came:
-            total = total + ref[za].astype(jnp.float32)
+def total_kernel(info_ref, kept_ref, swapped_ref, came_ref, *refs):
+    out_refs, pieces_ref = refs[:4], refs[4]
+    y_count, za_count, _, wide = came_ref.shape
+    cols = wide // 2
+    here = info_ref[0]
+    for za in range(za_count):
+        total = kept_ref[0, za] + swapped_ref[0, za].astype(jnp.float32)
+        for i in range(y_count):
+            part = came_ref[i, za].astype(jnp.float32)
+            total = total + jnp.where(here == i, jnp.zeros_like(part), part)
         turned = total.T
         for zb in range(2):
-            out_ref[2 * zb + za] = turned[zb * cols : (zb + 1) * cols]
+            pieces_ref[2 * zb + za] = turned[zb * cols : (zb + 1) * cols]
+    for i, s in enumerate((0,) + Z_STEPS):
+        out_refs[i][...] = pieces_ref[(info_ref[1] + s) & 3]
 
 
 def arrange(info, own, other):
@@ -198,12 +202,23 @@
     )(info, *([mine] * SIZE["y"] + [came] * SIZE["y"]), *blocks)
 
 
-def total_of(mine, came, cols):
+def total_of(info, kept, swapped, came):
+    _, za_count, rows, wide = came.shape
+    piece = (wide // 2, rows)
+    own = pl.BlockSpec((1, za_count, rows, wide), lambda i, p: (p[0], 0, 0, 0))
+    full = pl.BlockSpec(came.shape, lambda i, p: (0, 0, 0, 0))
     return pl.pallas_call(
         total_kernel,
-        out_shape=jax.ShapeDtypeStruct((4, cols, mine.shape[1]), jnp.float32),
+        grid_spec=pltpu.PrefetchScalarGridSpec(
+            num_scalar_prefetch=1,
+            grid=(1,),
+            in_specs=[own, own, full],
+            out_specs=[pl.BlockSpec(piece, lambda i, p: (0, 0))] * 4,
+            scratch_shapes=[pltpu.VMEM((4,) + piece, jnp.float32)],
+        ),
+        out_shape=[jax.ShapeDtypeStruct(piece, jnp.float32)] * 4,
         name="total",
-    )(mine, *came)
+    )(info, kept, swapped, came)
 
 
 def per_device(context, cotangent, lengths, weight, row_stat, col_stat):
@@ -248,20 +263,19 @@
     row_held, col_held = stats[:heads], stats[heads:]
 
     kept, sent = grad_of(ctx, blocks)
-    parts = kept + flip(sent, "c").astype(jnp.float32)
+    swapped = flip(sent, "c")
+    narrow = (kept + swapped.astype(jnp.float32)).astype(jnp.bfloat16)
 
     own, other = back_of(info, w, w_came, blocks)
-    context_grad = (own + flip(other, "zh").astype(jnp.float32)).astype(jnp.bfloat16)
+    came = flip(other, "zh")
+    context_grad = (own + came.astype(jnp.float32)).astype(jnp.bfloat16)
     context_grad = context_grad.reshape(context.shape)
 
-    narrow = parts.astype(jnp.bfloat16)
-    last = SIZE["y"] - 1
-    came = [shift(pick(narrow, (y + s) & last), "y", s) for s in Y_STEPS]
-    pieces = total_of(pick(parts, y), came, cols)
+    came = lax.all_to_all(narrow, "y", 0, 0, tiled=True)
     zl = zb * 2 + za
-    part = pick(pieces, zl)
-    for s in Z_STEPS:
-        part = part + shift(pick(pieces, (zl + s) & 3), ("zb", "za"), s)
+    part, *pieces = total_of(jnp.stack([y, zl]).astype(jnp.int32), kept, swapped, came)
+    for i, s in enumerate(Z_STEPS):
+        part = part + shift(pieces[i], ("zb", "za"), s)
     grad = part / groups
     grad_own = rotate(grad, False)
 

time: 274 us -> 254 us (0.927)
  starting transfers between devices: 125 us -> 97.3 us
  waiting for transfers between devices: 40.7 us -> 58.8 us
  blocking collectives: 65.1 us -> 58.7 us
  local copies, waits for them, and re-layouts: 9.72 us -> 6.67 us
    ppermute x16 -> x9, starting transfers between devices: 65.7 us -> 27 us  [shift(): lax.ppermute(value, axes, [(i, (i + step) % size) for i in range(size)])]
    ppermute x2, waiting for transfers between devices: 7.98 us -> 19.9 us  [turn(): return lax.ppermute(value, ('zb', 'zh'), pairs)]
    ppermute x2, starting transfers between devices: 6.05 us -> 14.7 us  [turn(): return lax.ppermute(value, ('zb', 'zh'), pairs)]
    all_to_all x0 -> x1, starting transfers between devices: none -> 6.82 us  [per_device(): came = lax.all_to_all(narrow, 'y', 0, 0, tiled=True)]
    ppermute x16 -> x9, waiting for transfers between devices: 15.3 us -> 22.1 us  [shift(): lax.ppermute(value, axes, [(i, (i + step) % size) for i in range(size)])]
    psum x1, blocking collectives: 15.2 us -> 8.61 us  [per_device(): col_all = lax.psum(col_all, 'x')]
    ppermute x9, waiting for transfers between devices: 17.4 us -> 13.1 us  [flip(): return lax.ppermute(value, axis, [(i, i ^ mask) for i in range(SIZE[axis])])]
    ppermute x9, starting transfers between devices: 43.9 us -> 39.8 us  [flip(): return lax.ppermute(value, axis, [(i, i ^ mask) for i in range(SIZE[axis])])]
  transfers between devices with their start and end apart: 29 -> 23, of which waited for: 8 -> 12; matrix products, arithmetic and copies ran while one was open for 4% -> 3% of each run, Pallas kernels for 7% -> 8%
where the time goes in v6:
time: 254 us; the launch traced here: 251 us
  starting transfers between devices  97.3 us (38%)
  waiting for transfers between devices  58.8 us (23%)
  blocking collectives  58.7 us (23%)
  Pallas kernels  19.4 us (8%)
  other arithmetic  8.58 us (3%)
  local copies, waits for them, and re-layouts  6.67 us (3%)
    ppermute x9, starting transfers between devices, flip(): return lax.ppermute(value, axis, [(i, i ^ mask) for i in range(SIZE[axis])])  39.8 us
    ppermute x9, starting transfers between devices, shift(): lax.ppermute(value, axes, [(i, (i + step) % size) for i in range(size)])  27 us
    ppermute x9, waiting for transfers between devices, shift(): lax.ppermute(value, axes, [(i, (i + step) % size) for i in range(size)])  22.1 us
    ppermute x2, waiting for transfers between devices, turn(): return lax.ppermute(value, ('zb', 'zh'), pairs)  19.9 us
    ppermute x2, starting transfers between devices, turn(): return lax.ppermute(value, ('zb', 'zh'), pairs)  14.7 us
    psum x1, blocking collectives, per_device(): rows = lax.psum(rows, 'y')  13.8 us
    ppermute x9, waiting for transfers between devices, flip(): return lax.ppermute(value, axis, [(i, i ^ mask) for i in range(SIZE[axis])])  13.1 us
    psum x1, blocking collectives, per_device(): sums = lax.psum(jnp.concatenate([slot(row_here, c, 2), tail]), 'c')  11.2 us
  transfers between devices with their start and end apart: 23, of which 12 were waited for; matrix products, arithmetic and copies ran while one was open for 3% of the time, Pallas kernels for 8%

profile of v6, /device:TPU:1, one launch (start us, length us, event | category | flops | bytes accessed | tf_op | source)
XLA Modules:
  0.0 251.4 jit_solution(2850477186953444828)
XLA Ops:
  0.6 0.7 iota_compare_fusion
  1.5 1.4 broadcast_select_fusion
  3.0 11.5 %collective-permute-start.10 = (bf16[128,2048]{1,0:T(8,128)(2,1)S(1)}, bf16[128,2048]{1,0:T(8,128)(2,1)S(1)}, u32[]{:S(2)}, u32[]{:S(2)}) collective-permute-start(bf16[128,2048]{1,0:T(8,128)(2,1)S(1)} %get-tuple-element.26), channel_id=1, source_target_pairs={{0,1},{1,0},{2,3},{3,2},{4,5},{5,4},{6,7},{7,6},{8,9},{9,8},{10,11... | collective-permute-start | bytes 1572872 | tf_op jit(solution)/shard_map/ppermute | solution.py:26
  14.4 3.1 %collective-permute-start.7 = (bf16[128,2048]{1,0:T(8,128)(2,1)S(1)}, bf16[128,2048]{1,0:T(8,128)(2,1)S(1)}, u32[]{:S(2)}, u32[]{:S(2)}) collective-permute-start(bf16[128,2048]{1,0:T(8,128)(2,1)S(1)} %get-tuple-element.27.refs_16_.refs_0_), channel_id=1, source_target_pairs={{0,2},{2,4},{4,6},{6,0},{1,3},{3,5},{5,7},{7,1},{8,10},{10,12},{12... | collective-permute-start | bytes 1572872 | tf_op jit(solution)/shard_map/ppermute | solution.py:22
  17.6 1.9 collective-permute-start.15
  19.5 7.5 %collective-permute-start = (bf16[1,64,256]{2,1,0:T(8,128)(2,1)S(1)}, bf16[1,64,256]{2,1,0:T(8,128)(2,1)S(1)}, u32[]{:S(2)}, u32[]{:S(2)}) collective-permute-start(bf16[1,64,256]{2,1,0:T(8,128)(2,1)S(1)} %convert_bitcast_fusion), channel_id=1, source_target_pairs={{0,64},{16,80},{32,96},{48,112},{64,0},{80,16},{96,32},{112,48},{1... | collective-permute-start | bytes 98312 | tf_op jit(solution)/shard_map/ppermute | solution.py:26
  27.0 3.4 %collective-permute-start.8 = (bf16[128,2048]{1,0:T(8,128)(2,1)S(1)}, bf16[128,2048]{1,0:T(8,128)(2,1)S(1)}, u32[]{:S(2)}, u32[]{:S(2)}) collective-permute-start(bf16[128,2048]{1,0:T(8,128)(2,1)S(1)} %get-tuple-element.27.refs_16_.refs_0_), channel_id=1, source_target_pairs={{0,6},{2,0},{4,2},{6,4},{1,7},{3,1},{5,3},{7,5},{8,14},{10,8},{12,... | collective-permute-start | bytes 1572872 | tf_op jit(solution)/shard_map/ppermute | solution.py:22
  30.4 3.4 %collective-permute-start.9 = (bf16[128,2048]{1,0:T(8,128)(2,1)S(1)}, bf16[128,2048]{1,0:T(8,128)(2,1)S(1)}, u32[]{:S(2)}, u32[]{:S(2)}) collective-permute-start(bf16[128,2048]{1,0:T(8,128)(2,1)S(1)} %get-tuple-element.27.refs_16_.refs_0_), channel_id=1, source_target_pairs={{0,4},{2,6},{4,0},{6,2},{1,5},{3,7},{5,1},{7,3},{8,12},{10,14},{12... | collective-permute-start | bytes 1572872 | tf_op jit(solution)/shard_map/ppermute | solution.py:22
  33.9 2.2 collective-permute-start.11
  36.1 4.3 %collective-permute-start.12 = (bf16[128,2048]{1,0:T(8,128)(2,1)S(1)}, bf16[128,2048]{1,0:T(8,128)(2,1)}, u32[]{:S(2)}, u32[]{:S(2)}) collective-permute-start(bf16[128,2048]{1,0:T(8,128)(2,1)S(1)} %collective-permute-done.10.refs_20_.refs_4_), channel_id=1, source_target_pairs={{0,6},{2,0},{4,2},{6,4},{1,7},{3,1},{5,3},{7,5},{8,14},{10,8},{12,... | collective-permute-start | bytes 1572872 | tf_op jit(solution)/shard_map/ppermute | solution.py:22
  40.4 0.8 copy-done.12
  41.2 2.1 collective-permute-start.13
  43.3 0.6 stack.62.info_ref
  44.0 3.2 %arrange.1.ctx_ref = bf16[512,1024]{1,0:T(8,128)(2,1)} custom-call(s32[13]{0:T(128)} %stack.62.info_ref, bf16[8,128,256]{2,1,0:T(8,128)(2,1)} %bitcast.33, bf16[8,128,256]{2,1,0:T(8,128)(2,1)} %bitcast.34), custom_call_target="tpu_custom_call" | custom-call | tf_op jit(solution)/shard_map/arrange/pallas_call | solution.py:132
  47.2 3.8 %collective-permute-start.1 = (bf16[2,64,256]{2,1,0:T(8,128)(2,1)S(1)}, bf16[2,64,256]{2,1,0:T(8,128)(2,1)S(1)}, u32[]{:S(2)}, u32[]{:S(2)}) collective-permute-start(bf16[2,64,256]{2,1,0:T(8,128)(2,1)S(1)} %pad_maximum_fusion.3), channel_id=1, source_target_pairs={{0,32},{16,48},{32,0},{48,16},{64,96},{80,112},{96,64},{112,80},{1... | collective-permute-start | bytes 196616 | tf_op jit(solution)/shard_map/ppermute | solution.py:26
  51.0 10.1 %collective-permute-done.11.refs_21_.refs_5_ = bf16[128,2048]{1,0:T(8,128)(2,1)} collective-permute-done((bf16[128,2048]{1,0:T(8,128)(2,1)S(1)}, bf16[128,2048]{1,0:T(8,128)(2,1)}, u32[]{:S(2)}, u32[]{:S(2)}) %collective-permute-start.11) | collective-permute-done | bytes 524320 | tf_op jit(solution)/shard_map/ppermute | solution.py:22
  61.1 2.4 collective-permute-done.12.refs_22_.refs_6_
  63.5 4.5 %collective-permute-done.13.refs_23_.refs_7_ = bf16[128,2048]{1,0:T(8,128)(2,1)S(1)} collective-permute-done((bf16[128,2048]{1,0:T(8,128)(2,1)S(1)}, bf16[128,2048]{1,0:T(8,128)(2,1)S(1)}, u32[]{:S(2)}, u32[]{:S(2)}) %collective-permute-start.13) | collective-permute-done | bytes 524320 | tf_op jit(solution)/shard_map/ppermute | solution.py:22
  68.0 0.8 copy-done.11
  68.8 6.0 %grad.1 = (f32[8,2,256,128]{3,2,1,0:T(8,128)}, bf16[8,2,256,128]{3,2,1,0:T(8,128)(2,1)}) custom-call(bf16[512,1024]{1,0:T(8,128)(2,1)} %arrange.1.ctx_ref, bf16[128,2048]{1,0:T(8,128)(2,1)} %copy-done.4, bf16[128,2048]{1,0:T(8,128)(2,1)} %copy-done.8, bf16[128,2048]{1,0:T(8,128)(2,1)} %copy-done.9, bf16[128,2048]{1,0:T(8,128)(2,1)} %copy-done.10, ...), custom_call_target="tpu_custom_call" | custom-call | flops 2147483648 | bytes 9437184 | tf_op jit(solution)/shard_map/grad/pallas_call | solution.py:151
  74.8 4.6 %collective-permute-start.16 = (bf16[8,2,256,128]{3,2,1,0:T(8,128)(2,1)}, bf16[8,2,256,128]{3,2,1,0:T(8,128)(2,1)S(1)}, u32[]{:S(2)}, u32[]{:S(2)}) collective-permute-start(bf16[8,2,256,128]{3,2,1,0:T(8,128)(2,1)} %get-tuple-element.15), channel_id=1, source_target_pairs={{0,8},{8,0},{1,9},{9,1},{2,10},{10,2},{3,11},{11,3},{4,12},{12,4},... | collective-permute-start | bytes 3145736 | tf_op jit(solution)/shard_map/ppermute | solution.py:26
  79.4 2.3 collective-permute-start.2
  81.7 4.6 %collective-permute-done.2 = bf16[4,64,256]{2,1,0:T(8,128)(2,1)S(1)} collective-permute-done((bf16[4,64,256]{2,1,0:T(8,128)(2,1)S(1)}, bf16[4,64,256]{2,1,0:T(8,128)(2,1)S(1)}, u32[]{:S(2)}, u32[]{:S(2)}) %collective-permute-start.2) | collective-permute-done | bytes 131104 | tf_op jit(solution)/shard_map/ppermute | solution.py:26
  86.4 0.7 collective-permute-start.3
  87.1 14.0 %collective-permute-start.4 = (bf16[8,64,256]{2,1,0:T(8,128)(2,1)S(1)}, bf16[8,64,256]{2,1,0:T(8,128)(2,1)S(1)}, u32[]{:S(2)}, u32[]{:S(2)}) collective-permute-start(bf16[8,64,256]{2,1,0:T(8,128)(2,1)S(1)} %pad_maximum_fusion.1), channel_id=1, source_target_pairs={{0,256},{1,0},{256,257},{257,1},{2,258},{3,2},{258,259},{259,3},{4... | collective-permute-start | bytes 786440 | tf_op jit(solution)/shard_map/ppermute | solution.py:35
  101.1 19.9 %collective-permute-done.4 = bf16[8,64,256]{2,1,0:T(8,128)(2,1)S(1)} collective-permute-done((bf16[8,64,256]{2,1,0:T(8,128)(2,1)S(1)}, bf16[8,64,256]{2,1,0:T(8,128)(2,1)S(1)}, u32[]{:S(2)}, u32[]{:S(2)}) %collective-permute-start.4) | collective-permute-done | bytes 262176 | tf_op jit(solution)/shard_map/ppermute | solution.py:35
  121.0 1.9 collective-permute-start.5
  123.0 1.0 copy-done.3
  123.9 2.9 %add_convert_fusion = bf16[8,2,256,128]{3,2,1,0:T(8,128)(2,1)} fusion(f32[8,2,256,128]{3,2,1,0:T(8,128)} %get-tuple-element.14.kept_ref, bf16[8,2,256,128]{3,2,1,0:T(8,128)(2,1)S(1)} %collective-permute-done.16.swapped_ref), kind=kLoop, calls=%fused_computation | loop fusion | flops 1572864 | bytes 4194304 | tf_op jit(solution)/shard_map/convert_element_type | solution.py:267
  126.8 6.8 %all-to-all-start = ((bf16[8,2,256,128]{3,2,1,0:T(8,128)(2,1)}), bf16[8,2,256,128]{3,2,1,0:T(8,128)(2,1)S(1)}, u32[]{:S(2)}, u32[]{:S(2)}) async-start(bf16[8,2,256,128]{3,2,1,0:T(8,128)(2,1)} %add_convert_fusion), calls=%async_computation | async-start | bytes 2097152 | tf_op jit(solution)/shard_map/all_to_all | solution.py:274
  133.6 1.1 collective-permute-done.5
  134.8 0.1 pad_maximum_fusion.refs_0_.refs_1_.refs_2_.refs_3_.refs_4_.refs_5_.refs_6_.refs_7_
  134.9 4.5 %collective-permute-start.6 = (bf16[16,64,512]{2,1,0:T(8,128)(2,1)S(1)}, bf16[16,64,512]{2,1,0:T(8,128)(2,1)S(1)}, u32[]{:S(2)}, u32[]{:S(2)}) collective-permute-start(bf16[16,64,512]{2,1,0:T(8,128)(2,1)S(1)} %pad_maximum_fusion.refs_0_.refs_1_.refs_2_.refs_3_.refs_4_.refs_5_.refs_6_.refs_7_), channel_id=1, source_target_pairs={{0,8},{8,0},{1,9},{9,1},{2,10},{10,2},{3,11},{11,3},{4,12},{12,4},... | collective-permute-start | bytes 3145736 | tf_op jit(solution)/shard_map/ppermute | solution.py:26
  139.4 2.3 collective-permute-done.6.refs_8_.refs_9_.refs_10_.refs_11_.refs_12_.refs_13_.refs_14_.refs_15_
  141.7 1.0 copy-done.1
  142.7 7.2 %back.1 = (f32[8,128,256]{2,1,0:T(8,128)}, bf16[8,128,256]{2,1,0:T(8,128)(2,1)}) custom-call(s32[13]{0:T(128)} %stack.62.info_ref, bf16[16,64,512]{2,1,0:T(8,128)(2,1)} %copy-done, bf16[16,64,512]{2,1,0:T(8,128)(2,1)} %copy-done, bf16[16,64,512]{2,1,0:T(8,128)(2,1)} %copy-done, bf16[16,64,512]{2,1,0:T(8,128)(2,1)} %copy-done, bf16[16,64,512]{2,1,0:T(8,128)(2,1)} %copy-done, ...), custom_call_target="tpu_custom_call" | custom-call | flops 2147483648 | bytes 8388608 | tf_op jit(solution)/shard_map/back/pallas_call | solution.py:184
  149.9 1.9 collective-permute-start.14
  151.9 6.6 %collective-permute-start.21 = (f32[320]{0:T(512)S(1)}, f32[320]{0:T(512)S(1)}, u32[]{:S(2)}, u32[]{:S(2)}) collective-permute-start(f32[320]{0:T(512)S(1)} %pad_maximum_fusion.6), channel_id=1, source_target_pairs={{0,0},{1,8},{8,256},{9,264},{256,1},{257,9},{264,257},{265,265},{2... | collective-permute-start | bytes 3848 | tf_op jit(solution)/shard_map/ppermute | solution.py:45
  158.5 0.6 pad_add_fusion.info_ref
  159.1 3.7 %all-to-all-done.came_ref = bf16[8,2,256,128]{3,2,1,0:T(8,128)(2,1)S(1)} async-done(((bf16[8,2,256,128]{3,2,1,0:T(8,128)(2,1)}), bf16[8,2,256,128]{3,2,1,0:T(8,128)(2,1)S(1)}, u32[]{:S(2)}, u32[]{:S(2)}) %all-to-all-start) | async-done | bytes 1048608 | tf_op jit(solution)/shard_map/all_to_all | solution.py:274
  162.8 1.0 copy-done.2
  163.8 3.1 %total.1 = (f32[64,256]{1,0:T(8,128)}, f32[64,256]{1,0:T(8,128)}, f32[64,256]{1,0:T(8,128)}, f32[64,256]{1,0:T(8,128)}) custom-call(s32[2]{0:T(128)} %pad_add_fusion.info_ref, f32[8,2,256,128]{3,2,1,0:T(8,128)} %get-tuple-element.14.kept_ref, bf16[8,2,256,128]{3,2,1,0:T(8,128)(2,1)} %copy-done.3, bf16[8,2,256,128]{3,2,1,0:T(8,128)(2,1)} %copy-done.2), custom_call_target="tpu_custom_call" | custom-call | tf_op jit(solution)/shard_map/total/pallas_call | solution.py:210
  166.9 2.0 collective-permute-start.19
  168.9 3.4 %collective-permute-start.18 = (f32[64,256]{1,0:T(8,128)}, f32[64,256]{1,0:T(8,128)S(1)}, u32[]{:S(2)}, u32[]{:S(2)}) collective-permute-start(f32[64,256]{1,0:T(8,128)} %get-tuple-element.18), channel_id=1, source_target_pairs={{0,128},{128,256},{256,384},{384,0},{1,129},{129,257},{257,385},{3... | collective-permute-start | bytes 196616 | tf_op jit(solution)/shard_map/ppermute | solution.py:22
  172.3 3.1 %collective-permute-start.17 = (f32[64,256]{1,0:T(8,128)}, f32[64,256]{1,0:T(8,128)S(1)}, u32[]{:S(2)}, u32[]{:S(2)}) collective-permute-start(f32[64,256]{1,0:T(8,128)} %get-tuple-element.17), channel_id=1, source_target_pairs={{0,256},{128,384},{256,0},{384,128},{1,257},{129,385},{257,1},{385... | collective-permute-start | bytes 196616 | tf_op jit(solution)/shard_map/ppermute | solution.py:22
  175.4 5.0 %collective-permute-done.14 = bf16[8,128,256]{2,1,0:T(8,128)(2,1)S(1)} collective-permute-done((bf16[8,128,256]{2,1,0:T(8,128)(2,1)}, bf16[8,128,256]{2,1,0:T(8,128)(2,1)S(1)}, u32[]{:S(2)}, u32[]{:S(2)}) %collective-permute-start.14) | collective-permute-done | bytes 524320 | tf_op jit(solution)/shard_map/ppermute | solution.py:26
  180.4 0.9 add_convert_fusion.1
  181.3 0.7 collective-permute-done.19
  182.0 1.7 collective-permute-done.18
  183.7 2.7 %collective-permute-done.17 = f32[64,256]{1,0:T(8,128)S(1)} collective-permute-done((f32[64,256]{1,0:T(8,128)}, f32[64,256]{1,0:T(8,128)S(1)}, u32[]{:S(2)}, u32[]{:S(2)}) %collective-permute-start.17) | collective-permute-done | bytes 65568 | tf_op jit(solution)/shard_map/ppermute | solution.py:22
  186.4 0.1 add_reduce_fusion
  186.5 2.3 collective-permute-start.20
  188.9 2.5 psum.49
  191.3 8.6 %psum.50 = f32[64]{0:T(128)S(1)} all-reduce(f32[64]{0:T(128)S(1)} %psum.49), channel_id=1, replica_groups=mesh['zb'=2,'za'=2,'y'=8,'c'=2,'x'=4,'zh'=2] {'x'}, use_global_device_ids=true, to_apply=%region_3.4 | all-reduce | flops 64 | bytes 512 | tf_op jit(solution)/shard_map/psum | solution.py:285
  200.0 0.1 add_reduce_fusion.1
  200.2 13.8 %psum.51 = f32[512]{0:T(512)S(1)} all-reduce(f32[512]{0:T(512)S(1)} %pad_maximum_fusion.7), channel_id=1, replica_groups=mesh['zb'=2,'za'=2,'y'=8,'c'=2,'x'=4,'zh'=2] {'y'}, use_global_device_ids=true, to_apply=%region_5.6 | all-reduce | flops 512 | bytes 4096 | tf_op jit(solution)/shard_map/psum | solution.py:289
  214.0 8.2 %psum.52 = f32[768]{0:T(1024)S(1)} all-reduce(f32[768]{0:T(1024)S(1)} %pad_maximum_fusion.4), channel_id=1, replica_groups=mesh['zb'=2,'za'=2,'y'=8,'c'=2,'x'=4,'zh'=2] {'zb','za'}, use_global_device_ids=true, to_apply=%region_6.7 | all-reduce | flops 768 | bytes 6144 | tf_op jit(solution)/shard_map/psum | solution.py:290
  222.3 7.7 %psum.53 = f32[1024]{0:T(1024)S(1)} all-reduce(f32[1024]{0:T(1024)S(1)} %pad_maximum_fusion.5), channel_id=1, replica_groups=mesh['zb'=2,'za'=2,'y'=8,'c'=2,'x'=4,'zh'=2] {'zh'}, use_global_device_ids=true, to_apply=%region_7.8 | all-reduce | flops 1024 | bytes 8192 | tf_op jit(solution)/shard_map/psum | solution.py:292
  230.0 0.6 fusion
  230.7 0.6 concatenate.41
  231.4 11.2 %psum.54 = f32[640]{0:T(1024)S(1)} all-reduce(f32[640]{0:T(1024)S(1)} %concatenate.41), channel_id=1, replica_groups=mesh['zb'=2,'za'=2,'y'=8,'c'=2,'x'=4,'zh'=2] {'c'}, use_global_device_ids=true, to_apply=%region_9.10 | all-reduce | flops 640 | bytes 5120 | tf_op jit(solution)/shard_map/psum | solution.py:298
  242.6 0.5 slice.51
  243.1 6.7 %psum.55 = f32[]{:T(128)} all-reduce(f32[]{:T(128)} %bitcast.22), channel_id=1, replica_groups=mesh['zb'=2,'za'=2,'y'=8,'c'=2,'x'=4,'zh'=2] {'x'}, use_global_device_ids=true, to_apply=%region_10.11 | all-reduce | flops 1 | bytes 8 | tf_op jit(solution)/shard_map/psum | solution.py:300
  250.7 0.7 divide_bitcast_fusion
  (74 shorter events, 0.9 us)
Async XLA Ops:
  1.5 16.1 %copy-start.6 = (bf16[1024,256]{1,0:T(8,128)(2,1)S(1)}, bf16[1024,256]{1,0:T(8,128)(2,1)}, u32[]{:S(2)}) copy-start(bf16[1024,256]{1,0:T(8,128)(2,1)} %param.6) | copy-start | bytes 1572868
  1.5 18.1 %copy-start.14 = (f32[256,64]{0,1:T(8,128)S(1)}, f32[256,64]{0,1:T(8,128)}, u32[]{:S(2)}) copy-start(f32[256,64]{0,1:T(8,128)} %param.9) | copy-start | bytes 196612
  3.0 65.0 %copy-start.4 = (bf16[128,2048]{1,0:T(8,128)(2,1)}, bf16[128,2048]{1,0:T(8,128)(2,1)S(1)}, u32[]{:S(2)}) copy-start(bf16[128,2048]{1,0:T(8,128)(2,1)S(1)} %get-tuple-element.27.refs_16_.refs_0_) | copy-start | bytes 1572868
  3.0 30.9 %collective-permute-start.10 = (bf16[128,2048]{1,0:T(8,128)(2,1)S(1)}, bf16[128,2048]{1,0:T(8,128)(2,1)S(1)}, u32[]{:S(2)}, u32[]{:S(2)}) collective-permute-start(bf16[128,2048]{1,0:T(8,128)(2,1)S(1)} %get-tuple-element.26), channel_id=1, source_target_pairs={{0,1},{1,0},{2,3},{3,2},{4,5},{5,4},{6,7},{7,6},{8,9},{9,8},{10,11... | collective-permute-start | bytes 1572872 | tf_op jit(solution)/shard_map/ppermute | solution.py:26
  14.4 21.6 %collective-permute-start.7 = (bf16[128,2048]{1,0:T(8,128)(2,1)S(1)}, bf16[128,2048]{1,0:T(8,128)(2,1)S(1)}, u32[]{:S(2)}, u32[]{:S(2)}) collective-permute-start(bf16[128,2048]{1,0:T(8,128)(2,1)S(1)} %get-tuple-element.27.refs_16_.refs_0_), channel_id=1, source_target_pairs={{0,2},{2,4},{4,6},{6,0},{1,3},{3,5},{5,7},{7,1},{8,10},{10,12},{12... | collective-permute-start | bytes 1572872 | tf_op jit(solution)/shard_map/ppermute | solution.py:22
  17.6 22.8 %collective-permute-start.15 = (bf16[1024,256]{1,0:T(8,128)(2,1)S(1)}, bf16[1024,256]{1,0:T(8,128)(2,1)S(1)}, u32[]{:S(2)}, u32[]{:S(2)}) collective-permute-start(bf16[1024,256]{1,0:T(8,128)(2,1)S(1)} %copy-done.6), channel_id=1, source_target_pairs={{0,1},{1,0},{2,3},{3,2},{4,5},{5,4},{6,7},{7,6},{8,9},{9,8},{10,11... | collective-permute-start | bytes 1572872 | tf_op jit(solution)/shard_map/ppermute | solution.py:26
  19.5 10.8 %collective-permute-start = (bf16[1,64,256]{2,1,0:T(8,128)(2,1)S(1)}, bf16[1,64,256]{2,1,0:T(8,128)(2,1)S(1)}, u32[]{:S(2)}, u32[]{:S(2)}) collective-permute-start(bf16[1,64,256]{2,1,0:T(8,128)(2,1)S(1)} %convert_bitcast_fusion), channel_id=1, source_target_pairs={{0,64},{16,80},{32,96},{48,112},{64,0},{80,16},{96,32},{112,48},{1... | collective-permute-start | bytes 98312 | tf_op jit(solution)/shard_map/ppermute | solution.py:26
  27.0 20.2 %collective-permute-start.8 = (bf16[128,2048]{1,0:T(8,128)(2,1)S(1)}, bf16[128,2048]{1,0:T(8,128)(2,1)S(1)}, u32[]{:S(2)}, u32[]{:S(2)}) collective-permute-start(bf16[128,2048]{1,0:T(8,128)(2,1)S(1)} %get-tuple-element.27.refs_16_.refs_0_), channel_id=1, source_target_pairs={{0,6},{2,0},{4,2},{6,4},{1,7},{3,1},{5,3},{7,5},{8,14},{10,8},{12,... | collective-permute-start | bytes 1572872 | tf_op jit(solution)/shard_map/ppermute | solution.py:22
  30.4 20.6 %collective-permute-start.9 = (bf16[128,2048]{1,0:T(8,128)(2,1)S(1)}, bf16[128,2048]{1,0:T(8,128)(2,1)S(1)}, u32[]{:S(2)}, u32[]{:S(2)}) collective-permute-start(bf16[128,2048]{1,0:T(8,128)(2,1)S(1)} %get-tuple-element.27.refs_16_.refs_0_), channel_id=1, source_target_pairs={{0,4},{2,6},{4,0},{6,2},{1,5},{3,7},{5,1},{7,3},{8,12},{10,14},{12... | collective-permute-start | bytes 1572872 | tf_op jit(solution)/shard_map/ppermute | solution.py:22
  33.8 34.1 %copy-start.7 = (bf16[128,2048]{1,0:T(8,128)(2,1)}, bf16[128,2048]{1,0:T(8,128)(2,1)S(1)}, u32[]{:S(2)}) copy-start(bf16[128,2048]{1,0:T(8,128)(2,1)S(1)} %collective-permute-done.10.refs_20_.refs_4_) | copy-start | bytes 1572868
  33.9 27.2 %collective-permute-start.11 = (bf16[128,2048]{1,0:T(8,128)(2,1)S(1)}, bf16[128,2048]{1,0:T(8,128)(2,1)}, u32[]{:S(2)}, u32[]{:S(2)}) collective-permute-start(bf16[128,2048]{1,0:T(8,128)(2,1)S(1)} %collective-permute-done.10.refs_20_.refs_4_), channel_id=1, source_target_pairs={{0,2},{2,4},{4,6},{6,0},{1,3},{3,5},{5,7},{7,1},{8,10},{10,12},{12... | collective-permute-start | bytes 1572872 | tf_op jit(solution)/shard_map/ppermute | solution.py:22
  36.1 31.9 %copy-start.8 = (bf16[128,2048]{1,0:T(8,128)(2,1)}, bf16[128,2048]{1,0:T(8,128)(2,1)S(1)}, u32[]{:S(2)}) copy-start(bf16[128,2048]{1,0:T(8,128)(2,1)S(1)} %collective-permute-done.7.refs_17_.refs_1_) | copy-start | bytes 1572868
  36.1 27.4 %collective-permute-start.12 = (bf16[128,2048]{1,0:T(8,128)(2,1)S(1)}, bf16[128,2048]{1,0:T(8,128)(2,1)}, u32[]{:S(2)}, u32[]{:S(2)}) collective-permute-start(bf16[128,2048]{1,0:T(8,128)(2,1)S(1)} %collective-permute-done.10.refs_20_.refs_4_), channel_id=1, source_target_pairs={{0,6},{2,0},{4,2},{6,4},{1,7},{3,1},{5,3},{7,5},{8,14},{10,8},{12,... | collective-permute-start | bytes 1572872 | tf_op jit(solution)/shard_map/ppermute | solution.py:22
  40.4 0.8 copy-start.12
  41.2 26.8 %collective-permute-start.13 = (bf16[128,2048]{1,0:T(8,128)(2,1)S(1)}, bf16[128,2048]{1,0:T(8,128)(2,1)S(1)}, u32[]{:S(2)}, u32[]{:S(2)}) collective-permute-start(bf16[128,2048]{1,0:T(8,128)(2,1)S(1)} %collective-permute-done.10.refs_20_.refs_4_), channel_id=1, source_target_pairs={{0,4},{2,6},{4,0},{6,2},{1,5},{3,7},{5,1},{7,3},{8,12},{10,14},{12... | collective-permute-start | bytes 1572872 | tf_op jit(solution)/shard_map/ppermute | solution.py:22
  47.1 20.8 %copy-start.9 = (bf16[128,2048]{1,0:T(8,128)(2,1)}, bf16[128,2048]{1,0:T(8,128)(2,1)S(1)}, u32[]{:S(2)}) copy-start(bf16[128,2048]{1,0:T(8,128)(2,1)S(1)} %collective-permute-done.8.refs_18_.refs_2_) | copy-start | bytes 1572868
  47.2 32.2 %collective-permute-start.1 = (bf16[2,64,256]{2,1,0:T(8,128)(2,1)S(1)}, bf16[2,64,256]{2,1,0:T(8,128)(2,1)S(1)}, u32[]{:S(2)}, u32[]{:S(2)}) collective-permute-start(bf16[2,64,256]{2,1,0:T(8,128)(2,1)S(1)} %pad_maximum_fusion.3), channel_id=1, source_target_pairs={{0,32},{16,48},{32,0},{48,16},{64,96},{80,112},{96,64},{112,80},{1... | collective-permute-start | bytes 196616 | tf_op jit(solution)/shard_map/ppermute | solution.py:26
  51.0 17.1 %copy-start.10 = (bf16[128,2048]{1,0:T(8,128)(2,1)}, bf16[128,2048]{1,0:T(8,128)(2,1)S(1)}, u32[]{:S(2)}) copy-start(bf16[128,2048]{1,0:T(8,128)(2,1)S(1)} %collective-permute-done.9.refs_19_.refs_3_) | copy-start | bytes 1572868
  68.0 0.8 copy-start.11
  74.8 48.1 %collective-permute-start.16 = (bf16[8,2,256,128]{3,2,1,0:T(8,128)(2,1)}, bf16[8,2,256,128]{3,2,1,0:T(8,128)(2,1)S(1)}, u32[]{:S(2)}, u32[]{:S(2)}) collective-permute-start(bf16[8,2,256,128]{3,2,1,0:T(8,128)(2,1)} %get-tuple-element.15), channel_id=1, source_target_pairs={{0,8},{8,0},{1,9},{9,1},{2,10},{10,2},{3,11},{11,3},{4,12},{12,4},... | collective-permute-start | bytes 3145736 | tf_op jit(solution)/shard_map/ppermute | solution.py:26
  79.4 6.9 %collective-permute-start.2 = (bf16[4,64,256]{2,1,0:T(8,128)(2,1)S(1)}, bf16[4,64,256]{2,1,0:T(8,128)(2,1)S(1)}, u32[]{:S(2)}, u32[]{:S(2)}) collective-permute-start(bf16[4,64,256]{2,1,0:T(8,128)(2,1)S(1)} %pad_maximum_fusion.2), channel_id=1, source_target_pairs={{0,16},{16,0},{32,48},{48,32},{64,80},{80,64},{96,112},{112,96},{1... | collective-permute-start | bytes 393224 | tf_op jit(solution)/shard_map/ppermute | solution.py:26
  86.4 14.7 %collective-permute-start.3 = (bf16[8,64,256]{2,1,0:T(8,128)(2,1)S(1)}, bf16[8,64,256]{2,1,0:T(8,128)(2,1)S(1)}, u32[]{:S(2)}, u32[]{:S(2)}) collective-permute-start(bf16[8,64,256]{2,1,0:T(8,128)(2,1)S(1)} %pad_maximum_fusion.1), channel_id=1, source_target_pairs={{0,0},{1,256},{256,1},{257,257},{2,2},{3,258},{258,3},{259,259},{4... | collective-permute-start | bytes 786440 | tf_op jit(solution)/shard_map/ppermute | solution.py:35
  87.1 33.9 %collective-permute-start.4 = (bf16[8,64,256]{2,1,0:T(8,128)(2,1)S(1)}, bf16[8,64,256]{2,1,0:T(8,128)(2,1)S(1)}, u32[]{:S(2)}, u32[]{:S(2)}) collective-permute-start(bf16[8,64,256]{2,1,0:T(8,128)(2,1)S(1)} %pad_maximum_fusion.1), channel_id=1, source_target_pairs={{0,256},{1,0},{256,257},{257,1},{2,258},{3,2},{258,259},{259,3},{4... | collective-permute-start | bytes 786440 | tf_op jit(solution)/shard_map/ppermute | solution.py:35
  121.0 13.7 %collective-permute-start.5 = (bf16[8,64,512]{2,1,0:T(8,128)(2,1)S(1)}, bf16[8,64,512]{2,1,0:T(8,128)(2,1)S(1)}, u32[]{:S(2)}, u32[]{:S(2)}) collective-permute-start(bf16[8,64,512]{2,1,0:T(8,128)(2,1)S(1)} %constant_dynamic-update-slice_fusion), channel_id=1, source_target_pairs={{0,128},{128,0},{1,129},{129,1},{2,130},{130,2},{3,131},{131,3},{4... | collective-permute-start | bytes 1572872 | tf_op jit(solution)/shard_map/ppermute | solution.py:26
  123.0 1.0 copy-start.3
  126.8 36.0 %all-to-all-start = ((bf16[8,2,256,128]{3,2,1,0:T(8,128)(2,1)}), bf16[8,2,256,128]{3,2,1,0:T(8,128)(2,1)S(1)}, u32[]{:S(2)}, u32[]{:S(2)}) async-start(bf16[8,2,256,128]{3,2,1,0:T(8,128)(2,1)} %add_convert_fusion), calls=%async_computation | async-start | bytes 2097152 | tf_op jit(solution)/shard_map/all_to_all | solution.py:274
  134.9 6.8 %copy-start = (bf16[16,64,512]{2,1,0:T(8,128)(2,1)}, bf16[16,64,512]{2,1,0:T(8,128)(2,1)S(1)}, u32[]{:S(2)}) copy-start(bf16[16,64,512]{2,1,0:T(8,128)(2,1)S(1)} %pad_maximum_fusion.refs_0_.refs_1_.refs_2_.refs_3_.refs_4_.refs_5_.refs_6_.refs_7_) | copy-start | bytes 3145732
  134.9 16.9 %copy-start.16 = (f32[256]{0:T(256)S(1)}, f32[256]{0:T(256)}, u32[]{:S(2)}) copy-start(f32[256]{0:T(256)} %param.10) | copy-start | bytes 3076
  134.9 16.9 %copy-start.18 = (f32[64]{0:T(128)S(1)}, f32[64]{0:T(128)}, u32[]{:S(2)}) copy-start(f32[64]{0:T(128)} %param.11) | copy-start | bytes 772
  134.9 6.8 %collective-permute-start.6 = (bf16[16,64,512]{2,1,0:T(8,128)(2,1)S(1)}, bf16[16,64,512]{2,1,0:T(8,128)(2,1)S(1)}, u32[]{:S(2)}, u32[]{:S(2)}) collective-permute-start(bf16[16,64,512]{2,1,0:T(8,128)(2,1)S(1)} %pad_maximum_fusion.refs_0_.refs_1_.refs_2_.refs_3_.refs_4_.refs_5_.refs_6_.refs_7_), channel_id=1, source_target_pairs={{0,8},{8,0},{1,9},{9,1},{2,10},{10,2},{3,11},{11,3},{4,12},{12,4},... | collective-permute-start | bytes 3145736 | tf_op jit(solution)/shard_map/ppermute | solution.py:26
  141.7 1.0 copy-start.1
  149.9 30.5 %collective-permute-start.14 = (bf16[8,128,256]{2,1,0:T(8,128)(2,1)}, bf16[8,128,256]{2,1,0:T(8,128)(2,1)S(1)}, u32[]{:S(2)}, u32[]{:S(2)}) collective-permute-start(bf16[8,128,256]{2,1,0:T(8,128)(2,1)} %get-tuple-element.13), channel_id=1, source_target_pairs={{0,1},{1,0},{2,3},{3,2},{4,5},{5,4},{6,7},{7,6},{8,9},{9,8},{10,11... | collective-permute-start | bytes 1572872 | tf_op jit(solution)/shard_map/ppermute | solution.py:26
  151.9 48.1 %collective-permute-start.21 = (f32[320]{0:T(512)S(1)}, f32[320]{0:T(512)S(1)}, u32[]{:S(2)}, u32[]{:S(2)}) collective-permute-start(f32[320]{0:T(512)S(1)} %pad_maximum_fusion.6), channel_id=1, source_target_pairs={{0,0},{1,8},{8,256},{9,264},{256,1},{257,9},{264,257},{265,265},{2... | collective-permute-start | bytes 3848 | tf_op jit(solution)/shard_map/ppermute | solution.py:45
  159.1 21.3 %copy-start.5 = (f32[8,128,256]{2,1,0:T(8,128)S(1)}, f32[8,128,256]{2,1,0:T(8,128)}, u32[]{:S(2)}) copy-start(f32[8,128,256]{2,1,0:T(8,128)} %get-tuple-element.12) | copy-start | bytes 3145732
  162.8 1.0 copy-start.2
  166.9 19.6 %copy-start.13 = (f32[64,256]{1,0:T(8,128)S(1)}, f32[64,256]{1,0:T(8,128)}, u32[]{:S(2)}) copy-start(f32[64,256]{1,0:T(8,128)} %get-tuple-element.16) | copy-start | bytes 196612
  166.9 15.2 %collective-permute-start.19 = (f32[64,256]{1,0:T(8,128)}, f32[64,256]{1,0:T(8,128)S(1)}, u32[]{:S(2)}, u32[]{:S(2)}) collective-permute-start(f32[64,256]{1,0:T(8,128)} %get-tuple-element.19), channel_id=1, source_target_pairs={{0,384},{128,0},{256,128},{384,256},{1,385},{129,1},{257,129},{385... | collective-permute-start | bytes 196616 | tf_op jit(solution)/shard_map/ppermute | solution.py:22
  168.9 14.8 %collective-permute-start.18 = (f32[64,256]{1,0:T(8,128)}, f32[64,256]{1,0:T(8,128)S(1)}, u32[]{:S(2)}, u32[]{:S(2)}) collective-permute-start(f32[64,256]{1,0:T(8,128)} %get-tuple-element.18), channel_id=1, source_target_pairs={{0,128},{128,256},{256,384},{384,0},{1,129},{129,257},{257,385},{3... | collective-permute-start | bytes 196616 | tf_op jit(solution)/shard_map/ppermute | solution.py:22
  172.3 14.1 %collective-permute-start.17 = (f32[64,256]{1,0:T(8,128)}, f32[64,256]{1,0:T(8,128)S(1)}, u32[]{:S(2)}, u32[]{:S(2)}) collective-permute-start(f32[64,256]{1,0:T(8,128)} %get-tuple-element.17), channel_id=1, source_target_pairs={{0,256},{128,384},{256,0},{384,128},{1,257},{129,385},{257,1},{385... | collective-permute-start | bytes 196616 | tf_op jit(solution)/shard_map/ppermute | solution.py:22
  186.5 64.1 %collective-permute-start.20 = (f32[64,256]{1,0:T(8,128)S(1)}, f32[64,256]{1,0:T(8,128)S(1)}, u32[]{:S(2)}, u32[]{:S(2)}) collective-permute-start(f32[64,256]{1,0:T(8,128)S(1)} %get-tuple-element.25), channel_id=1, source_target_pairs={{0,0},{1,256},{8,1},{9,257},{256,8},{257,264},{264,9},{265,265},{2... | collective-permute-start | bytes 196616 | tf_op jit(solution)/shard_map/ppermute | solution.py:45
  250.6 0.8 copy-start.15
  250.6 0.7 copy-start.17

commit v7 on v6

--- a/solution.py
+++ b/solution.py
@@ -14,12 +14,11 @@
 DP = ("zb", "za", "y", "c")
 MP = ("x", "zh")
 X_STEPS = (1, 3, 2)
-Z_STEPS = (2, 1, 3)
-
-
-def shift(value, axes, step):
-    size = 4 if axes == ("zb", "za") else SIZE[axes]
-    return lax.ppermute(value, axes, [(i, (i + step) % size) for i in range(size)])
+
+
+def shift(value, axis, step):
+    size = SIZE[axis]
+    return lax.ppermute(value, axis, [(i, (i + step) % size) for i in range(size)])
 
 
 def flip(value, axis, mask=1):
@@ -109,21 +108,18 @@
             other_ref[at] = jnp.where(straight, right, left).astype(other_ref.dtype)
 
 
-def total_kernel(info_ref, kept_ref, swapped_ref, came_ref, *refs):
-    out_refs, pieces_ref = refs[:4], refs[4]
+def total_kernel(info_ref, kept_ref, swapped_ref, came_ref, out_ref):
     y_count, za_count, _, wide = came_ref.shape
     cols = wide // 2
     here = info_ref[0]
     for za in range(za_count):
-        total = kept_ref[0, za] + swapped_ref[0, za].astype(jnp.float32)
+        total = kept_ref[za] + swapped_ref[za].astype(jnp.float32)
         for i in range(y_count):
             part = came_ref[i, za].astype(jnp.float32)
             total = total + jnp.where(here == i, jnp.zeros_like(part), part)
         turned = total.T
         for zb in range(2):
-            pieces_ref[2 * zb + za] = turned[zb * cols : (zb + 1) * cols]
-    for i, s in enumerate((0,) + Z_STEPS):
-        out_refs[i][...] = pieces_ref[(info_ref[1] + s) & 3]
+            out_ref[2 * zb + za] = turned[zb * cols : (zb + 1) * cols]
 
 
 def arrange(info, own, other):
@@ -204,19 +200,13 @@
 
 def total_of(info, kept, swapped, came):
     _, za_count, rows, wide = came.shape
-    piece = (wide // 2, rows)
-    own = pl.BlockSpec((1, za_count, rows, wide), lambda i, p: (p[0], 0, 0, 0))
-    full = pl.BlockSpec(came.shape, lambda i, p: (0, 0, 0, 0))
+    out = (2 * za_count, wide // 2, rows)
+    whole = pl.BlockSpec(memory_space=pltpu.VMEM)
     return pl.pallas_call(
         total_kernel,
-        grid_spec=pltpu.PrefetchScalarGridSpec(
-            num_scalar_prefetch=1,
-            grid=(1,),
-            in_specs=[own, own, full],
-            out_specs=[pl.BlockSpec(piece, lambda i, p: (0, 0))] * 4,
-            scratch_shapes=[pltpu.VMEM((4,) + piece, jnp.float32)],
-        ),
-        out_shape=[jax.ShapeDtypeStruct(piece, jnp.float32)] * 4,
+        in_specs=[pl.BlockSpec(memory_space=pltpu.SMEM), whole, whole, whole],
+        out_specs=whole,
+        out_shape=jax.ShapeDtypeStruct(out, jnp.float32),
         name="total",
     )(info, kept, swapped, came)
 
@@ -273,9 +263,9 @@
 
     came = lax.all_to_all(narrow, "y", 0, 0, tiled=True)
     zl = zb * 2 + za
-    part, *pieces = total_of(jnp.stack([y, zl]).astype(jnp.int32), kept, swapped, came)
-    for i, s in enumerate(Z_STEPS):
-        part = part + shift(pieces[i], ("zb", "za"), s)
+    pieces = total_of(y.astype(jnp.int32)[None], pick(kept, y), pick(swapped, y), came)
+    pieces = lax.all_to_all(pieces, ("zb", "za"), 0, 0, tiled=True)
+    part = jnp.sum(pieces, axis=0)
     grad = part / groups
     grad_own = rotate(grad, False)
 

time: 254 us -> 262 us (1.031)
  starting transfers between devices: 97.3 us -> 118 us
  waiting for transfers between devices: 58.8 us -> 46.3 us
  local copies, waits for them, and re-layouts: 6.67 us -> 10 us
    all_to_all x0 -> x1, waiting for transfers between devices: none -> 16.5 us  [per_device(): pieces = lax.all_to_all(pieces, ('zb', 'za'), 0, 0, tiled=True)]
    ppermute x2, waiting for transfers between devices: 19.9 us -> 4.96 us  [turn(): return lax.ppermute(value, ('zb', 'zh'), pairs)]
    ppermute x9, starting transfers between devices: 39.8 us -> 54.7 us  [flip(): return lax.ppermute(value, axis, [(i, i ^ mask) for i in range(SIZE[axis])])]
    ppermute x9 -> x6, waiting for transfers between devices: 22.1 us -> 11.3 us  [shift(): lax.ppermute(value, axis, [(i, (i + step) % size) for i in range(size)])]
    ppermute x2, starting transfers between devices: 14.7 us -> 23.5 us  [turn(): return lax.ppermute(value, ('zb', 'zh'), pairs)]
    ppermute x9 -> x6, starting transfers between devices: 27 us -> 20.8 us  [shift(): lax.ppermute(value, axis, [(i, (i + step) % size) for i in range(size)])]
    ppermute x9, waiting for transfers between devices: 13.1 us -> 9.16 us  [flip(): return lax.ppermute(value, axis, [(i, i ^ mask) for i in range(SIZE[axis])])]
    all_to_all x0 -> x1, starting transfers between devices: none -> 3.4 us  [per_device(): pieces = lax.all_to_all(pieces, ('zb', 'za'), 0, 0, tiled=True)]
  transfers between devices with their start and end apart: 23 -> 21, of which waited for: 12 -> 11; matrix products, arithmetic and copies ran while one was open for 3% -> 3% of each run, Pallas kernels for 8% -> 7%
where the time goes in v7:
time: 262 us; the launch traced here: 261 us
  starting transfers between devices  118 us (45%)
  blocking collectives  57.7 us (22%)
  waiting for transfers between devices  46.3 us (18%)
  Pallas kernels  18.8 us (7%)
  local copies, waits for them, and re-layouts  10 us (4%)
  other arithmetic  8 us (3%)
    ppermute x9, starting transfers between devices, flip(): return lax.ppermute(value, axis, [(i, i ^ mask) for i in range(SIZE[axis])])  54.7 us
    ppermute x2, starting transfers between devices, turn(): return lax.ppermute(value, ('zb', 'zh'), pairs)  23.5 us
    ppermute x6, starting transfers between devices, shift(): lax.ppermute(value, axis, [(i, (i + step) % size) for i in range(size)])  20.8 us
    all_to_all x1, waiting for transfers between devices, per_device(): pieces = lax.all_to_all(pieces, ('zb', 'za'), 0, 0, tiled=True)  16.5 us
    psum x1, blocking collectives, per_device(): rows = lax.psum(rows, 'y')  14.2 us
    psum x1, blocking collectives, per_device(): sums = lax.psum(jnp.concatenate([slot(row_here, c, 2), tail]), 'c')  11.4 us
    ppermute x6, waiting for transfers between devices, shift(): lax.ppermute(value, axis, [(i, (i + step) % size) for i in range(size)])  11.3 us
    ppermute x9, waiting for transfers between devices, flip(): return lax.ppermute(value, axis, [(i, i ^ mask) for i in range(SIZE[axis])])  9.16 us
  transfers between devices with their start and end apart: 21, of which 11 were waited for; matrix products, arithmetic and copies ran while one was open for 3% of the time, Pallas kernels for 7%

profile of v7, /device:TPU:1, one launch (start us, length us, event | category | flops | bytes accessed | tf_op | source)
XLA Modules:
  0.0 260.7 jit_solution(18134813886461136049)
XLA Ops:
  0.6 0.7 iota_compare_fusion
  1.4 0.1 lt.37
  1.5 1.4 broadcast_select_fusion
  3.0 11.5 %collective-permute-start.10 = (bf16[128,2048]{1,0:T(8,128)(2,1)S(1)}, bf16[128,2048]{1,0:T(8,128)(2,1)S(1)}, u32[]{:S(2)}, u32[]{:S(2)}) collective-permute-start(bf16[128,2048]{1,0:T(8,128)(2,1)S(1)} %get-tuple-element.16), channel_id=1, source_target_pairs={{0,1},{1,0},{2,3},{3,2},{4,5},{5,4},{6,7},{7,6},{8,9},{9,8},{10,11... | collective-permute-start | bytes 1572872 | tf_op jit(solution)/shard_map/ppermute | solution.py:25
  14.4 3.1 %collective-permute-start.7 = (bf16[128,2048]{1,0:T(8,128)(2,1)S(1)}, bf16[128,2048]{1,0:T(8,128)(2,1)S(1)}, u32[]{:S(2)}, u32[]{:S(2)}) collective-permute-start(bf16[128,2048]{1,0:T(8,128)(2,1)S(1)} %get-tuple-element.17.refs_16_.refs_0_), channel_id=1, source_target_pairs={{0,2},{2,4},{4,6},{6,0},{1,3},{3,5},{5,7},{7,1},{8,10},{10,12},{12... | collective-permute-start | bytes 1572872 | tf_op jit(solution)/shard_map/ppermute | solution.py:21
  17.6 1.9 collective-permute-start.15
  19.5 3.4 %collective-permute-start.8 = (bf16[128,2048]{1,0:T(8,128)(2,1)S(1)}, bf16[128,2048]{1,0:T(8,128)(2,1)S(1)}, u32[]{:S(2)}, u32[]{:S(2)}) collective-permute-start(bf16[128,2048]{1,0:T(8,128)(2,1)S(1)} %get-tuple-element.17.refs_16_.refs_0_), channel_id=1, source_target_pairs={{0,6},{2,0},{4,2},{6,4},{1,7},{3,1},{5,3},{7,5},{8,14},{10,8},{12,... | collective-permute-start | bytes 1572872 | tf_op jit(solution)/shard_map/ppermute | solution.py:21
  22.9 3.4 %collective-permute-start.9 = (bf16[128,2048]{1,0:T(8,128)(2,1)S(1)}, bf16[128,2048]{1,0:T(8,128)(2,1)S(1)}, u32[]{:S(2)}, u32[]{:S(2)}) collective-permute-start(bf16[128,2048]{1,0:T(8,128)(2,1)S(1)} %get-tuple-element.17.refs_16_.refs_0_), channel_id=1, source_target_pairs={{0,4},{2,6},{4,0},{6,2},{1,5},{3,7},{5,1},{7,3},{8,12},{10,14},{12... | collective-permute-start | bytes 1572872 | tf_op jit(solution)/shard_map/ppermute | solution.py:21
  26.4 2.9 %collective-permute-start.11 = (bf16[128,2048]{1,0:T(8,128)(2,1)S(1)}, bf16[128,2048]{1,0:T(8,128)(2,1)}, u32[]{:S(2)}, u32[]{:S(2)}) collective-permute-start(bf16[128,2048]{1,0:T(8,128)(2,1)S(1)} %collective-permute-done.10.refs_20_.refs_4_), channel_id=1, source_target_pairs={{0,2},{2,4},{4,6},{6,0},{1,3},{3,5},{5,7},{7,1},{8,10},{10,12},{12... | collective-permute-start | bytes 1572872 | tf_op jit(solution)/shard_map/ppermute | solution.py:21
  29.3 0.8 collective-permute-done.7.refs_17_.refs_1_
  30.1 3.2 %collective-permute-start.12 = (bf16[128,2048]{1,0:T(8,128)(2,1)S(1)}, bf16[128,2048]{1,0:T(8,128)(2,1)}, u32[]{:S(2)}, u32[]{:S(2)}) collective-permute-start(bf16[128,2048]{1,0:T(8,128)(2,1)S(1)} %collective-permute-done.10.refs_20_.refs_4_), channel_id=1, source_target_pairs={{0,6},{2,0},{4,2},{6,4},{1,7},{3,1},{5,3},{7,5},{8,14},{10,8},{12,... | collective-permute-start | bytes 1572872 | tf_op jit(solution)/shard_map/ppermute | solution.py:21
  33.3 4.1 %collective-permute-done.15 = bf16[1024,256]{1,0:T(8,128)(2,1)S(1)} collective-permute-done((bf16[1024,256]{1,0:T(8,128)(2,1)S(1)}, bf16[1024,256]{1,0:T(8,128)(2,1)S(1)}, u32[]{:S(2)}, u32[]{:S(2)}) %collective-permute-start.15) | collective-permute-done | bytes 524320 | tf_op jit(solution)/shard_map/ppermute | solution.py:25
  37.4 0.8 copy-done.12
  38.2 4.7 %collective-permute-start.13 = (bf16[128,2048]{1,0:T(8,128)(2,1)S(1)}, bf16[128,2048]{1,0:T(8,128)(2,1)S(1)}, u32[]{:S(2)}, u32[]{:S(2)}) collective-permute-start(bf16[128,2048]{1,0:T(8,128)(2,1)S(1)} %collective-permute-done.10.refs_20_.refs_4_), channel_id=1, source_target_pairs={{0,4},{2,6},{4,0},{6,2},{1,5},{3,7},{5,1},{7,3},{8,12},{10,14},{12... | collective-permute-start | bytes 1572872 | tf_op jit(solution)/shard_map/ppermute | solution.py:21
  42.9 0.7 stack.55.info_ref
  43.6 3.2 %arrange.1.ctx_ref = bf16[512,1024]{1,0:T(8,128)(2,1)} custom-call(s32[13]{0:T(128)} %stack.55.info_ref, bf16[8,128,256]{2,1,0:T(8,128)(2,1)} %bitcast.36, bf16[8,128,256]{2,1,0:T(8,128)(2,1)} %bitcast.37), custom_call_target="tpu_custom_call" | custom-call | tf_op jit(solution)/shard_map/arrange/pallas_call | solution.py:128
  46.8 7.4 %collective-permute-start = (bf16[1,64,256]{2,1,0:T(8,128)(2,1)S(1)}, bf16[1,64,256]{2,1,0:T(8,128)(2,1)S(1)}, u32[]{:S(2)}, u32[]{:S(2)}) collective-permute-start(bf16[1,64,256]{2,1,0:T(8,128)(2,1)S(1)} %convert_bitcast_fusion), channel_id=1, source_target_pairs={{0,64},{16,80},{32,96},{48,112},{64,0},{80,16},{96,32},{112,48},{1... | collective-permute-start | bytes 98312 | tf_op jit(solution)/shard_map/ppermute | solution.py:25
  54.3 1.3 collective-permute-done.12.refs_22_.refs_6_
  55.7 9.2 %collective-permute-done.13.refs_23_.refs_7_ = bf16[128,2048]{1,0:T(8,128)(2,1)S(1)} collective-permute-done((bf16[128,2048]{1,0:T(8,128)(2,1)S(1)}, bf16[128,2048]{1,0:T(8,128)(2,1)S(1)}, u32[]{:S(2)}, u32[]{:S(2)}) %collective-permute-start.13) | collective-permute-done | bytes 524320 | tf_op jit(solution)/shard_map/ppermute | solution.py:21
  64.9 0.8 copy-done.11
  65.6 6.0 %grad.1 = (f32[8,2,256,128]{3,2,1,0:T(8,128)}, bf16[8,2,256,128]{3,2,1,0:T(8,128)(2,1)}) custom-call(bf16[512,1024]{1,0:T(8,128)(2,1)} %arrange.1.ctx_ref, bf16[128,2048]{1,0:T(8,128)(2,1)} %copy-done.3, bf16[128,2048]{1,0:T(8,128)(2,1)} %copy-done.8, bf16[128,2048]{1,0:T(8,128)(2,1)} %copy-done.9, bf16[128,2048]{1,0:T(8,128)(2,1)} %copy-done.10, ...), custom_call_target="tpu_custom_call" | custom-call | flops 2147483648 | bytes 9437184 | tf_op jit(solution)/shard_map/grad/pallas_call | solution.py:147
  71.6 3.7 %collective-permute-start.16 = (bf16[8,2,256,128]{3,2,1,0:T(8,128)(2,1)}, bf16[8,2,256,128]{3,2,1,0:T(8,128)(2,1)S(1)}, u32[]{:S(2)}, u32[]{:S(2)}) collective-permute-start(bf16[8,2,256,128]{3,2,1,0:T(8,128)(2,1)} %get-tuple-element.11), channel_id=1, source_target_pairs={{0,8},{8,0},{1,9},{9,1},{2,10},{10,2},{3,11},{11,3},{4,12},{12,4},... | collective-permute-start | bytes 3145736 | tf_op jit(solution)/shard_map/ppermute | solution.py:25
  75.4 4.2 %collective-permute-start.1 = (bf16[2,64,256]{2,1,0:T(8,128)(2,1)S(1)}, bf16[2,64,256]{2,1,0:T(8,128)(2,1)S(1)}, u32[]{:S(2)}, u32[]{:S(2)}) collective-permute-start(bf16[2,64,256]{2,1,0:T(8,128)(2,1)S(1)} %pad_maximum_fusion.3), channel_id=1, source_target_pairs={{0,32},{16,48},{32,0},{48,16},{64,96},{80,112},{96,64},{112,80},{1... | collective-permute-start | bytes 196616 | tf_op jit(solution)/shard_map/ppermute | solution.py:25
  79.6 2.2 collective-permute-done.1
  81.8 4.1 %collective-permute-start.2 = (bf16[4,64,256]{2,1,0:T(8,128)(2,1)S(1)}, bf16[4,64,256]{2,1,0:T(8,128)(2,1)S(1)}, u32[]{:S(2)}, u32[]{:S(2)}) collective-permute-start(bf16[4,64,256]{2,1,0:T(8,128)(2,1)S(1)} %pad_maximum_fusion.2), channel_id=1, source_target_pairs={{0,16},{16,0},{32,48},{48,32},{64,80},{80,64},{96,112},{112,96},{1... | collective-permute-start | bytes 393224 | tf_op jit(solution)/shard_map/ppermute | solution.py:25
  86.0 2.4 collective-permute-done.2
  88.4 0.7 collective-permute-start.3
  89.1 22.9 %collective-permute-start.4 = (bf16[8,64,256]{2,1,0:T(8,128)(2,1)S(1)}, bf16[8,64,256]{2,1,0:T(8,128)(2,1)S(1)}, u32[]{:S(2)}, u32[]{:S(2)}) collective-permute-start(bf16[8,64,256]{2,1,0:T(8,128)(2,1)S(1)} %pad_maximum_fusion.1), channel_id=1, source_target_pairs={{0,256},{1,0},{256,257},{257,1},{2,258},{3,2},{258,259},{259,3},{4... | collective-permute-start | bytes 786440 | tf_op jit(solution)/shard_map/ppermute | solution.py:34
  112.0 5.0 %collective-permute-done.4 = bf16[8,64,256]{2,1,0:T(8,128)(2,1)S(1)} collective-permute-done((bf16[8,64,256]{2,1,0:T(8,128)(2,1)S(1)}, bf16[8,64,256]{2,1,0:T(8,128)(2,1)S(1)}, u32[]{:S(2)}, u32[]{:S(2)}) %collective-permute-start.4) | collective-permute-done | bytes 262176 | tf_op jit(solution)/shard_map/ppermute | solution.py:34
  117.0 12.6 %collective-permute-start.5 = (bf16[8,64,512]{2,1,0:T(8,128)(2,1)S(1)}, bf16[8,64,512]{2,1,0:T(8,128)(2,1)S(1)}, u32[]{:S(2)}, u32[]{:S(2)}) collective-permute-start(bf16[8,64,512]{2,1,0:T(8,128)(2,1)S(1)} %constant_dynamic-update-slice_fusion), channel_id=1, source_target_pairs={{0,128},{128,0},{1,129},{129,1},{2,130},{130,2},{3,131},{131,3},{4... | collective-permute-start | bytes 1572872 | tf_op jit(solution)/shard_map/ppermute | solution.py:25
  129.6 1.0 copy-done.4
  130.6 2.9 %add_convert_fusion = bf16[8,2,256,128]{3,2,1,0:T(8,128)(2,1)} fusion(f32[8,2,256,128]{3,2,1,0:T(8,128)} %get-tuple-element.10, bf16[8,2,256,128]{3,2,1,0:T(8,128)(2,1)S(1)} %collective-permute-done.16), kind=kLoop, calls=%fused_computation | loop fusion | flops 1572864 | bytes 4194304 | tf_op jit(solution)/shard_map/convert_element_type | solution.py:257
  133.5 7.2 %all-to-all-start = ((bf16[8,2,256,128]{3,2,1,0:T(8,128)(2,1)}), bf16[8,2,256,128]{3,2,1,0:T(8,128)(2,1)S(1)}, u32[]{:S(2)}, u32[]{:S(2)}) async-start(bf16[8,2,256,128]{3,2,1,0:T(8,128)(2,1)} %add_convert_fusion), calls=%async_computation | async-start | bytes 2097152 | tf_op jit(solution)/shard_map/all_to_all | solution.py:264
  140.7 0.1 pad_maximum_fusion.refs_0_.refs_1_.refs_2_.refs_3_.refs_4_.refs_5_.refs_6_.refs_7_
  140.8 4.4 %collective-permute-start.6 = (bf16[16,64,512]{2,1,0:T(8,128)(2,1)S(1)}, bf16[16,64,512]{2,1,0:T(8,128)(2,1)S(1)}, u32[]{:S(2)}, u32[]{:S(2)}) collective-permute-start(bf16[16,64,512]{2,1,0:T(8,128)(2,1)S(1)} %pad_maximum_fusion.refs_0_.refs_1_.refs_2_.refs_3_.refs_4_.refs_5_.refs_6_.refs_7_), channel_id=1, source_target_pairs={{0,8},{8,0},{1,9},{9,1},{2,10},{10,2},{3,11},{11,3},{4,12},{12,4},... | collective-permute-start | bytes 3145736 | tf_op jit(solution)/shard_map/ppermute | solution.py:25
  145.3 1.9 collective-permute-start.18
  147.2 0.3 collective-permute-done.6.refs_8_.refs_9_.refs_10_.refs_11_.refs_12_.refs_13_.refs_14_.refs_15_
  147.5 1.0 copy-done.1
  148.5 7.2 %back.1 = (f32[8,128,256]{2,1,0:T(8,128)}, bf16[8,128,256]{2,1,0:T(8,128)(2,1)}) custom-call(s32[13]{0:T(128)} %stack.55.info_ref, bf16[16,64,512]{2,1,0:T(8,128)(2,1)} %copy-done, bf16[16,64,512]{2,1,0:T(8,128)(2,1)} %copy-done, bf16[16,64,512]{2,1,0:T(8,128)(2,1)} %copy-done, bf16[16,64,512]{2,1,0:T(8,128)(2,1)} %copy-done, bf16[16,64,512]{2,1,0:T(8,128)(2,1)} %copy-done, ...), custom_call_target="tpu_custom_call" | custom-call | flops 2147483648 | bytes 8388608 | tf_op jit(solution)/shard_map/back/pallas_call | solution.py:180
  155.7 4.8 %collective-permute-start.14 = (bf16[8,128,256]{2,1,0:T(8,128)(2,1)}, bf16[8,128,256]{2,1,0:T(8,128)(2,1)S(1)}, u32[]{:S(2)}, u32[]{:S(2)}) collective-permute-start(bf16[8,128,256]{2,1,0:T(8,128)(2,1)} %get-tuple-element.9), channel_id=1, source_target_pairs={{0,1},{1,0},{2,3},{3,2},{4,5},{5,4},{6,7},{7,6},{8,9},{9,8},{10,11... | collective-permute-start | bytes 1572872 | tf_op jit(solution)/shard_map/ppermute | solution.py:25
  160.5 1.7 dynamic-slice_bitcast_fusion.kept_ref
  162.2 1.6 dynamic-slice_bitcast_fusion.1.swapped_ref
  163.8 4.4 %all-to-all-done.came_ref = bf16[8,2,256,128]{3,2,1,0:T(8,128)(2,1)S(1)} async-done(((bf16[8,2,256,128]{3,2,1,0:T(8,128)(2,1)}), bf16[8,2,256,128]{3,2,1,0:T(8,128)(2,1)S(1)}, u32[]{:S(2)}, u32[]{:S(2)}) %all-to-all-start) | async-done | bytes 1048608 | tf_op jit(solution)/shard_map/all_to_all | solution.py:264
  168.2 1.0 copy-done.2
  169.2 2.4 total.1
  171.5 3.4 %all-to-all-start.1 = ((f32[4,64,256]{2,1,0:T(8,128)}), f32[4,64,256]{2,1,0:T(8,128)S(1)}, u32[]{:S(2)}, u32[]{:S(2)}) async-start(f32[4,64,256]{2,1,0:T(8,128)} %total.1), calls=%async_computation.1 | async-start | bytes 524288 | tf_op jit(solution)/shard_map/all_to_all | solution.py:267
  175.0 0.2 collective-permute-done.14
  175.2 0.9 add_convert_fusion.1
  176.1 16.5 %all-to-all-done.1 = f32[4,64,256]{2,1,0:T(8,128)S(1)} async-done(((f32[4,64,256]{2,1,0:T(8,128)}), f32[4,64,256]{2,1,0:T(8,128)S(1)}, u32[]{:S(2)}, u32[]{:S(2)}) %all-to-all-start.1) | async-done | bytes 262176 | tf_op jit(solution)/shard_map/all_to_all | solution.py:267
  192.6 0.1 add_reduce_fusion.1
  192.7 2.6 %psum.49 = f32[64]{0:T(128)S(1)} all-reduce(f32[64]{0:T(128)S(1)} %get-tuple-element.13), channel_id=1, replica_groups=mesh['zb'=2,'za'=2,'y'=8,'c'=2,'x'=4,'zh'=2] {'c'}, use_global_device_ids=true, to_apply=%region_3.4 | all-reduce | flops 64 | bytes 512 | tf_op jit(solution)/shard_map/psum | solution.py:274
  195.4 8.5 %psum.50 = f32[64]{0:T(128)S(1)} all-reduce(f32[64]{0:T(128)S(1)} %psum.49), channel_id=1, replica_groups=mesh['zb'=2,'za'=2,'y'=8,'c'=2,'x'=4,'zh'=2] {'x'}, use_global_device_ids=true, to_apply=%region_4.5 | all-reduce | flops 64 | bytes 512 | tf_op jit(solution)/shard_map/psum | solution.py:275
  203.9 0.1 divide_reduce_fusion
  204.1 0.1 select_n.60
  204.2 14.2 %psum.51 = f32[512]{0:T(512)S(1)} all-reduce(f32[512]{0:T(512)S(1)} %pad_maximum_fusion.7), channel_id=1, replica_groups=mesh['zb'=2,'za'=2,'y'=8,'c'=2,'x'=4,'zh'=2] {'y'}, use_global_device_ids=true, to_apply=%region_6.7 | all-reduce | flops 512 | bytes 4096 | tf_op jit(solution)/shard_map/psum | solution.py:279
  218.4 6.6 %psum.52 = f32[768]{0:T(1024)S(1)} all-reduce(f32[768]{0:T(1024)S(1)} %pad_maximum_fusion.4), channel_id=1, replica_groups=mesh['zb'=2,'za'=2,'y'=8,'c'=2,'x'=4,'zh'=2] {'zb','za'}, use_global_device_ids=true, to_apply=%region_7.8 | all-reduce | flops 768 | bytes 6144 | tf_op jit(solution)/shard_map/psum | solution.py:280
  225.1 7.7 %psum.53 = f32[1024]{0:T(1024)S(1)} all-reduce(f32[1024]{0:T(1024)S(1)} %pad_maximum_fusion.5), channel_id=1, replica_groups=mesh['zb'=2,'za'=2,'y'=8,'c'=2,'x'=4,'zh'=2] {'zh'}, use_global_device_ids=true, to_apply=%region_8.9 | all-reduce | flops 1024 | bytes 8192 | tf_op jit(solution)/shard_map/psum | solution.py:282
  232.8 0.6 fusion
  233.5 0.6 concatenate.41
  234.2 11.4 %psum.54 = f32[640]{0:T(1024)S(1)} all-reduce(f32[640]{0:T(1024)S(1)} %concatenate.41), channel_id=1, replica_groups=mesh['zb'=2,'za'=2,'y'=8,'c'=2,'x'=4,'zh'=2] {'c'}, use_global_device_ids=true, to_apply=%region_10.11 | all-reduce | flops 640 | bytes 5120 | tf_op jit(solution)/shard_map/psum | solution.py:288
  245.6 0.5 slice.51
  246.1 6.4 %collective-permute-start.17 = (f32[64,256]{1,0:T(8,128)S(1)}, f32[64,256]{1,0:T(8,128)S(1)}, u32[]{:S(2)}, u32[]{:S(2)}) collective-permute-start(f32[64,256]{1,0:T(8,128)S(1)} %get-tuple-element.19), channel_id=1, source_target_pairs={{0,0},{1,256},{8,1},{9,257},{256,8},{257,264},{264,9},{265,265},{2... | collective-permute-start | bytes 196616 | tf_op jit(solution)/shard_map/ppermute | solution.py:44
  252.5 6.6 %psum.55 = f32[]{:T(128)} all-reduce(f32[]{:T(128)} %bitcast.23), channel_id=1, replica_groups=mesh['zb'=2,'za'=2,'y'=8,'c'=2,'x'=4,'zh'=2] {'x'}, use_global_device_ids=true, to_apply=%region_11.12 | all-reduce | flops 1 | bytes 8 | tf_op jit(solution)/shard_map/psum | solution.py:290
  259.9 0.7 divide_bitcast_fusion
  (70 shorter events, 0.7 us)
Async XLA Ops:
  1.5 16.1 %copy-start.6 = (bf16[1024,256]{1,0:T(8,128)(2,1)S(1)}, bf16[1024,256]{1,0:T(8,128)(2,1)}, u32[]{:S(2)}) copy-start(bf16[1024,256]{1,0:T(8,128)(2,1)} %param.6) | copy-start | bytes 1572868
  1.5 42.2 %copy-start.13 = (f32[256,64]{0,1:T(8,128)S(1)}, f32[256,64]{0,1:T(8,128)}, u32[]{:S(2)}) copy-start(f32[256,64]{0,1:T(8,128)} %param.9) | copy-start | bytes 196612
  3.0 61.8 %copy-start.3 = (bf16[128,2048]{1,0:T(8,128)(2,1)}, bf16[128,2048]{1,0:T(8,128)(2,1)S(1)}, u32[]{:S(2)}) copy-start(bf16[128,2048]{1,0:T(8,128)(2,1)S(1)} %get-tuple-element.17.refs_16_.refs_0_) | copy-start | bytes 1572868
  3.0 23.4 %collective-permute-start.10 = (bf16[128,2048]{1,0:T(8,128)(2,1)S(1)}, bf16[128,2048]{1,0:T(8,128)(2,1)S(1)}, u32[]{:S(2)}, u32[]{:S(2)}) collective-permute-start(bf16[128,2048]{1,0:T(8,128)(2,1)S(1)} %get-tuple-element.16), channel_id=1, source_target_pairs={{0,1},{1,0},{2,3},{3,2},{4,5},{5,4},{6,7},{7,6},{8,9},{9,8},{10,11... | collective-permute-start | bytes 1572872 | tf_op jit(solution)/shard_map/ppermute | solution.py:25
  14.4 15.6 %collective-permute-start.7 = (bf16[128,2048]{1,0:T(8,128)(2,1)S(1)}, bf16[128,2048]{1,0:T(8,128)(2,1)S(1)}, u32[]{:S(2)}, u32[]{:S(2)}) collective-permute-start(bf16[128,2048]{1,0:T(8,128)(2,1)S(1)} %get-tuple-element.17.refs_16_.refs_0_), channel_id=1, source_target_pairs={{0,2},{2,4},{4,6},{6,0},{1,3},{3,5},{5,7},{7,1},{8,10},{10,12},{12... | collective-permute-start | bytes 1572872 | tf_op jit(solution)/shard_map/ppermute | solution.py:21
  17.6 19.8 %collective-permute-start.15 = (bf16[1024,256]{1,0:T(8,128)(2,1)S(1)}, bf16[1024,256]{1,0:T(8,128)(2,1)S(1)}, u32[]{:S(2)}, u32[]{:S(2)}) collective-permute-start(bf16[1024,256]{1,0:T(8,128)(2,1)S(1)} %copy-done.6), channel_id=1, source_target_pairs={{0,1},{1,0},{2,3},{3,2},{4,5},{5,4},{6,7},{7,6},{8,9},{9,8},{10,11... | collective-permute-start | bytes 1572872 | tf_op jit(solution)/shard_map/ppermute | solution.py:25
  19.5 27.3 %collective-permute-start.8 = (bf16[128,2048]{1,0:T(8,128)(2,1)S(1)}, bf16[128,2048]{1,0:T(8,128)(2,1)S(1)}, u32[]{:S(2)}, u32[]{:S(2)}) collective-permute-start(bf16[128,2048]{1,0:T(8,128)(2,1)S(1)} %get-tuple-element.17.refs_16_.refs_0_), channel_id=1, source_target_pairs={{0,6},{2,0},{4,2},{6,4},{1,7},{3,1},{5,3},{7,5},{8,14},{10,8},{12,... | collective-permute-start | bytes 1572872 | tf_op jit(solution)/shard_map/ppermute | solution.py:21
  22.9 31.4 %collective-permute-start.9 = (bf16[128,2048]{1,0:T(8,128)(2,1)S(1)}, bf16[128,2048]{1,0:T(8,128)(2,1)S(1)}, u32[]{:S(2)}, u32[]{:S(2)}) collective-permute-start(bf16[128,2048]{1,0:T(8,128)(2,1)S(1)} %get-tuple-element.17.refs_16_.refs_0_), channel_id=1, source_target_pairs={{0,4},{2,6},{4,0},{6,2},{1,5},{3,7},{5,1},{7,3},{8,12},{10,14},{12... | collective-permute-start | bytes 1572872 | tf_op jit(solution)/shard_map/ppermute | solution.py:21
  26.4 38.5 %copy-start.7 = (bf16[128,2048]{1,0:T(8,128)(2,1)}, bf16[128,2048]{1,0:T(8,128)(2,1)S(1)}, u32[]{:S(2)}) copy-start(bf16[128,2048]{1,0:T(8,128)(2,1)S(1)} %collective-permute-done.10.refs_20_.refs_4_) | copy-start | bytes 1572868
  26.4 28.0 %collective-permute-start.11 = (bf16[128,2048]{1,0:T(8,128)(2,1)S(1)}, bf16[128,2048]{1,0:T(8,128)(2,1)}, u32[]{:S(2)}, u32[]{:S(2)}) collective-permute-start(bf16[128,2048]{1,0:T(8,128)(2,1)S(1)} %collective-permute-done.10.refs_20_.refs_4_), channel_id=1, source_target_pairs={{0,2},{2,4},{4,6},{6,0},{1,3},{3,5},{5,7},{7,1},{8,10},{10,12},{12... | collective-permute-start | bytes 1572872 | tf_op jit(solution)/shard_map/ppermute | solution.py:21
  30.1 34.7 %copy-start.8 = (bf16[128,2048]{1,0:T(8,128)(2,1)}, bf16[128,2048]{1,0:T(8,128)(2,1)S(1)}, u32[]{:S(2)}) copy-start(bf16[128,2048]{1,0:T(8,128)(2,1)S(1)} %collective-permute-done.7.refs_17_.refs_1_) | copy-start | bytes 1572868
  30.1 25.6 %collective-permute-start.12 = (bf16[128,2048]{1,0:T(8,128)(2,1)S(1)}, bf16[128,2048]{1,0:T(8,128)(2,1)}, u32[]{:S(2)}, u32[]{:S(2)}) collective-permute-start(bf16[128,2048]{1,0:T(8,128)(2,1)S(1)} %collective-permute-done.10.refs_20_.refs_4_), channel_id=1, source_target_pairs={{0,6},{2,0},{4,2},{6,4},{1,7},{3,1},{5,3},{7,5},{8,14},{10,8},{12,... | collective-permute-start | bytes 1572872 | tf_op jit(solution)/shard_map/ppermute | solution.py:21
  37.4 0.8 copy-start.12
  38.2 26.7 %collective-permute-start.13 = (bf16[128,2048]{1,0:T(8,128)(2,1)S(1)}, bf16[128,2048]{1,0:T(8,128)(2,1)S(1)}, u32[]{:S(2)}, u32[]{:S(2)}) collective-permute-start(bf16[128,2048]{1,0:T(8,128)(2,1)S(1)} %collective-permute-done.10.refs_20_.refs_4_), channel_id=1, source_target_pairs={{0,4},{2,6},{4,0},{6,2},{1,5},{3,7},{5,1},{7,3},{8,12},{10,14},{12... | collective-permute-start | bytes 1572872 | tf_op jit(solution)/shard_map/ppermute | solution.py:21
  46.8 18.0 %copy-start.9 = (bf16[128,2048]{1,0:T(8,128)(2,1)}, bf16[128,2048]{1,0:T(8,128)(2,1)S(1)}, u32[]{:S(2)}) copy-start(bf16[128,2048]{1,0:T(8,128)(2,1)S(1)} %collective-permute-done.8.refs_18_.refs_2_) | copy-start | bytes 1572868
  46.8 28.5 %collective-permute-start = (bf16[1,64,256]{2,1,0:T(8,128)(2,1)S(1)}, bf16[1,64,256]{2,1,0:T(8,128)(2,1)S(1)}, u32[]{:S(2)}, u32[]{:S(2)}) collective-permute-start(bf16[1,64,256]{2,1,0:T(8,128)(2,1)S(1)} %convert_bitcast_fusion), channel_id=1, source_target_pairs={{0,64},{16,80},{32,96},{48,112},{64,0},{80,16},{96,32},{112,48},{1... | collective-permute-start | bytes 98312 | tf_op jit(solution)/shard_map/ppermute | solution.py:25
  54.3 10.5 %copy-start.10 = (bf16[128,2048]{1,0:T(8,128)(2,1)}, bf16[128,2048]{1,0:T(8,128)(2,1)S(1)}, u32[]{:S(2)}) copy-start(bf16[128,2048]{1,0:T(8,128)(2,1)S(1)} %collective-permute-done.9.refs_19_.refs_3_) | copy-start | bytes 1572868
  64.8 0.8 copy-start.11
  71.6 57.9 %collective-permute-start.16 = (bf16[8,2,256,128]{3,2,1,0:T(8,128)(2,1)}, bf16[8,2,256,128]{3,2,1,0:T(8,128)(2,1)S(1)}, u32[]{:S(2)}, u32[]{:S(2)}) collective-permute-start(bf16[8,2,256,128]{3,2,1,0:T(8,128)(2,1)} %get-tuple-element.11), channel_id=1, source_target_pairs={{0,8},{8,0},{1,9},{9,1},{2,10},{10,2},{3,11},{11,3},{4,12},{12,4},... | collective-permute-start | bytes 3145736 | tf_op jit(solution)/shard_map/ppermute | solution.py:25
  75.4 6.4 %collective-permute-start.1 = (bf16[2,64,256]{2,1,0:T(8,128)(2,1)S(1)}, bf16[2,64,256]{2,1,0:T(8,128)(2,1)S(1)}, u32[]{:S(2)}, u32[]{:S(2)}) collective-permute-start(bf16[2,64,256]{2,1,0:T(8,128)(2,1)S(1)} %pad_maximum_fusion.3), channel_id=1, source_target_pairs={{0,32},{16,48},{32,0},{48,16},{64,96},{80,112},{96,64},{112,80},{1... | collective-permute-start | bytes 196616 | tf_op jit(solution)/shard_map/ppermute | solution.py:25
  81.8 6.5 %collective-permute-start.2 = (bf16[4,64,256]{2,1,0:T(8,128)(2,1)S(1)}, bf16[4,64,256]{2,1,0:T(8,128)(2,1)S(1)}, u32[]{:S(2)}, u32[]{:S(2)}) collective-permute-start(bf16[4,64,256]{2,1,0:T(8,128)(2,1)S(1)} %pad_maximum_fusion.2), channel_id=1, source_target_pairs={{0,16},{16,0},{32,48},{48,32},{64,80},{80,64},{96,112},{112,96},{1... | collective-permute-start | bytes 393224 | tf_op jit(solution)/shard_map/ppermute | solution.py:25
  88.4 23.5 %collective-permute-start.3 = (bf16[8,64,256]{2,1,0:T(8,128)(2,1)S(1)}, bf16[8,64,256]{2,1,0:T(8,128)(2,1)S(1)}, u32[]{:S(2)}, u32[]{:S(2)}) collective-permute-start(bf16[8,64,256]{2,1,0:T(8,128)(2,1)S(1)} %pad_maximum_fusion.1), channel_id=1, source_target_pairs={{0,0},{1,256},{256,1},{257,257},{2,2},{3,258},{258,3},{259,259},{4... | collective-permute-start | bytes 786440 | tf_op jit(solution)/shard_map/ppermute | solution.py:34
  89.1 27.9 %collective-permute-start.4 = (bf16[8,64,256]{2,1,0:T(8,128)(2,1)S(1)}, bf16[8,64,256]{2,1,0:T(8,128)(2,1)S(1)}, u32[]{:S(2)}, u32[]{:S(2)}) collective-permute-start(bf16[8,64,256]{2,1,0:T(8,128)(2,1)S(1)} %pad_maximum_fusion.1), channel_id=1, source_target_pairs={{0,256},{1,0},{256,257},{257,1},{2,258},{3,2},{258,259},{259,3},{4... | collective-permute-start | bytes 786440 | tf_op jit(solution)/shard_map/ppermute | solution.py:34
  117.0 23.8 %collective-permute-start.5 = (bf16[8,64,512]{2,1,0:T(8,128)(2,1)S(1)}, bf16[8,64,512]{2,1,0:T(8,128)(2,1)S(1)}, u32[]{:S(2)}, u32[]{:S(2)}) collective-permute-start(bf16[8,64,512]{2,1,0:T(8,128)(2,1)S(1)} %constant_dynamic-update-slice_fusion), channel_id=1, source_target_pairs={{0,128},{128,0},{1,129},{129,1},{2,130},{130,2},{3,131},{131,3},{4... | collective-permute-start | bytes 1572872 | tf_op jit(solution)/shard_map/ppermute | solution.py:25
  129.6 1.0 copy-start.4
  133.5 11.8 %copy-start.15 = (f32[256]{0:T(256)S(1)}, f32[256]{0:T(256)}, u32[]{:S(2)}) copy-start(f32[256]{0:T(256)} %param.10) | copy-start | bytes 3076
  133.5 11.8 %copy-start.17 = (f32[64]{0:T(128)S(1)}, f32[64]{0:T(128)}, u32[]{:S(2)}) copy-start(f32[64]{0:T(128)} %param.11) | copy-start | bytes 772
  133.5 34.7 %all-to-all-start = ((bf16[8,2,256,128]{3,2,1,0:T(8,128)(2,1)}), bf16[8,2,256,128]{3,2,1,0:T(8,128)(2,1)S(1)}, u32[]{:S(2)}, u32[]{:S(2)}) async-start(bf16[8,2,256,128]{3,2,1,0:T(8,128)(2,1)} %add_convert_fusion), calls=%async_computation | async-start | bytes 2097152 | tf_op jit(solution)/shard_map/all_to_all | solution.py:264
  140.8 6.7 %copy-start = (bf16[16,64,512]{2,1,0:T(8,128)(2,1)}, bf16[16,64,512]{2,1,0:T(8,128)(2,1)S(1)}, u32[]{:S(2)}) copy-start(bf16[16,64,512]{2,1,0:T(8,128)(2,1)S(1)} %pad_maximum_fusion.refs_0_.refs_1_.refs_2_.refs_3_.refs_4_.refs_5_.refs_6_.refs_7_) | copy-start | bytes 3145732
  140.8 6.7 %collective-permute-start.6 = (bf16[16,64,512]{2,1,0:T(8,128)(2,1)S(1)}, bf16[16,64,512]{2,1,0:T(8,128)(2,1)S(1)}, u32[]{:S(2)}, u32[]{:S(2)}) collective-permute-start(bf16[16,64,512]{2,1,0:T(8,128)(2,1)S(1)} %pad_maximum_fusion.refs_0_.refs_1_.refs_2_.refs_3_.refs_4_.refs_5_.refs_6_.refs_7_), channel_id=1, source_target_pairs={{0,8},{8,0},{1,9},{9,1},{2,10},{10,2},{3,11},{11,3},{4,12},{12,4},... | collective-permute-start | bytes 3145736 | tf_op jit(solution)/shard_map/ppermute | solution.py:25
  145.3 58.6 %collective-permute-start.18 = (f32[320]{0:T(512)S(1)}, f32[320]{0:T(512)S(1)}, u32[]{:S(2)}, u32[]{:S(2)}) collective-permute-start(f32[320]{0:T(512)S(1)} %pad_maximum_fusion.6), channel_id=1, source_target_pairs={{0,0},{1,8},{8,256},{9,264},{256,1},{257,9},{264,257},{265,265},{2... | collective-permute-start | bytes 3848 | tf_op jit(solution)/shard_map/ppermute | solution.py:44
  147.5 1.0 copy-start.1
  155.7 19.4 %copy-start.5 = (f32[8,128,256]{2,1,0:T(8,128)S(1)}, f32[8,128,256]{2,1,0:T(8,128)}, u32[]{:S(2)}) copy-start(f32[8,128,256]{2,1,0:T(8,128)} %get-tuple-element.8) | copy-start | bytes 3145732
  155.7 19.4 %collective-permute-start.14 = (bf16[8,128,256]{2,1,0:T(8,128)(2,1)}, bf16[8,128,256]{2,1,0:T(8,128)(2,1)S(1)}, u32[]{:S(2)}, u32[]{:S(2)}) collective-permute-start(bf16[8,128,256]{2,1,0:T(8,128)(2,1)} %get-tuple-element.9), channel_id=1, source_target_pairs={{0,1},{1,0},{2,3},{3,2},{4,5},{5,4},{6,7},{7,6},{8,9},{9,8},{10,11... | collective-permute-start | bytes 1572872 | tf_op jit(solution)/shard_map/ppermute | solution.py:25
  168.2 1.0 copy-start.2
  171.5 21.1 %all-to-all-start.1 = ((f32[4,64,256]{2,1,0:T(8,128)}), f32[4,64,256]{2,1,0:T(8,128)S(1)}, u32[]{:S(2)}, u32[]{:S(2)}) async-start(f32[4,64,256]{2,1,0:T(8,128)} %total.1), calls=%async_computation.1 | async-start | bytes 524288 | tf_op jit(solution)/shard_map/all_to_all | solution.py:267
  246.1 13.9 %collective-permute-start.17 = (f32[64,256]{1,0:T(8,128)S(1)}, f32[64,256]{1,0:T(8,128)S(1)}, u32[]{:S(2)}, u32[]{:S(2)}) collective-permute-start(f32[64,256]{1,0:T(8,128)S(1)} %get-tuple-element.19), channel_id=1, source_target_pairs={{0,0},{1,256},{8,1},{9,257},{256,8},{257,264},{264,9},{265,265},{2... | collective-permute-start | bytes 196616 | tf_op jit(solution)/shard_map/ppermute | solution.py:44
  259.9 0.8 copy-start.14
  259.9 0.7 copy-start.16
